TPU v7x, 32 devices: a whole 2x2x4 slice. The times are simulated.
32 devices in a mesh: section: 2 (over core), et: 2 (over x), dp: 8 (over z, y).
Axes of the slice: x: 2, y: 2, z: 4, core: 2. Of those that a mesh axis runs over, the one named last changes fastest.
Arguments:
- layer_inputs: bfloat16 [2, 1, 2048, 2048], P('section', None, ('dp', 'et')), may hold values from -6 to 6
- out_grad: bfloat16 [1, 2048, 2048], P(None, ('dp', 'et')), may hold values from -6 to 6
- w_gate: bfloat16 [2, 2048, 7168], P('section', None, 'et'), may hold values from -0.125 to 0.125
- w_up: bfloat16 [2, 2048, 7168], P('section', None, 'et'), may hold values from -0.125 to 0.125
- w_down: bfloat16 [2, 2048, 7168], P('section', None, 'et'), may hold values from -0.0625 to 0.0625
- slot_token: int32 [2, 1, 1024], P('section', None, 'dp'), may hold values from -1 to 255, as said below
- slot_gate: float32 [2, 1, 1024], P('section', None, 'dp'), may hold values from 0.1 to 0.9
Outputs:
- in_grad: bfloat16 [2, 1, 2048, 2048], P('section', None, ('dp', 'et'))
- gate_w_grad: bfloat16 [2, 2048, 7168], P('section', 'dp', 'et')
- up_w_grad: bfloat16 [2, 2048, 7168], P('section', 'dp', 'et')
- down_w_grad: bfloat16 [2, 2048, 7168], P('section', 'dp', 'et')
- gate_value_grad: float32 [2, 1, 1024], P('section', None, 'dp')
Inputs may be any that keep to these rules, and one draw needn't show every extreme that they name: `slot_token`: each layout (one section, micro-batch and replica) holds distinct tokens of its replica in rising order in its first slots and -1 in the rest; from 64 to 128 slots are live, and in every draw some layout is full.
All inputs are finite; a program needn't handle non-finite values.
Results may differ from a plain program's by a relative error of at most 0.024.
Values may be sent and summed in bfloat16 or wider, within the bound.
No kernel may reach another device: no remote copies, remote signals or barrier semaphores. Data moves between devices by JAX's collectives and lax.ppermute only.
A program may use at most 320 MiB of HBM per device.

v0:
```python
import jax
import jax.numpy as jnp
from jax import lax
from jax.sharding import PartitionSpec as P


def from_behind(value, axis, steps):
    count = lax.axis_size(axis)
    leading, last = (max(0, -steps), min(count, count - steps))
    return lax.ppermute(value, axis, [(source, source + steps) for source in range(leading, last)])


def for_sending(array):
    return jax.tree.map(lambda a: a.astype(jnp.bfloat16) if a.dtype == jnp.float32 else a, array)


def selector_of(slots, total):
    return (slots[:, None] == jnp.arange(total, dtype=jnp.int32)[None, :]).astype(jnp.bfloat16)


def expert_backward(selector, x_full, g_full, gates, w_one, w_three, w_two, sums):
    contract_rows = (((0,), (0,)), ((), ()))
    contract_hidden = (((1,), (1,)), ((), ()))
    x_rows = jnp.dot(selector, x_full, preferred_element_type=jnp.float32).astype(jnp.bfloat16)
    g_rows = jnp.dot(selector, g_full, preferred_element_type=jnp.float32).astype(jnp.bfloat16)
    pre_gate = jnp.dot(x_rows, w_one, preferred_element_type=jnp.float32)
    pre_up = jnp.dot(x_rows, w_three, preferred_element_type=jnp.float32)
    sigma = jax.nn.sigmoid(pre_gate)
    active = pre_gate * sigma
    hidden = (active * pre_up).astype(jnp.bfloat16)
    back_hidden = jnp.dot(g_rows, w_two, preferred_element_type=jnp.float32)
    gate_part = jnp.sum(hidden.astype(jnp.float32) * back_hidden, axis=1)
    scaled_back = gates[:, None] * back_hidden
    grad_pre_gate = (scaled_back * pre_up * sigma * (1.0 + pre_gate * (1.0 - sigma))).astype(
        jnp.bfloat16
    )
    grad_pre_up = (scaled_back * active).astype(jnp.bfloat16)
    scaled_rows = (gates[:, None] * g_rows.astype(jnp.float32)).astype(jnp.bfloat16)
    grad_one = sums[0] + lax.dot_general(
        x_rows, grad_pre_gate, contract_rows, preferred_element_type=jnp.float32
    )
    grad_three = sums[1] + lax.dot_general(
        x_rows, grad_pre_up, contract_rows, preferred_element_type=jnp.float32
    )
    grad_two = sums[2] + lax.dot_general(
        scaled_rows, hidden, contract_rows, preferred_element_type=jnp.float32
    )
    rows_back = (
        lax.dot_general(grad_pre_gate, w_one, contract_hidden, preferred_element_type=jnp.float32)
        + lax.dot_general(grad_pre_up, w_three, contract_hidden, preferred_element_type=jnp.float32)
    ).astype(jnp.bfloat16)
    token_back = lax.dot_general(
        selector, rows_back, contract_rows, preferred_element_type=jnp.float32
    )
    return (token_back, gate_part, (grad_one, grad_three, grad_two))


def per_device(layer_inputs, out_grad, w_gate, w_up, w_down, slot_token, slot_gate):
    segment_count = lax.axis_size("section")
    segment_here = lax.axis_index("section")
    micro_count = layer_inputs.shape[1]
    tok_shard = layer_inputs.shape[2]
    width = layer_inputs.shape[3]
    tok_group = tok_shard * lax.axis_size("et")
    slot_count = slot_token.shape[2]
    w_one = w_gate[0]
    w_three = w_up[0]
    w_two = w_down[0]
    hidden_width = w_one.shape[1]
    zero_grad = jnp.zeros((width, hidden_width), jnp.float32)
    sums = (zero_grad, zero_grad, zero_grad)
    received = jnp.zeros((tok_shard, width), jnp.bfloat16)
    in_grads = jnp.zeros((micro_count, tok_shard, width), jnp.bfloat16)
    gate_grads = jnp.zeros((micro_count, slot_count), jnp.float32)
    micro_ids = jnp.arange(micro_count, dtype=jnp.int32)
    tick_total = micro_count + segment_count - 1
    for tick_index in range(tick_total):
        micro_index = tick_index - (segment_count - 1 - segment_here)
        is_valid = (micro_index >= 0) & (micro_index < micro_count)
        micro_safe = jnp.clip(micro_index, 0, micro_count - 1)
        own_grad = lax.dynamic_index_in_dim(out_grad, micro_safe, 0, keepdims=False)
        grad_shard = jnp.where(segment_here == segment_count - 1, own_grad, received)
        x_shard = lax.dynamic_index_in_dim(layer_inputs[0], micro_safe, 0, keepdims=False)
        x_full, g_full = (
            lax.all_gather(x_shard, "et", axis=0, tiled=True),
            lax.all_gather(grad_shard, "et", axis=0, tiled=True),
        )
        slots = lax.dynamic_index_in_dim(slot_token[0], micro_safe, 0, keepdims=False)
        gates = lax.dynamic_index_in_dim(slot_gate[0], micro_safe, 0, keepdims=False)
        selector = selector_of(slots, tok_group)

        def run_work(operands):
            return expert_backward(selector, x_full, g_full, gates, w_one, w_three, w_two, operands)

        def skip_work(operands):
            return (
                jnp.zeros((tok_group, width), jnp.float32),
                jnp.zeros((slot_count,), jnp.float32),
                operands,
            )

        token_back, gate_part, sums = lax.cond(is_valid, run_work, skip_work, sums)
        expert_mine = lax.psum_scatter(
            token_back.astype(jnp.bfloat16), "et", scatter_dimension=0, tiled=True
        ).astype(jnp.float32)
        new_grad = (grad_shard.astype(jnp.float32) + expert_mine).astype(jnp.bfloat16)
        micro_mask = is_valid & (micro_ids == micro_safe)
        in_grads = jnp.where(micro_mask[:, None, None], new_grad[None], in_grads)
        gate_full = lax.psum(gate_part, "et")
        gate_grads = jnp.where(micro_mask[:, None], gate_full[None], gate_grads)
        if tick_index + 1 < tick_total:
            received = from_behind(new_grad, "section", -1)
    reduced = jax.tree.map(
        lambda part: part.astype(jnp.float32),
        lax.psum_scatter(for_sending(sums), "dp", scatter_dimension=0, tiled=True),
    )
    scale = 1.0 / lax.axis_size("dp")
    grad_one = (reduced[0] * scale).astype(jnp.bfloat16)[None]
    grad_three = (reduced[1] * scale).astype(jnp.bfloat16)[None]
    grad_two = (reduced[2] * scale).astype(jnp.bfloat16)[None]
    return (in_grads[None], grad_one, grad_three, grad_two, gate_grads[None])


def solution(mesh):
    placed = (
        P("section", None, ("dp", "et"), None),
        P(None, ("dp", "et"), None),
        P("section", None, "et"),
        P("section", None, "et"),
        P("section", None, "et"),
        P("section", None, "dp"),
        P("section", None, "dp"),
    )
    return jax.shard_map(
        per_device,
        mesh=mesh,
        in_specs=placed,
        out_specs=(
            P("section", None, ("dp", "et"), None),
            P("section", "dp", "et"),
            P("section", "dp", "et"),
            P("section", "dp", "et"),
            P("section", None, "dp"),
        ),
        check_vma=False,
    )
```

profile of v0, /device:TPU:0, one launch (start us, length us, event | category | flops | bytes accessed | tf_op | source)
XLA Modules:
  0.0 1040.9 jit_solution(11976694757808886168)
XLA Ops:
  7.2 0.0 all-gather.9.cloned.1.call-start
  7.2 0.7 all-gather.9.cloned.1.call-update
  7.9 0.0 all-gather.5.cloned.1.call-start
  8.0 1.9 bitcast_select_fusion.1
  9.8 0.0 all-gather.5.cloned.1.call-update
  9.8 0.0 reduce-scatter.6.cloned.1.call-start
  9.9 0.7 fusion.12
  10.7 22.9 %all-gather.9.cloned.1.call-done = bf16[1,1,256,2048]{3,2,1,0:T(8,128)(2,1)} async-done(((bf16[1,1,128,2048]{3,2,1,0:T(8,128)(2,1)}), bf16[1,1,256,2048]{3,2,1,0:T(8,128)(2,1)}) %all-gather.9.cloned.1.call-update) | async-done | bytes 1048592 | tf_op jit(solution)/shard_map/all_gather | solution.py:85
  33.6 23.4 %all-gather.5.cloned.1.call-done = bf16[256,2048]{1,0:T(8,128)(2,1)} async-done(((bf16[128,2048]{1,0:T(8,128)(2,1)}), bf16[256,2048]{1,0:T(8,128)(2,1)}) %all-gather.5.cloned.1.call-update) | async-done | bytes 1048592 | tf_op jit(solution)/shard_map/all_gather | solution.py:86
  57.0 46.9 %conditional.2 = (bf16[256,2048]{0,1:T(8,128)(2,1)S(1)}, f32[128]{0:T(128)}, f32[2048,3584]{1,0:T(8,128)}, f32[2048,3584]{1,0:T(8,128)}, f32[2048,3584]{1,0:T(8,128)}) conditional(s32[]{:T(128)} %convert_element_type.116, () %tuple.24, (f32[128]{0:T(128)}, bf16[128,256]{1,0:T(8,128)(2,1)S(1)}, bf16[256,2048]{1,0:T(8,128)(2,1)}, ...), branch_computations={%region_0.1_spmd, %region_1.3_spmd} | conditional | flops 15445590016 | bytes 259723008 | solution.py:102
  57.0 0.6 broadcast.29
  57.6 0.1 broadcast.28
  57.6 13.4 %broadcast_in_dim.35.clone.1 = f32[2048,3584]{1,0:T(8,128)} broadcast(f32[]{:T(128)} %constant.35.clone), dimensions={} | broadcast | bytes 29360132 | tf_op jit(solution)/shard_map/broadcast_in_dim | solution.py:70
  71.0 13.4 %broadcast_in_dim.35.clone = f32[2048,3584]{1,0:T(8,128)} broadcast(f32[]{:T(128)} %constant.35.clone), dimensions={} | broadcast | bytes 29360132 | tf_op jit(solution)/shard_map/broadcast_in_dim | solution.py:70
  84.5 13.4 %broadcast_in_dim.35 = f32[2048,3584]{1,0:T(8,128)} broadcast(f32[]{:T(128)} %constant.35.clone), dimensions={} | broadcast | bytes 29360132 | tf_op jit(solution)/shard_map/broadcast_in_dim | solution.py:70
  103.8 0.0 copy-start.4
  103.9 0.0 copy-start.12
  103.9 1.4 copy.12
  105.3 0.0 reduce-scatter.6.cloned.1.call-update
  105.3 0.0 all-gather.7.cloned.1.call-start
  105.4 56.0 %reduce-scatter.6.cloned.1.call-done = bf16[128,2048]{1,0:T(8,128)(2,1)} async-done(((bf16[256,2048]{1,0:T(8,128)(2,1)}), bf16[128,2048]{1,0:T(8,128)(2,1)}) %reduce-scatter.6.cloned.1.call-update) | async-done | bytes 524304 | tf_op jit(solution)/shard_map/reduce_scatter | solution.py:103
  161.4 1.2 add_convert_fusion.1
  162.6 0.0 copy-start.9
  162.6 1.3 collective-permute-start
  163.9 2.5 collective-permute-done
  166.4 0.8 bitcast_select_fusion
  167.3 0.0 all-gather.7.cloned.1.call-update
  167.3 0.0 reduce-scatter.8.cloned.1.call-start
  167.4 21.4 %all-gather.7.cloned.1.call-done = bf16[256,2048]{1,0:T(8,128)(2,1)} async-done(((bf16[128,2048]{1,0:T(8,128)(2,1)}), bf16[256,2048]{1,0:T(8,128)(2,1)}) %all-gather.7.cloned.1.call-update) | async-done | bytes 1048592 | tf_op jit(solution)/shard_map/all_gather | solution.py:86
  188.8 0.0 copy-done.9
  188.8 101.0 %conditional.3 = (bf16[256,2048]{0,1:T(8,128)(2,1)S(1)}, f32[128]{0:T(128)S(1)}, f32[2048,3584]{1,0:T(8,128)}, f32[2048,3584]{1,0:T(8,128)}, f32[2048,3584]{1,0:T(8,128)}) conditional(s32[]{:T(128)} %convert_element_type.122, (f32[2048,3584]{1,0:T(8,128)}, f32[2048,3584]{1,0:T(8,128)}, f32[2048,3584]{1,0:T(8,128)}) %tuple.26, (f32[128]{0:T(128)S(1)}, ...), branch_computations={%region_4.5_spmd, %region_5.7_spmd} | conditional | flops 15467610112 | bytes 332596800 | solution.py:102
  188.8 1.5 convolution_convert_fusion.3
  190.3 0.3 convolution_convert_fusion.2
  190.6 0.0 copy-start.1
  190.6 7.4 fusion.20
  198.0 1.9 copy-done.1
  200.0 2.2 fusion.19
  202.1 9.0 multiply_reduce_fusion.1
  211.1 19.2 %convolution_add_fusion.3 = f32[2048,3584]{1,0:T(8,128)} fusion(f32[2048,3584]{1,0:T(8,128)} %get-tuple-element.57, bf16[128,2048]{1,0:T(8,128)(2,1)S(1)} %convolution_convert_fusion.2, bf16[128,3584]{1,0:T(8,128)(2,1)S(1)} %get-tuple-element.93), kind=kOutput, calls=%fused_computation.16 | convolution fusion | flops 1886388224 | bytes 60162048 | tf_op jit(solution)/shard_map/cond/branch_1_fun/dot_general | solution.py:39
  230.3 19.4 %convolution_add_fusion.2 = f32[2048,3584]{1,0:T(8,128)} fusion(f32[2048,3584]{1,0:T(8,128)} %get-tuple-element.58, bf16[128,2048]{1,0:T(8,128)(2,1)S(1)} %convolution_convert_fusion.2, bf16[128,3584]{1,0:T(8,128)(2,1)S(1)} %get-tuple-element.94), kind=kOutput, calls=%fused_computation.15 | convolution fusion | flops 1886388224 | bytes 60162048 | tf_op jit(solution)/shard_map/cond/branch_1_fun/dot_general | solution.py:42
  249.7 19.6 %convolution_add_fusion.1 = f32[2048,3584]{1,0:T(8,128)} fusion(f32[2048,3584]{1,0:T(8,128)} %get-tuple-element.59, bf16[128,3584]{1,0:T(8,128)(2,1)} %get-tuple-element.90, bf16[128,2048]{1,0:T(8,128)(2,1)S(1)} %convolution_convert_fusion.3, f32[128]{0:T(128)S(1)} %get-tuple-element.50), kind=kOutput, calls=%fused_computation.14 | convolution fusion | flops 1887174656 | bytes 60162560 | tf_op jit(solution)/shard_map/cond/branch_1_fun/dot_general | solution.py:45
  269.3 9.9 fusion.21
  279.2 10.2 convolution_bitcast_fusion.1
  289.7 1.4 copy.13
  291.1 0.0 reduce-scatter.8.cloned.1.call-update
  291.2 0.0 reduce-scatter.10.cloned.1.call-start
  291.2 16.5 %convert_element_type.126 = bf16[2048,3584]{1,0:T(8,128)(2,1)} convert(f32[2048,3584]{1,0:T(8,128)} %get-tuple-element.80) | non-fusion elementwise | flops 7340032 | bytes 44040192 | tf_op jit(solution)/shard_map/convert_element_type | solution.py:14
  307.7 0.0 reduce-scatter.10.cloned.1.call-update
  307.8 0.0 reduce-scatter.12.cloned.1.call-start
  307.8 16.6 %convert_element_type.129 = bf16[2048,3584]{1,0:T(8,128)(2,1)} convert(f32[2048,3584]{1,0:T(8,128)} %get-tuple-element.81) | non-fusion elementwise | flops 7340032 | bytes 44040192 | tf_op jit(solution)/shard_map/convert_element_type | solution.py:14
  324.4 0.0 reduce-scatter.12.cloned.1.call-update
  324.4 0.0 reduce-scatter.14.cloned.1.call-start
  324.5 16.4 %convert_element_type.132 = bf16[2048,3584]{1,0:T(8,128)(2,1)} convert(f32[2048,3584]{1,0:T(8,128)} %get-tuple-element.82) | non-fusion elementwise | flops 7340032 | bytes 44040192 | tf_op jit(solution)/shard_map/convert_element_type | solution.py:14
  340.9 0.0 reduce-scatter.14.cloned.1.call-update
  341.0 5.1 all-reduce
  346.1 0.5 fusion.13
  346.6 0.0 copy-done.3
  346.6 2.1 fusion.11
  348.7 203.2 %reduce-scatter.10.cloned.1.call-done = bf16[256,3584]{1,0:T(8,128)(2,1)} async-done(((bf16[2048,3584]{1,0:T(8,128)(2,1)}), bf16[256,3584]{1,0:T(8,128)(2,1)}) %reduce-scatter.10.cloned.1.call-update) | async-done | bytes 1835024 | tf_op jit(solution)/shard_map/reduce_scatter | solution.py:115
  551.8 3.0 fusion.7
  554.9 236.3 %reduce-scatter.12.cloned.1.call-done = bf16[256,3584]{1,0:T(8,128)(2,1)} async-done(((bf16[2048,3584]{1,0:T(8,128)(2,1)}), bf16[256,3584]{1,0:T(8,128)(2,1)}) %reduce-scatter.12.cloned.1.call-update) | async-done | bytes 1835024 | tf_op jit(solution)/shard_map/reduce_scatter | solution.py:115
  791.2 3.0 fusion.8
  794.2 236.3 %reduce-scatter.14.cloned.1.call-done = bf16[256,3584]{1,0:T(8,128)(2,1)} async-done(((bf16[2048,3584]{1,0:T(8,128)(2,1)}), bf16[256,3584]{1,0:T(8,128)(2,1)}) %reduce-scatter.14.cloned.1.call-update) | async-done | bytes 1835024 | tf_op jit(solution)/shard_map/reduce_scatter | solution.py:115
  1030.6 3.0 fusion.9
  (8 shorter events, 0.0 us)
Async XLA Ops:
  7.2 26.4 %all-gather.9.cloned.1.call-start = ((), (), s32[]{:S(2)}) async-start(), calls=%async_computation.12 | async-start | bytes 1572864 | tf_op jit(solution)/shard_map/all_gather | solution.py:85
  7.9 49.1 %all-gather.5.cloned.1.call-start = ((), (), s32[]{:S(2)}) async-start(), calls=%async_computation.5 | async-start | bytes 1572864 | tf_op jit(solution)/shard_map/all_gather | solution.py:86
  9.8 151.6 %reduce-scatter.6.cloned.1.call-start = ((), (), s32[]{:S(2)}) async-start(), calls=%async_computation.6 | async-start | bytes 1572864 | tf_op jit(solution)/shard_map/reduce_scatter | solution.py:103
  57.0 104.4 %copy-start.2 = (bf16[1,128,2048]{2,1,0:T(8,128)(2,1)S(1)}, bf16[1,128,2048]{2,1,0:T(8,128)(2,1)}, u32[]{:S(2)}) copy-start(bf16[1,128,2048]{2,1,0:T(8,128)(2,1)} %param.12) | copy-start | bytes 1572868
  103.8 84.9 %copy-start.4 = (bf16[1,1,256,2048]{3,2,1,0:T(8,128)(2,1)S(1)}, bf16[1,1,256,2048]{3,2,1,0:T(8,128)(2,1)}, u32[]{:S(2)}) copy-start(bf16[1,1,256,2048]{3,2,1,0:T(8,128)(2,1)} %all-gather.9.cloned.1.call-done) | copy-start | bytes 3145732
  103.9 84.9 %copy-start.12 = (f32[1,1,128]{2,1,0:T(1,128)S(1)}, f32[1,1,128]{2,1,0:T(1,128)}, u32[]{:S(2)}) copy-start(f32[1,1,128]{2,1,0:T(1,128)} %param.17) | copy-start | bytes 1540
  105.3 83.4 %all-gather.7.cloned.1.call-start = ((), (), s32[]{:S(2)}) async-start(), calls=%async_computation.7 | async-start | bytes 1572864 | tf_op jit(solution)/shard_map/all_gather | solution.py:86
  162.6 26.1 %copy-start.9 = (bf16[128,2048]{1,0:T(8,128)(2,1)}, bf16[128,2048]{1,0:T(8,128)(2,1)S(1)}, u32[]{:S(2)}) copy-start(bf16[128,2048]{1,0:T(8,128)(2,1)S(1)} %add_convert_fusion.1) | copy-start | bytes 1572868
  162.6 3.8 collective-permute-start
  167.3 179.3 %reduce-scatter.8.cloned.1.call-start = ((), (), s32[]{:S(2)}) async-start(), calls=%async_computation.8 | async-start | bytes 1572864 | tf_op jit(solution)/shard_map/reduce_scatter | solution.py:103
  190.6 9.4 copy-start.1
  291.2 260.7 %reduce-scatter.10.cloned.1.call-start = ((), (), s32[]{:S(2)}) async-start(), calls=%async_computation.9 | async-start | bytes 16515072 | tf_op jit(solution)/shard_map/reduce_scatter | solution.py:115
  307.8 483.4 %reduce-scatter.12.cloned.1.call-start = ((), (), s32[]{:S(2)}) async-start(), calls=%async_computation.10 | async-start | bytes 16515072 | tf_op jit(solution)/shard_map/reduce_scatter | solution.py:115
  324.4 706.1 %reduce-scatter.14.cloned.1.call-start = ((), (), s32[]{:S(2)}) async-start(), calls=%async_computation.11 | async-start | bytes 16515072 | tf_op jit(solution)/shard_map/reduce_scatter | solution.py:115
  340.9 5.6 copy-start.3
  340.9 5.6 copy-start.10
Sparse Core Ops, SparseCore 0:
  9.5 23.9 all-gather.8
  35.7 21.2 all-gather.4
  105.4 55.9 reduce-scatter.5
  167.4 21.2 all-gather.6
  291.3 20.3 reduce-scatter.7
  315.1 236.6 reduce-scatter.9
  555.4 235.7 reduce-scatter.11
  794.8 235.7 reduce-scatter.13
where the time goes:
time: 1050 us; the launch traced here: 1040 us
  waiting for transfers between devices  803 us (76%)
  matrix products  98.7 us (9%)
  other arithmetic  65.9 us (6%)
  local copies, waits for them, and re-layouts  45.7 us (4%)
  between operations  14.7 us (1%)
    reduce_scatter x3, waiting for transfers between devices, per_device(): lax.psum_scatter(for_sending(sums), 'dp', scatter_dimension=0, tiled=True)  676 us
    reduce_scatter x2, waiting for transfers between devices, per_device(): lax.psum_scatter(token_back.astype(jnp.bfloat16), 'et', scatter_dimension...  56 us
    convert_element_type x3, other arithmetic, for_sending(): a.astype(jnp.bfloat16)  49.6 us
    all_gather x2, waiting for transfers between devices, per_device(): lax.all_gather(grad_shard, 'et', axis=0, tiled=True)  44.8 us
    broadcast_in_dim x3, local copies, waits for them, and re-layouts, per_device(): zero_grad = jnp.zeros((width, hidden_width), jnp.float32)  40.2 us
    all_gather x1, waiting for transfers between devices, per_device(): lax.all_gather(x_shard, 'et', axis=0, tiled=True)  22.9 us
  transfers between devices with their start and end apart: 9, of which 8 were waited for; matrix products, arithmetic and copies ran while one was open for 6% of the time, Pallas kernels for 0%

commit v1 on v0

v1 whole, which is shorter than its diff:
```python
import jax
import jax.numpy as jnp
from jax import lax
from jax.experimental import pallas as pl
from jax.experimental.pallas import tpu as pltpu
from jax.sharding import PartitionSpec as P

F32 = jnp.float32
BF16 = jnp.bfloat16
BY_ROWS_T = (((1,), (1,)), ((), ()))
BY_ROWS = (((0,), (0,)), ((), ()))


def tile_of(width, most):
    return max(t for t in range(128, most + 1, 128) if width % t == 0)


def params():
    return pltpu.CompilerParams(
        dimension_semantics=("arbitrary",), vmem_limit_bytes=60 << 20
    )


def held(array):
    return pl.BlockSpec(
        array.shape, lambda i: (0,) * array.ndim, pipeline_mode=pl.Buffered(1)
    )


def columns(rows, tile):
    return pl.BlockSpec((rows, tile), lambda i: (0, i))


def forward_parts(pre_gate, pre_up):
    sigma = jax.nn.sigmoid(pre_gate)
    active = pre_gate * sigma
    slope = pre_up * sigma * (1.0 + pre_gate * (1.0 - sigma))
    return active, slope, active * pre_up


def stacked(refs):
    values = [ref[...] for ref in refs]
    return values[0] if len(values) == 1 else jnp.concatenate(values, axis=0)


def forward_rows(blocks, w_one, w_three):
    count, rows, (width, hidden) = len(blocks), sum(b.shape[0] for b in blocks), w_one.shape
    tile = tile_of(hidden, 512)

    def kernel(*refs):
        x_refs, (one, three, slope_ref, active_ref, hidden_ref) = refs[:count], refs[count:]
        x = stacked(x_refs)
        active, slope, product = forward_parts(
            jnp.dot(x, one[...], preferred_element_type=F32),
            jnp.dot(x, three[...], preferred_element_type=F32),
        )
        slope_ref[...] = slope.astype(BF16)
        active_ref[...] = active.astype(BF16)
        hidden_ref[...] = product.astype(BF16)

    return pl.pallas_call(
        kernel,
        grid=(hidden // tile,),
        in_specs=[held(b) for b in blocks] + [columns(width, tile)] * 2,
        out_specs=[columns(rows, tile)] * 3,
        out_shape=[jax.ShapeDtypeStruct((rows, hidden), BF16)] * 3,
        compiler_params=params(),
        cost_estimate=pl.CostEstimate(
            flops=4 * rows * width * hidden,
            bytes_accessed=4 * width * hidden + 6 * rows * hidden,
            transcendentals=rows * hidden,
        ),
        name="forward_rows",
    )(*blocks, w_one, w_three)


def backward_rows(x, g, gates, w_one, w_three, w_two, parts):
    rows, (width, hidden) = g.shape[0], w_one.shape
    tile = tile_of(hidden, 512)
    fresh = parts is None

    def kernel(*refs):
        if fresh:
            x_ref, g_ref, gate_ref, one, three, two, back_ref, part_ref, slope_ref, active_ref, hidden_ref, total = refs
        else:
            g_ref, gate_ref, one, three, two, slope_ref, active_ref, hidden_ref, back_ref, part_ref, total = refs
        step = pl.program_id(0)

        @pl.when(step == 0)
        def _():
            total[...] = jnp.zeros_like(total)
            part_ref[...] = jnp.zeros_like(part_ref)

        back = jnp.dot(g_ref[...], two[...], preferred_element_type=F32)
        if fresh:
            x = x_ref[...]
            active, slope, product = forward_parts(
                jnp.dot(x, one[...], preferred_element_type=F32),
                jnp.dot(x, three[...], preferred_element_type=F32),
            )
            product = product.astype(BF16)
            slope_ref[...] = slope.astype(BF16)
            active_ref[...] = active.astype(BF16)
            hidden_ref[...] = product
        else:
            active, slope, product = active_ref[...], slope_ref[...], hidden_ref[...]
        part_ref[...] += jnp.sum(product.astype(F32) * back, axis=1, keepdims=True)
        scaled = gate_ref[...] * back
        grad_gate = (scaled * slope.astype(F32)).astype(BF16)
        grad_up = (scaled * active.astype(F32)).astype(BF16)
        total[...] += lax.dot_general(
            grad_gate, one[...], BY_ROWS_T, preferred_element_type=F32
        ) + lax.dot_general(grad_up, three[...], BY_ROWS_T, preferred_element_type=F32)

        @pl.when(step == pl.num_programs(0) - 1)
        def _():
            back_ref[...] = total[...].astype(BF16)

    small = [x, g, gates] if fresh else [g, gates]
    whole = pl.BlockSpec((rows, width), lambda i: (0, 0))
    tiles = [columns(rows, tile)] * 3
    made = jax.ShapeDtypeStruct((rows, hidden), BF16)
    return pl.pallas_call(
        kernel,
        grid=(hidden // tile,),
        in_specs=[held(a) for a in small] + [columns(width, tile)] * 3 + ([] if fresh else tiles),
        out_specs=[whole, pl.BlockSpec((rows, 1), lambda i: (0, 0))] + (tiles if fresh else []),
        out_shape=[jax.ShapeDtypeStruct((rows, width), BF16), jax.ShapeDtypeStruct((rows, 1), F32)]
        + ([made] * 3 if fresh else []),
        scratch_shapes=[pltpu.VMEM((rows, width), F32)],
        compiler_params=params(),
        cost_estimate=pl.CostEstimate(
            flops=(10 if fresh else 6) * rows * width * hidden,
            bytes_accessed=6 * width * hidden,
            transcendentals=rows * hidden,
        ),
        name="backward_rows",
    )(*small, w_one, w_three, w_two, *([] if fresh else parts))


def weight_grads(x_blocks, s_blocks, replica, cut, w_two, groups, scale):
    count, size, (width, hidden) = len(s_blocks), s_blocks[0].shape[0], w_two.shape
    rows = count * size
    tile = tile_of(hidden, 512 if rows <= 1024 else 256)
    sizes = [group[0].shape[0] for group in groups]
    aligned = cut % 128 == 0

    def kernel(*refs):
        x_cuts, refs = refs[1 : 1 + count], refs[1 + count :]
        s_cuts, refs = refs[:count], refs[count:]
        s_refs, two, refs = refs[:count], refs[count], refs[count + 1 :]
        given, refs = refs[: 3 * len(sizes)], refs[3 * len(sizes) :]
        out_one, out_three, out_two, x_turned, s_turned, grad_gate, grad_up, product = refs

        @pl.when(pl.program_id(0) == 0)
        def _():
            x_turned[...] = stacked(x_cuts).T
            s_turned[...] = stacked(s_cuts).T

        back = jnp.dot(stacked(s_refs), two[...], preferred_element_type=F32)
        start = 0
        for index, group_rows in enumerate(sizes):
            slope_ref, active_ref, hidden_ref = given[3 * index : 3 * index + 3]
            piece = back[start : start + group_rows, :]
            here = pl.ds(start, group_rows)
            grad_gate[here, :] = (piece * slope_ref[...].astype(F32)).astype(BF16)
            grad_up[here, :] = (piece * active_ref[...].astype(F32)).astype(BF16)
            product[here, :] = hidden_ref[...]
            start += group_rows

        def put(out, left, right):
            out[...] = (jnp.dot(left[...], right[...], preferred_element_type=F32) * scale).astype(BF16)

        put(out_one, x_turned, grad_gate)
        put(out_three, x_turned, grad_up)
        put(out_two, s_turned, product)

    def by_tile(height):
        return pl.BlockSpec((height, tile), lambda i, at: (0, i))

    def kept_whole(shape, column=None):
        return pl.BlockSpec(shape, lambda i, at: (0, 0 if column is None else at[0]), pipeline_mode=pl.Buffered(1))

    if aligned:
        x_cuts, s_cuts = x_blocks, s_blocks
    else:
        x_cuts, s_cuts = (
            [lax.dynamic_slice_in_dim(b, replica * cut, cut, 1) for b in blocks] for blocks in (x_blocks, s_blocks)
        )
    place = replica if aligned else jnp.zeros_like(replica)
    return pl.pallas_call(
        kernel,
        grid_spec=pltpu.PrefetchScalarGridSpec(
            num_scalar_prefetch=1,
            grid=(hidden // tile,),
            in_specs=[kept_whole((size, cut), 0)] * (2 * count)
            + [kept_whole((size, width))] * count
            + [by_tile(width)]
            + [by_tile(group_rows) for group_rows in sizes for _ in range(3)],
            out_specs=[by_tile(cut)] * 3,
            scratch_shapes=[pltpu.VMEM((cut, rows), BF16)] * 2 + [pltpu.VMEM((rows, tile), BF16)] * 3,
        ),
        out_shape=[jax.ShapeDtypeStruct((cut, hidden), BF16)] * 3,
        compiler_params=params(),
        cost_estimate=pl.CostEstimate(
            flops=2 * rows * width * hidden + 6 * rows * cut * hidden,
            bytes_accessed=2 * width * hidden + 6 * rows * hidden + 6 * cut * hidden,
            transcendentals=0,
        ),
        name="weight_grads",
    )(place.reshape(1).astype(jnp.int32), *x_cuts, *s_cuts, *s_blocks, w_two, *[a for group in groups for a in group])


def ring_of(count):
    if count % 2:
        return list(range(count))
    return list(range(0, count, 2)) + list(range(count - 1, 0, -2))


def around(block, sections, count):
    walk = ring_of(count)

    def shift(step):
        return [
            (s * count + walk[i], s * count + walk[(i + step) % count])
            for s in range(sections)
            for i in range(count)
        ]

    axes = ("section", "dp")
    groups, ahead, behind = [[block]], block, block
    for _ in range((count - 1) // 2):
        ahead = lax.ppermute(ahead, axes, shift(1))
        behind = lax.ppermute(behind, axes, shift(-1))
        groups.append([ahead, behind])
    if count % 2 == 0:
        half = block.shape[0] // 2
        groups.append(
            [
                jnp.concatenate(
                    [
                        lax.ppermute(ahead[:half], axes, shift(1)),
                        lax.ppermute(behind[half:], axes, shift(-1)),
                    ],
                    axis=0,
                )
            ]
        )
    return groups


def per_device(layer_inputs, out_grad, w_gate, w_up, w_down, slot_token, slot_gate):
    sections, replicas = lax.axis_size("section"), lax.axis_size("dp")
    last = lax.axis_index("section") == sections - 1
    half, replica = lax.axis_index("et"), lax.axis_index("dp")
    w_one, w_three, w_two = w_gate[0], w_up[0], w_down[0]
    x_mine, dy_mine = layer_inputs[0, 0], out_grad[0]
    slots, gates = slot_token[0, 0], slot_gate[0, 0][:, None]
    shard, width = x_mine.shape
    cut = width // replicas
    last_only = [(2 * (sections - 1) + e, 2 * (sections - 1) + 1 - e) for e in range(2)]
    first_only = [(e, 1 - e) for e in range(2)]

    def swapped(value, pairs):
        return lax.ppermute(value, ("section", "et"), pairs)

    def selector(of):
        return (slots[:, None] == of * shard + jnp.arange(shard, dtype=jnp.int32)[None, :]).astype(BF16)

    pick_mine, pick_theirs = selector(half), selector(1 - half)

    def picked(mine, theirs):
        return (
            jnp.dot(pick_mine, mine, preferred_element_type=F32)
            + jnp.dot(pick_theirs, theirs, preferred_element_type=F32)
        ).astype(BF16)

    def placed_back(pick, dy, back_mine, back_theirs):
        added = lax.dot_general(pick, back_mine, BY_ROWS, preferred_element_type=F32) + lax.dot_general(
            pick, back_theirs, BY_ROWS, preferred_element_type=F32
        )
        return (dy.astype(F32) + added).astype(BF16)

    dy_theirs = swapped(dy_mine, last_only)
    x_theirs = swapped(x_mine, last_only + first_only)
    x_rows = picked(x_mine, x_theirs)
    g_last = picked(dy_mine, dy_theirs)
    x_groups = around(x_rows, sections, replicas)
    x_blocks = [block for group in x_groups for block in group]

    no_back = lambda: (jnp.zeros(x_rows.shape, BF16), jnp.zeros((x_rows.shape[0], 1), F32))
    back_last, part_last, *own = lax.cond(
        last,
        lambda: tuple(backward_rows(x_rows, g_last, gates, w_one, w_three, w_two, None)),
        lambda: (*no_back(), *forward_rows([x_rows], w_one, w_three)),
    )
    other_last = swapped(back_last, last_only)
    kept = [tuple(own), tuple(forward_rows(x_groups[1], w_one, w_three))]
    ig_mine = placed_back(pick_mine, dy_mine, back_last, other_last)
    ig_theirs = placed_back(pick_theirs, dy_theirs, back_last, other_last)
    down = [(1, 0)]
    dy_first_mine = lax.ppermute(ig_mine, "section", down)
    dy_first_theirs = lax.ppermute(ig_theirs, "section", down)
    kept.append(tuple(forward_rows(x_groups[2], w_one, w_three)))
    g_first = picked(dy_first_mine, dy_first_theirs)
    g_rows = jnp.where(last, g_last, g_first)
    s_rows = (gates * g_rows.astype(F32)).astype(BF16)
    s_blocks = [block for group in around(s_rows, sections, replicas) for block in group]

    back_first, part_first = lax.cond(
        last,
        no_back,
        lambda: tuple(backward_rows(None, g_first, gates, w_one, w_three, w_two, own)),
    )
    other_first = swapped(back_first, first_only)
    ig_first = placed_back(pick_mine, dy_first_mine, back_first, other_first)
    in_grad = jnp.where(last, ig_mine, ig_first)
    part = jnp.where(last, part_last, part_first)[:, 0]
    gate_grad = part + lax.ppermute(part, "et", first_only)
    rest = [block for group in x_groups[3:] for block in group]
    for start in range(0, len(rest), 4):
        kept.append(tuple(forward_rows(rest[start : start + 4], w_one, w_three)))

    grads = weight_grads(x_blocks, s_blocks, replica, cut, w_two, kept, 1.0 / replicas)
    return (in_grad[None, None], *[grad[None] for grad in grads], gate_grad[None, None])


def solution(mesh):
    placed = (
        P("section", None, ("dp", "et"), None),
        P(None, ("dp", "et"), None),
        P("section", None, "et"),
        P("section", None, "et"),
        P("section", None, "et"),
        P("section", None, "dp"),
        P("section", None, "dp"),
    )
    return jax.shard_map(
        per_device,
        mesh=mesh,
        in_specs=placed,
        out_specs=(
            P("section", None, ("dp", "et"), None),
            P("section", "dp", "et"),
            P("section", "dp", "et"),
            P("section", "dp", "et"),
            P("section", None, "dp"),
        ),
        check_vma=False,
    )
```

time: 1050 us -> 192 us (0.18)
  waiting for transfers between devices: 803 us -> 34.3 us
  Pallas kernels: 0 us -> 116 us
  matrix products: 98.7 us -> 7.13 us
  other arithmetic: 65.9 us -> 1.5 us
  local copies, waits for them, and re-layouts: 45.7 us -> 2.68 us
  starting transfers between devices: 1.62 us -> 28.6 us
  between operations: 14.7 us -> 1.13 us
    reduce_scatter x5 -> x0, waiting for transfers between devices: 732 us -> none  [the longest x3 676 us: per_device(): lax.psum_scatter(for_sending(sums), 'dp', scatter_dimension=0, tiled=True)]
    pallas_call x0 -> x6, Pallas kernels: none -> 116 us  [the longest x4 66.6 us: forward_rows(): pl.pallas_call(kernel, grid=(hidden // tile,), in_specs=[held(b) for b in...]
    dot_general x10 -> x12, matrix products: 98.7 us -> 7.13 us  [the longest x3 2.78 us: picked(): jnp.dot(pick_mine, mine, preferred_element_type=F32)]
    all_gather x3 -> x0, waiting for transfers between devices: 67.7 us -> none  [the longest x2 44.8 us: per_device(): lax.all_gather(grad_shard, 'et', axis=0, tiled=True)]
    convert_element_type x5 -> x0, other arithmetic: 51.5 us -> none  [the longest x3 49.6 us: for_sending(): a.astype(jnp.bfloat16)]
    broadcast_in_dim x3 -> x0, local copies, waits for them, and re-layouts: 40.2 us -> none  [per_device(): zero_grad = jnp.zeros((width, hidden_width), jnp.float32)]
    ppermute x1 -> x23, waiting for transfers between devices: 2.5 us -> 34.3 us  [the longest x6 13.8 us: around(): behind = lax.ppermute(behind, axes, shift(-1))]
    ppermute x1 -> x23, starting transfers between devices: 1.29 us -> 28.6 us  [the longest x6 10.4 us: around(): behind = lax.ppermute(behind, axes, shift(-1))]
  transfers between devices with their start and end apart: 9 -> 23, of which waited for: 8 -> 6; matrix products, arithmetic and copies ran while one was open for 6% -> 5% of each run, Pallas kernels for 0% -> 45%
where the time goes in v1:
time: 192 us
  Pallas kernels  116 us (60%)
  waiting for transfers between devices  34.3 us (18%)
  starting transfers between devices  28.6 us (15%)
  matrix products  7.13 us (4%)
  local copies, waits for them, and re-layouts  2.68 us (1%)
    pallas_call x4, Pallas kernels, forward_rows(): pl.pallas_call(kernel, grid=(hidden // tile,), in_specs=[held(b) for b in...  66.6 us
    pallas_call x1, Pallas kernels, weight_grads(): pl.pallas_call(kernel, grid_spec=pltpu.PrefetchScalarGridSpec(num_scalar_...  29.8 us
    pallas_call x1, Pallas kernels, backward_rows(): pl.pallas_call(kernel, grid=(hidden // tile,), in_specs=[held(a) for a in...  20.1 us
    ppermute x6, waiting for transfers between devices, around(): behind = lax.ppermute(behind, axes, shift(-1))  13.8 us
    ppermute x6, starting transfers between devices, around(): behind = lax.ppermute(behind, axes, shift(-1))  10.4 us
    ppermute x4, waiting for transfers between devices, swapped(): return lax.ppermute(value, ('section', 'et'), pairs)  10.3 us
    ppermute x4, starting transfers between devices, swapped(): return lax.ppermute(value, ('section', 'et'), pairs)  8.19 us
    ppermute x1, waiting for transfers between devices, per_device(): dy_first_theirs = lax.ppermute(ig_theirs, 'section', down)  6.92 us
  transfers between devices with their start and end apart: 23, of which 6 were waited for; matrix products, arithmetic and copies ran while one was open for 5% of the time, Pallas kernels for 45%

profile of v1, /device:TPU:0, one launch (start us, length us, event | category | flops | bytes accessed | tf_op | source)
XLA Modules:
  0.0 191.8 jit_solution(1632528539409075083)
XLA Ops:
  0.6 0.0 copy-start.7
  0.7 0.8 collective-permute-start.1
  1.5 3.0 %collective-permute-start = (bf16[128,2048]{1,0:T(8,128)(2,1)}, bf16[128,2048]{1,0:T(8,128)(2,1)S(1)}, u32[]{:S(2)}, u32[]{:S(2)}) collective-permute-start(bf16[128,2048]{1,0:T(8,128)(2,1)} %bitcast.47), channel_id=1, source_target_pairs={{16,24},{24,16},{0,8},{8,0},{17,25},{25,17},{1,9},{9,1},{18,26},{2... | collective-permute-start | bytes 1572872 | tf_op jit(solution)/shard_map/ppermute | solution.py:265
  4.5 1.4 fusion.14
  5.9 1.0 fusion.16
  6.9 0.0 copy-start.8
  7.0 10.3 %collective-permute-done = bf16[128,2048]{1,0:T(8,128)(2,1)S(1)} collective-permute-done((bf16[128,2048]{1,0:T(8,128)(2,1)}, bf16[128,2048]{1,0:T(8,128)(2,1)S(1)}, u32[]{:S(2)}, u32[]{:S(2)}) %collective-permute-start) | collective-permute-done | bytes 524320 | tf_op jit(solution)/shard_map/ppermute | solution.py:265
  17.2 0.3 fusion.1.refs_1_
  17.6 2.4 %collective-permute-start.7 = (bf16[128,2048]{1,0:T(8,128)(2,1)S(1)}, bf16[128,2048]{1,0:T(8,128)(2,1)}, u32[]{:S(2)}, u32[]{:S(2)}) collective-permute-start(bf16[128,2048]{1,0:T(8,128)(2,1)S(1)} %fusion.1.refs_1_), channel_id=1, source_target_pairs={{0,1},{2,0},{4,2},{6,4},{7,6},{5,7},{3,5},{1,3},{16,17},{18,16},{2... | collective-permute-start | bytes 1572872 | tf_op jit(solution)/shard_map/ppermute | solution.py:234
  20.0 0.1 collective-permute-start.6
  20.1 0.3 fusion.2
  20.4 13.9 %conditional.2 = ((bf16[128,2048]{1,0:T(8,128)(2,1)S(1)}, f32[128,1]{1,0:T(8,128)S(1)}, bf16[128,3584]{1,0:T(8,128)(2,1)}, bf16[128,3584]{1,0:T(8,128)(2,1)}, bf16[128,3584]{1,0:T(8,128)(2,1)})) conditional(s32[]{:T(128)} %convert_element_type.40, (bf16[128,2048]{1,0:T(8,128)(2,1)S(1)}, bf16[2048,3584]{1,0:T(8,128)(2,1)}, ...), branch_computations={%region_0.0_spmd, %region_1.0_spmd} | conditional | flops 9395240960 | bytes 44041224 | solution.py:292
  20.5 13.8 %forward_rows.4 = (bf16[128,3584]{1,0:T(8,128)(2,1)}, bf16[128,3584]{1,0:T(8,128)(2,1)}, bf16[128,3584]{1,0:T(8,128)(2,1)}) custom-call(bf16[128,2048]{1,0:T(8,128)(2,1)S(1)} %get-tuple-element.34.refs_0_, bf16[2048,3584]{1,0:T(8,128)(2,1)} %get-tuple-element.35.refs_1_, bf16[2048,3584]{1,0:T(8,128)(2,1)} %get-tuple-element.36.refs_2_), custom_call_target="tpu_custom_call" | custom-call | flops 3758096384 | bytes 32112640 | tf_op jit(solution)/shard_map/cond/branch_0_fun/forward_rows/pallas_call | solution.py:61
  34.3 0.0 copy-start
  34.3 0.8 collective-permute-start.2
  35.2 0.4 fusion.23
  35.6 0.4 fusion.12
  36.0 0.4 fusion.3
  36.5 1.3 collective-permute-start.3
  37.8 0.4 add_convert_fusion.1
  38.2 1.3 collective-permute-start.4
  39.5 2.0 %collective-permute-start.9 = (bf16[128,2048]{1,0:T(8,128)(2,1)}, bf16[128,2048]{1,0:T(8,128)(2,1)}, u32[]{:S(2)}, u32[]{:S(2)}) collective-permute-start(bf16[128,2048]{1,0:T(8,128)(2,1)} %collective-permute-done.7.refs_1_.refs_3_), channel_id=1, source_target_pairs={{0,1},{2,0},{4,2},{6,4},{7,6},{5,7},{3,5},{1,3},{16,17},{18,16},{2... | collective-permute-start | bytes 1572872 | tf_op jit(solution)/shard_map/ppermute | solution.py:234
  41.4 0.1 collective-permute-start.8
  41.6 16.7 %forward_rows.5 = (bf16[256,3584]{1,0:T(8,128)(2,1)}, bf16[256,3584]{1,0:T(8,128)(2,1)}, bf16[256,3584]{1,0:T(8,128)(2,1)}) custom-call(bf16[128,2048]{1,0:T(8,128)(2,1)} %collective-permute-done.6.refs_0_.refs_2_, bf16[128,2048]{1,0:T(8,128)(2,1)} %collective-permute-done.7.refs_1_.refs_3_, bf16[2048,3584]{1,0:T(8,128)(2,1)} %bitcast.33, ...), custom_call_target="tpu_custom_call" | custom-call | flops 7516192768 | bytes 34865152 | tf_op jit(solution)/shard_map/forward_rows/pallas_call | solution.py:61
  58.3 6.9 %collective-permute-done.4 = bf16[128,2048]{1,0:T(8,128)(2,1)S(1)} collective-permute-done((bf16[128,2048]{1,0:T(8,128)(2,1)S(1)}, bf16[128,2048]{1,0:T(8,128)(2,1)S(1)}, u32[]{:S(2)}, u32[]{:S(2)}) %collective-permute-start.4) | collective-permute-done | bytes 524320 | tf_op jit(solution)/shard_map/ppermute | solution.py:303
  65.2 0.3 fusion.20
  65.6 0.4 multiply_convert_fusion
  66.0 1.7 collective-permute-start.15
  67.7 0.4 collective-permute-start.14
  68.1 20.8 %conditional.3 = ((bf16[128,2048]{1,0:T(8,128)(2,1)S(1)}, f32[128,1]{1,0:T(8,128)S(1)})) conditional(s32[]{:T(128)} %convert_element_type.40, (bf16[128,2048]{1,0:T(8,128)(2,1)S(1)}, f32[128,1]{0,1:T(1,128)S(1)}, bf16[2048,3584]{1,0:T(8,128)(2,1)}, bf16[2048,3584]{1,0:T(8,128)(2,1)}, bf16[2048,3584]{1,0:T(8,128)(2,1)}, ...), branch_computations={%region_2.3_spmd, %region_3.4_spmd} | conditional | flops 5637144576 | bytes 44041224 | solution.py:310
  68.1 0.7 copy.15.refs_1_
  68.8 20.1 %backward_rows.3 = (bf16[128,2048]{1,0:T(8,128)(2,1)S(1)}, f32[128,1]{1,0:T(8,128)S(1)}) custom-call(bf16[128,2048]{1,0:T(8,128)(2,1)S(1)} %get-tuple-element.46.refs_0_, f32[128,1]{1,0:T(8,128)} %copy.15.refs_1_, bf16[2048,3584]{1,0:T(8,128)(2,1)} %get-tuple-element.48.refs_2_, bf16[2048,3584]{1,0:T(8,128)(2,1)} %get-tuple-element.49.refs_3_, ...), custom_call_target="tpu_custom_call" | custom-call | flops 5637144576 | bytes 44040192 | tf_op jit(solution)/shard_map/cond/branch_0_fun/backward_rows/pallas_call | solution.py:123
  88.9 3.5 %collective-permute-start.5 = (bf16[128,2048]{1,0:T(8,128)(2,1)S(1)}, bf16[128,2048]{1,0:T(8,128)(2,1)S(1)}, u32[]{:S(2)}, u32[]{:S(2)}) collective-permute-start(bf16[128,2048]{1,0:T(8,128)(2,1)S(1)} %get-tuple-element.82), channel_id=1, source_target_pairs={{0,8},{8,0},{1,9},{9,1},{2,10},{10,2},{3,11},{11,3},{4,12},{12,4},... | collective-permute-start | bytes 1572872 | tf_op jit(solution)/shard_map/ppermute | solution.py:265
  92.4 1.6 collective-permute-start.11
  94.0 0.5 collective-permute-start.10
  94.5 16.8 %forward_rows.6 = (bf16[256,3584]{1,0:T(8,128)(2,1)}, bf16[256,3584]{1,0:T(8,128)(2,1)}, bf16[256,3584]{1,0:T(8,128)(2,1)}) custom-call(bf16[128,2048]{1,0:T(8,128)(2,1)} %collective-permute-done.8.refs_0_.refs_4_, bf16[128,2048]{1,0:T(8,128)(2,1)} %collective-permute-done.9.refs_1_.refs_5_, bf16[2048,3584]{1,0:T(8,128)(2,1)} %bitcast.35, ...), custom_call_target="tpu_custom_call" | custom-call | flops 7516192768 | bytes 34865152 | tf_op jit(solution)/shard_map/forward_rows/pallas_call | solution.py:61
  111.3 0.0 collective-permute-done.15.refs_11_.refs_19_
  111.3 1.6 collective-permute-start.17
  112.9 0.5 collective-permute-start.16
  113.4 0.1 select_reduce_fusion
  113.5 0.0 collective-permute-done.10.refs_0_.refs_6_
  113.5 0.5 collective-permute-start.22
  114.0 0.4 fusion.8
  114.4 2.7 %collective-permute-done.22 = f32[128]{0:T(128)S(1)} collective-permute-done((f32[128]{0:T(128)S(1)}, f32[128]{0:T(128)S(1)}, u32[]{:S(2)}, u32[]{:S(2)}) %collective-permute-start.22) | collective-permute-done | bytes 544 | tf_op jit(solution)/shard_map/ppermute | solution.py:319
  117.1 1.6 collective-permute-start.12
  118.7 0.5 add_bitcast_fusion
  119.2 1.0 slice.17
  120.2 0.5 collective-permute-start.13
  120.7 5.6 %collective-permute-done.17.refs_13_.refs_21_ = bf16[128,2048]{1,0:T(8,128)(2,1)S(1)} collective-permute-done((bf16[128,2048]{1,0:T(8,128)(2,1)}, bf16[128,2048]{1,0:T(8,128)(2,1)S(1)}, u32[]{:S(2)}, u32[]{:S(2)}) %collective-permute-start.17) | collective-permute-done | bytes 524320 | tf_op jit(solution)/shard_map/ppermute | solution.py:234
  126.4 1.3 collective-permute-start.19
  127.7 0.0 collective-permute-done.16.refs_12_.refs_20_
  127.7 0.7 collective-permute-start.18
  128.4 0.0 collective-permute-done.5
  128.4 1.3 fusion.6
  129.7 0.5 collective-permute-done.12
  130.2 0.0 collective-permute-done.13
  130.3 8.2 %collective-permute-done.19.refs_15_.refs_23_ = bf16[128,2048]{1,0:T(8,128)(2,1)S(1)} collective-permute-done((bf16[128,2048]{1,0:T(8,128)(2,1)S(1)}, bf16[128,2048]{1,0:T(8,128)(2,1)S(1)}, u32[]{:S(2)}, u32[]{:S(2)}) %collective-permute-start.19) | collective-permute-done | bytes 524320 | tf_op jit(solution)/shard_map/ppermute | solution.py:234
  138.5 1.2 collective-permute-start.21
  139.7 0.8 copy-done.5
  140.5 1.2 collective-permute-start.20
  141.7 19.3 %forward_rows.7 = (bf16[384,3584]{1,0:T(8,128)(2,1)}, bf16[384,3584]{1,0:T(8,128)(2,1)}, bf16[384,3584]{1,0:T(8,128)(2,1)}) custom-call(bf16[128,2048]{1,0:T(8,128)(2,1)} %copy-done.3, bf16[128,2048]{1,0:T(8,128)(2,1)} %collective-permute-done.11.refs_1_.refs_7_, bf16[128,2048]{1,0:T(8,128)(2,1)} %copy-done.6, bf16[2048,3584]{1,0:T(8,128)(2,1)} %bitcast.36, ...), custom_call_target="tpu_custom_call" | custom-call | flops 11274289152 | bytes 37617664 | tf_op jit(solution)/shard_map/forward_rows/pallas_call | solution.py:61
  160.9 0.0 collective-permute-done.21
  161.0 0.9 pad_maximum_fusion.refs_16_.refs_24_
  161.8 29.8 %weight_grads.1 = (bf16[256,3584]{1,0:T(8,128)(2,1)}, bf16[256,3584]{1,0:T(8,128)(2,1)}, bf16[256,3584]{1,0:T(8,128)(2,1)}) custom-call(s32[1]{0:T(128)} %bitcast.8.refs_0_, bf16[128,2048]{1,0:T(8,128)(2,1)S(1)} %fusion.1.refs_1_, bf16[128,2048]{1,0:T(8,128)(2,1)} %collective-permute-done.6.refs_0_.refs_2_, ...), custom_call_target="tpu_custom_call" | custom-call | flops 20669530112 | bytes 42205184 | tf_op jit(solution)/shard_map/weight_grads/pallas_call | solution.py:191
  (38 shorter events, 0.2 us)
Async XLA Ops:
  0.6 5.3 %copy-start.1 = (bf16[1,1,128,2048]{3,2,1,0:T(8,128)(2,1)S(1)}, bf16[1,1,128,2048]{3,2,1,0:T(8,128)(2,1)}, u32[]{:S(2)}) copy-start(bf16[1,1,128,2048]{3,2,1,0:T(8,128)(2,1)} %param.11) | copy-start | bytes 1572868
  0.6 16.6 %copy-start.7 = (s32[1,1,128]{2,1,0:T(1,128)S(1)}, s32[1,1,128]{2,1,0:T(1,128)}, u32[]{:S(2)}) copy-start(s32[1,1,128]{2,1,0:T(1,128)} %param.16) | copy-start | bytes 1540
  0.7 19.4 %collective-permute-start.1 = (bf16[128,2048]{1,0:T(8,128)(2,1)}, bf16[128,2048]{1,0:T(8,128)(2,1)S(1)}, u32[]{:S(2)}, u32[]{:S(2)}) collective-permute-start(bf16[128,2048]{1,0:T(8,128)(2,1)} %bitcast.46), channel_id=1, source_target_pairs={{16,24},{24,16},{17,25},{25,17},{18,26},{26,18},{19,27},{27,19},{2... | collective-permute-start | bytes 1572872 | tf_op jit(solution)/shard_map/ppermute | solution.py:265
  1.5 15.7 %collective-permute-start = (bf16[128,2048]{1,0:T(8,128)(2,1)}, bf16[128,2048]{1,0:T(8,128)(2,1)S(1)}, u32[]{:S(2)}, u32[]{:S(2)}) collective-permute-start(bf16[128,2048]{1,0:T(8,128)(2,1)} %bitcast.47), channel_id=1, source_target_pairs={{16,24},{24,16},{0,8},{8,0},{17,25},{25,17},{1,9},{9,1},{18,26},{2... | collective-permute-start | bytes 1572872 | tf_op jit(solution)/shard_map/ppermute | solution.py:265
  6.9 13.5 %copy-start.8 = (f32[1,1,128]{2,1,0:T(1,128)S(1)}, f32[1,1,128]{2,1,0:T(1,128)}, u32[]{:S(2)}) copy-start(f32[1,1,128]{2,1,0:T(1,128)} %param.17) | copy-start | bytes 1540
  17.6 21.9 %collective-permute-start.7 = (bf16[128,2048]{1,0:T(8,128)(2,1)S(1)}, bf16[128,2048]{1,0:T(8,128)(2,1)}, u32[]{:S(2)}, u32[]{:S(2)}) collective-permute-start(bf16[128,2048]{1,0:T(8,128)(2,1)S(1)} %fusion.1.refs_1_), channel_id=1, source_target_pairs={{0,1},{2,0},{4,2},{6,4},{7,6},{5,7},{3,5},{1,3},{16,17},{18,16},{2... | collective-permute-start | bytes 1572872 | tf_op jit(solution)/shard_map/ppermute | solution.py:234
  20.0 21.5 %collective-permute-start.6 = (bf16[128,2048]{1,0:T(8,128)(2,1)S(1)}, bf16[128,2048]{1,0:T(8,128)(2,1)}, u32[]{:S(2)}, u32[]{:S(2)}) collective-permute-start(bf16[128,2048]{1,0:T(8,128)(2,1)S(1)} %fusion.1.refs_1_), channel_id=1, source_target_pairs={{0,2},{2,4},{4,6},{6,7},{7,5},{5,3},{3,1},{1,0},{16,18},{18,20},{2... | collective-permute-start | bytes 1572872 | tf_op jit(solution)/shard_map/ppermute | solution.py:233
  34.3 1.7 copy-start
  34.3 1.7 collective-permute-start.2
  36.5 29.1 %collective-permute-start.3 = (bf16[128,2048]{1,0:T(8,128)(2,1)S(1)}, bf16[128,2048]{1,0:T(8,128)(2,1)S(1)}, u32[]{:S(2)}, u32[]{:S(2)}) collective-permute-start(bf16[128,2048]{1,0:T(8,128)(2,1)S(1)} %fusion.3), channel_id=1, source_target_pairs={{16,0},{17,1},{18,2},{19,3},{20,4},{21,5},{22,6},{23,7},{24,8},{25... | collective-permute-start | bytes 1572872 | tf_op jit(solution)/shard_map/ppermute | solution.py:302
  38.2 27.1 %collective-permute-start.4 = (bf16[128,2048]{1,0:T(8,128)(2,1)S(1)}, bf16[128,2048]{1,0:T(8,128)(2,1)S(1)}, u32[]{:S(2)}, u32[]{:S(2)}) collective-permute-start(bf16[128,2048]{1,0:T(8,128)(2,1)S(1)} %add_convert_fusion.1), channel_id=1, source_target_pairs={{16,0},{17,1},{18,2},{19,3},{20,4},{21,5},{22,6},{23,7},{24,8},{25... | collective-permute-start | bytes 1572872 | tf_op jit(solution)/shard_map/ppermute | solution.py:303
  39.5 52.9 %collective-permute-start.9 = (bf16[128,2048]{1,0:T(8,128)(2,1)}, bf16[128,2048]{1,0:T(8,128)(2,1)}, u32[]{:S(2)}, u32[]{:S(2)}) collective-permute-start(bf16[128,2048]{1,0:T(8,128)(2,1)} %collective-permute-done.7.refs_1_.refs_3_), channel_id=1, source_target_pairs={{0,1},{2,0},{4,2},{6,4},{7,6},{5,7},{3,5},{1,3},{16,17},{18,16},{2... | collective-permute-start | bytes 1572872 | tf_op jit(solution)/shard_map/ppermute | solution.py:234
  41.4 52.6 %collective-permute-start.8 = (bf16[128,2048]{1,0:T(8,128)(2,1)}, bf16[128,2048]{1,0:T(8,128)(2,1)}, u32[]{:S(2)}, u32[]{:S(2)}) collective-permute-start(bf16[128,2048]{1,0:T(8,128)(2,1)} %collective-permute-done.6.refs_0_.refs_2_), channel_id=1, source_target_pairs={{0,2},{2,4},{4,6},{6,7},{7,5},{5,3},{3,1},{1,0},{16,18},{18,20},{2... | collective-permute-start | bytes 1572872 | tf_op jit(solution)/shard_map/ppermute | solution.py:233
  66.0 2.1 %copy-start.2 = (bf16[128,2048]{1,0:T(8,128)(2,1)}, bf16[128,2048]{1,0:T(8,128)(2,1)S(1)}, u32[]{:S(2)}) copy-start(bf16[128,2048]{1,0:T(8,128)(2,1)S(1)} %get-tuple-element.125.refs_9_.refs_17_) | copy-start | bytes 1572868
  66.0 45.3 %collective-permute-start.15 = (bf16[128,2048]{1,0:T(8,128)(2,1)S(1)}, bf16[128,2048]{1,0:T(8,128)(2,1)}, u32[]{:S(2)}, u32[]{:S(2)}) collective-permute-start(bf16[128,2048]{1,0:T(8,128)(2,1)S(1)} %get-tuple-element.125.refs_9_.refs_17_), channel_id=1, source_target_pairs={{0,1},{2,0},{4,2},{6,4},{7,6},{5,7},{3,5},{1,3},{16,17},{18,16},{2... | collective-permute-start | bytes 1572872 | tf_op jit(solution)/shard_map/ppermute | solution.py:234
  67.7 45.2 %collective-permute-start.14 = (bf16[128,2048]{1,0:T(8,128)(2,1)S(1)}, bf16[128,2048]{1,0:T(8,128)(2,1)}, u32[]{:S(2)}, u32[]{:S(2)}) collective-permute-start(bf16[128,2048]{1,0:T(8,128)(2,1)S(1)} %get-tuple-element.125.refs_9_.refs_17_), channel_id=1, source_target_pairs={{0,2},{2,4},{4,6},{6,7},{7,5},{5,3},{3,1},{1,0},{16,18},{18,20},{2... | collective-permute-start | bytes 1572872 | tf_op jit(solution)/shard_map/ppermute | solution.py:233
  88.9 39.5 %collective-permute-start.5 = (bf16[128,2048]{1,0:T(8,128)(2,1)S(1)}, bf16[128,2048]{1,0:T(8,128)(2,1)S(1)}, u32[]{:S(2)}, u32[]{:S(2)}) collective-permute-start(bf16[128,2048]{1,0:T(8,128)(2,1)S(1)} %get-tuple-element.82), channel_id=1, source_target_pairs={{0,8},{8,0},{1,9},{9,1},{2,10},{10,2},{3,11},{11,3},{4,12},{12,4},... | collective-permute-start | bytes 1572872 | tf_op jit(solution)/shard_map/ppermute | solution.py:265
  92.4 26.8 %collective-permute-start.11 = (bf16[128,2048]{1,0:T(8,128)(2,1)}, bf16[128,2048]{1,0:T(8,128)(2,1)}, u32[]{:S(2)}, u32[]{:S(2)}) collective-permute-start(bf16[128,2048]{1,0:T(8,128)(2,1)} %collective-permute-done.9.refs_1_.refs_5_), channel_id=1, source_target_pairs={{0,1},{2,0},{4,2},{6,4},{7,6},{5,7},{3,5},{1,3},{16,17},{18,16},{2... | collective-permute-start | bytes 1572872 | tf_op jit(solution)/shard_map/ppermute | solution.py:234
  94.0 19.5 %collective-permute-start.10 = (bf16[128,2048]{1,0:T(8,128)(2,1)}, bf16[128,2048]{1,0:T(8,128)(2,1)S(1)}, u32[]{:S(2)}, u32[]{:S(2)}) collective-permute-start(bf16[128,2048]{1,0:T(8,128)(2,1)} %collective-permute-done.8.refs_0_.refs_4_), channel_id=1, source_target_pairs={{0,2},{2,4},{4,6},{6,7},{7,5},{5,3},{3,1},{1,0},{16,18},{18,20},{2... | collective-permute-start | bytes 1572872 | tf_op jit(solution)/shard_map/ppermute | solution.py:233
  111.3 15.1 %collective-permute-start.17 = (bf16[128,2048]{1,0:T(8,128)(2,1)}, bf16[128,2048]{1,0:T(8,128)(2,1)S(1)}, u32[]{:S(2)}, u32[]{:S(2)}) collective-permute-start(bf16[128,2048]{1,0:T(8,128)(2,1)} %collective-permute-done.15.refs_11_.refs_19_), channel_id=1, source_target_pairs={{0,1},{2,0},{4,2},{6,4},{7,6},{5,7},{3,5},{1,3},{16,17},{18,16},{2... | collective-permute-start | bytes 1572872 | tf_op jit(solution)/shard_map/ppermute | solution.py:234
  112.9 14.8 %collective-permute-start.16 = (bf16[128,2048]{1,0:T(8,128)(2,1)}, bf16[128,2048]{1,0:T(8,128)(2,1)S(1)}, u32[]{:S(2)}, u32[]{:S(2)}) collective-permute-start(bf16[128,2048]{1,0:T(8,128)(2,1)} %collective-permute-done.14.refs_10_.refs_18_), channel_id=1, source_target_pairs={{0,2},{2,4},{4,6},{6,7},{7,5},{5,3},{3,1},{1,0},{16,18},{18,20},{2... | collective-permute-start | bytes 1572872 | tf_op jit(solution)/shard_map/ppermute | solution.py:233
  113.5 28.2 %copy-start.3 = (bf16[128,2048]{1,0:T(8,128)(2,1)}, bf16[128,2048]{1,0:T(8,128)(2,1)S(1)}, u32[]{:S(2)}) copy-start(bf16[128,2048]{1,0:T(8,128)(2,1)S(1)} %collective-permute-done.10.refs_0_.refs_6_) | copy-start | bytes 1572868
  113.5 3.6 %collective-permute-start.22 = (f32[128]{0:T(128)S(1)}, f32[128]{0:T(128)S(1)}, u32[]{:S(2)}, u32[]{:S(2)}) collective-permute-start(f32[128]{0:T(128)S(1)} %select_reduce_fusion), channel_id=1, source_target_pairs={{0,8},{8,0},{1,9},{9,1},{2,10},{10,2},{3,11},{11,3},{4,12},{12,4},... | collective-permute-start | bytes 1544 | tf_op jit(solution)/shard_map/ppermute | solution.py:319
  117.1 13.1 %collective-permute-start.12 = (bf16[64,2048]{1,0:T(8,128)(2,1)S(1)}, bf16[64,2048]{1,0:T(8,128)(2,1)S(1)}, u32[]{:S(2)}, u32[]{:S(2)}) collective-permute-start(bf16[64,2048]{1,0:T(8,128)(2,1)S(1)} %slice.16), channel_id=1, source_target_pairs={{0,2},{2,4},{4,6},{6,7},{7,5},{5,3},{3,1},{1,0},{16,18},{18,20},{2... | collective-permute-start | bytes 786440 | tf_op jit(solution)/shard_map/ppermute | solution.py:242
  120.2 10.0 %collective-permute-start.13 = (bf16[64,2048]{1,0:T(8,128)(2,1)S(1)}, bf16[64,2048]{1,0:T(8,128)(2,1)S(1)}, u32[]{:S(2)}, u32[]{:S(2)}) collective-permute-start(bf16[64,2048]{1,0:T(8,128)(2,1)S(1)} %slice.17), channel_id=1, source_target_pairs={{0,1},{2,0},{4,2},{6,4},{7,6},{5,7},{3,5},{1,3},{16,17},{18,16},{2... | collective-permute-start | bytes 786440 | tf_op jit(solution)/shard_map/ppermute | solution.py:243
  126.3 3.9 %copy-start.9 = (bf16[128,2048]{1,0:T(8,128)(2,1)}, bf16[128,2048]{1,0:T(8,128)(2,1)S(1)}, u32[]{:S(2)}) copy-start(bf16[128,2048]{1,0:T(8,128)(2,1)S(1)} %collective-permute-done.17.refs_13_.refs_21_) | copy-start | bytes 1572868
  126.4 12.1 %collective-permute-start.19 = (bf16[128,2048]{1,0:T(8,128)(2,1)S(1)}, bf16[128,2048]{1,0:T(8,128)(2,1)S(1)}, u32[]{:S(2)}, u32[]{:S(2)}) collective-permute-start(bf16[128,2048]{1,0:T(8,128)(2,1)S(1)} %collective-permute-done.17.refs_13_.refs_21_), channel_id=1, source_target_pairs={{0,1},{2,0},{4,2},{6,4},{7,6},{5,7},{3,5},{1,3},{16,17},{18,16},{2... | collective-permute-start | bytes 1572872 | tf_op jit(solution)/shard_map/ppermute | solution.py:234
  127.7 2.6 %copy-start.10 = (bf16[128,2048]{1,0:T(8,128)(2,1)}, bf16[128,2048]{1,0:T(8,128)(2,1)S(1)}, u32[]{:S(2)}) copy-start(bf16[128,2048]{1,0:T(8,128)(2,1)S(1)} %collective-permute-done.16.refs_12_.refs_20_) | copy-start | bytes 1572868
  127.7 12.0 %collective-permute-start.18 = (bf16[128,2048]{1,0:T(8,128)(2,1)S(1)}, bf16[128,2048]{1,0:T(8,128)(2,1)S(1)}, u32[]{:S(2)}, u32[]{:S(2)}) collective-permute-start(bf16[128,2048]{1,0:T(8,128)(2,1)S(1)} %collective-permute-done.16.refs_12_.refs_20_), channel_id=1, source_target_pairs={{0,2},{2,4},{4,6},{6,7},{7,5},{5,3},{3,1},{1,0},{16,18},{18,20},{2... | collective-permute-start | bytes 1572872 | tf_op jit(solution)/shard_map/ppermute | solution.py:233
  130.3 11.4 %copy-start.6 = (bf16[128,2048]{1,0:T(8,128)(2,1)}, bf16[128,2048]{1,0:T(8,128)(2,1)S(1)}, u32[]{:S(2)}) copy-start(bf16[128,2048]{1,0:T(8,128)(2,1)S(1)} %constant_dynamic-update-slice_fusion.refs_2_.refs_8_) | copy-start | bytes 1572868
  138.5 1.2 copy-start.4
  138.5 22.5 %collective-permute-start.21 = (bf16[64,2048]{1,0:T(8,128)(2,1)S(1)}, bf16[64,2048]{1,0:T(8,128)(2,1)S(1)}, u32[]{:S(2)}, u32[]{:S(2)}) collective-permute-start(bf16[64,2048]{1,0:T(8,128)(2,1)S(1)} %slice.19), channel_id=1, source_target_pairs={{0,1},{2,0},{4,2},{6,4},{7,6},{5,7},{3,5},{1,3},{16,17},{18,16},{2... | collective-permute-start | bytes 786440 | tf_op jit(solution)/shard_map/ppermute | solution.py:243
  139.7 0.8 copy-start.5
  140.5 20.5 %collective-permute-start.20 = (bf16[64,2048]{1,0:T(8,128)(2,1)S(1)}, bf16[64,2048]{1,0:T(8,128)(2,1)S(1)}, u32[]{:S(2)}, u32[]{:S(2)}) collective-permute-start(bf16[64,2048]{1,0:T(8,128)(2,1)S(1)} %slice.18), channel_id=1, source_target_pairs={{0,2},{2,4},{4,6},{6,7},{7,5},{5,3},{3,1},{1,0},{16,18},{18,20},{2... | collective-permute-start | bytes 786440 | tf_op jit(solution)/shard_map/ppermute | solution.py:242

commit v2 on v1

v2 whole, which is shorter than its diff:
```python
import jax
import jax.numpy as jnp
from jax import lax
from jax.experimental import pallas as pl
from jax.experimental.pallas import tpu as pltpu
from jax.sharding import PartitionSpec as P

F32 = jnp.float32
BF16 = jnp.bfloat16
BY_ROWS_T = (((1,), (1,)), ((), ()))
BY_ROWS = (((0,), (0,)), ((), ()))


def tile_of(width, most):
    return max(t for t in range(128, most + 1, 128) if width % t == 0)


def params(mib):
    return pltpu.CompilerParams(dimension_semantics=("arbitrary",), vmem_limit_bytes=mib << 20)


def in_hbm(arrays):
    return [pltpu.with_memory_space_constraint(a, pltpu.HBM) for a in arrays]


RESIDENT = pl.BlockSpec(memory_space=pltpu.VMEM)


def load(*arrays):
    count = len(arrays)

    def kernel(*refs):
        copies = [
            pltpu.make_async_copy(refs[i], refs[count + i], refs[2 * count].at[i]) for i in range(count)
        ]
        for copy in copies:
            copy.start()
        for copy in copies:
            copy.wait()

    return pl.pallas_call(
        kernel,
        in_specs=[pl.BlockSpec(memory_space=pltpu.HBM)] * count,
        out_specs=[RESIDENT] * count,
        out_shape=[pltpu.VMEM(a.shape, a.dtype) for a in arrays],
        scratch_shapes=[pltpu.SemaphoreType.DMA((count,))],
        compiler_params=pltpu.CompilerParams(vmem_limit_bytes=1 << 20),
        cost_estimate=pl.CostEstimate(
            flops=0, bytes_accessed=sum(2 * a.size for a in arrays), transcendentals=0
        ),
        name="load",
    )(*in_hbm(arrays))


def slab(tile):
    return pl.ds(pl.multiple_of(pl.program_id(0) * tile, tile), tile)


def held(array):
    return pl.BlockSpec(
        array.shape, lambda i: (0,) * array.ndim, pipeline_mode=pl.Buffered(1)
    )


def columns(rows, tile):
    return pl.BlockSpec((rows, tile), lambda i: (0, i))


def forward_parts(pre_gate, pre_up):
    sigma = jax.nn.sigmoid(pre_gate)
    active = pre_gate * sigma
    slope = pre_up * sigma * (1.0 + pre_gate * (1.0 - sigma))
    return active, slope, active * pre_up


def stacked(refs):
    values = [ref[...] for ref in refs]
    return values[0] if len(values) == 1 else jnp.concatenate(values, axis=0)


def forward_rows(blocks, w_one, w_three):
    count, rows, (width, hidden) = len(blocks), sum(b.shape[0] for b in blocks), w_one.shape
    tile = tile_of(hidden, 512)

    def kernel(*refs):
        x_refs, (one, three, slope_ref, active_ref, hidden_ref) = refs[:count], refs[count:]
        x, here = stacked(x_refs), slab(tile)
        active, slope, product = forward_parts(
            jnp.dot(x, one[:, here], preferred_element_type=F32),
            jnp.dot(x, three[:, here], preferred_element_type=F32),
        )
        slope_ref[...] = slope.astype(BF16)
        active_ref[...] = active.astype(BF16)
        hidden_ref[...] = product.astype(BF16)

    return pl.pallas_call(
        kernel,
        grid=(hidden // tile,),
        in_specs=[held(b) for b in blocks] + [RESIDENT] * 2,
        out_specs=[columns(rows, tile)] * 3,
        out_shape=[pltpu.HBM((rows, hidden), BF16)] * 3,
        compiler_params=params(20),
        cost_estimate=pl.CostEstimate(
            flops=4 * rows * width * hidden,
            bytes_accessed=6 * rows * hidden,
            transcendentals=rows * hidden,
        ),
        name="forward_rows",
    )(*in_hbm(blocks), w_one, w_three)


def backward_rows(active_here, x_blocks, g, gates, w_one, w_three, w_two, parts):
    rows, (width, hidden) = g.shape[0], w_one.shape
    tile = tile_of(hidden, 512)
    count, height = len(x_blocks), sum(b.shape[0] for b in x_blocks)
    parts = parts or []

    def kernel(flag, *refs):
        x_refs, refs = refs[:count], refs[count:]
        g_ref, gate_ref, one, three, two, *refs = refs
        stored, refs = refs[: len(parts)], refs[len(parts) :]
        back_ref, part_ref, slope_ref, active_ref, hidden_ref, total = refs
        step, here = pl.program_id(0), slab(tile)

        @pl.when(step == 0)
        def _():
            total[...] = jnp.zeros_like(total)
            part_ref[...] = jnp.zeros_like(part_ref)

        x = stacked(x_refs)
        active, slope, product = forward_parts(
            jnp.dot(x, one[:, here], preferred_element_type=F32),
            jnp.dot(x, three[:, here], preferred_element_type=F32),
        )
        slope_ref[...] = slope.astype(BF16)
        active_ref[...] = active.astype(BF16)
        hidden_ref[...] = product.astype(BF16)

        @pl.when(flag[0] > 0)
        def _():
            slope_of, active_of, hidden_of = stored if parts else (slope_ref, active_ref, hidden_ref)
            back = jnp.dot(g_ref[...], two[...], preferred_element_type=F32)
            part_ref[...] += jnp.sum(hidden_of[...].astype(F32) * back, axis=1, keepdims=True)
            scaled = gate_ref[...] * back
            grad_gate = (scaled * slope_of[...].astype(F32)).astype(BF16)
            grad_up = (scaled * active_of[...].astype(F32)).astype(BF16)
            total[...] += lax.dot_general(
                grad_gate, one[:, here], BY_ROWS_T, preferred_element_type=F32
            ) + lax.dot_general(grad_up, three[:, here], BY_ROWS_T, preferred_element_type=F32)

        @pl.when(step == pl.num_programs(0) - 1)
        def _():
            back_ref[...] = total[...].astype(BF16)

    return pl.pallas_call(
        kernel,
        grid=(hidden // tile,),
        in_specs=[pl.BlockSpec(memory_space=pltpu.SMEM)]
        + [held(a) for a in (*x_blocks, g, gates)]
        + [RESIDENT] * 2
        + [columns(width, tile)]
        + [columns(rows, tile)] * len(parts),
        out_specs=[pl.BlockSpec((rows, width), lambda i: (0, 0)), pl.BlockSpec((rows, 1), lambda i: (0, 0))]
        + [columns(height, tile)] * 3,
        out_shape=[jax.ShapeDtypeStruct((rows, width), BF16), jax.ShapeDtypeStruct((rows, 1), F32)]
        + [pltpu.HBM((height, hidden), BF16)] * 3,
        scratch_shapes=[pltpu.VMEM((rows, width), F32)],
        compiler_params=params(20),
        cost_estimate=pl.CostEstimate(
            flops=(6 * rows + 4 * height) * width * hidden,
            bytes_accessed=2 * width * hidden,
            transcendentals=height * hidden,
        ),
        name="backward_rows",
    )(active_here.astype(jnp.int32).reshape(1), *in_hbm(x_blocks), g, gates, w_one, w_three, w_two, *in_hbm(parts))


def weight_grads(x_blocks, s_blocks, replica, cut, w_two, groups, before, scale):
    count, size, (width, hidden) = len(s_blocks), s_blocks[0].shape[0], w_two.shape
    rows = count * size
    tile = tile_of(hidden, 512 if rows <= 1024 else 256)
    sizes = [group[0].shape[0] for group in groups]
    aligned = cut % 128 == 0

    def kernel(*refs):
        x_cuts, refs = refs[1 : 1 + count], refs[1 + count :]
        s_cuts, refs = refs[:count], refs[count:]
        s_refs, two, refs = refs[:count], refs[count], refs[count + 1 :]
        given, refs = refs[: 3 * len(sizes)], refs[3 * len(sizes) :]
        sums, refs = refs[: len(before)], refs[len(before) :]
        out_one, out_three, out_two, x_turned, s_turned, grad_gate, grad_up, product = refs

        @pl.when(pl.program_id(0) == 0)
        def _():
            x_turned[...] = stacked(x_cuts).T
            s_turned[...] = stacked(s_cuts).T

        back = jnp.dot(stacked(s_refs), two[...], preferred_element_type=F32)
        start = 0
        for index, group_rows in enumerate(sizes):
            slope_ref, active_ref, hidden_ref = given[3 * index : 3 * index + 3]
            piece = back[start : start + group_rows, :]
            here = pl.ds(start, group_rows)
            grad_gate[here, :] = (piece * slope_ref[...].astype(F32)).astype(BF16)
            grad_up[here, :] = (piece * active_ref[...].astype(F32)).astype(BF16)
            product[here, :] = hidden_ref[...]
            start += group_rows

        for index, (out, left, right) in enumerate(
            ((out_one, x_turned, grad_gate), (out_three, x_turned, grad_up), (out_two, s_turned, product))
        ):
            value = jnp.dot(left[...], right[...], preferred_element_type=F32)
            if sums:
                value = sums[index][...] + value
            out[...] = value if scale is None else (value * scale).astype(BF16)

    def by_tile(height):
        return pl.BlockSpec((height, tile), lambda i, at: (0, i))

    def kept_whole(shape, column=None):
        return pl.BlockSpec(shape, lambda i, at: (0, 0 if column is None else at[0]), pipeline_mode=pl.Buffered(1))

    if aligned:
        x_cuts, s_cuts = x_blocks, s_blocks
    else:
        x_cuts, s_cuts = (
            [lax.dynamic_slice_in_dim(b, replica * cut, cut, 1) for b in blocks] for blocks in (x_blocks, s_blocks)
        )
    place = replica if aligned else jnp.zeros_like(replica)
    return pl.pallas_call(
        kernel,
        grid_spec=pltpu.PrefetchScalarGridSpec(
            num_scalar_prefetch=1,
            grid=(hidden // tile,),
            in_specs=[kept_whole((size, cut), 0)] * (2 * count)
            + [kept_whole((size, width))] * count
            + [by_tile(width)]
            + [by_tile(group_rows) for group_rows in sizes for _ in range(3)]
            + [by_tile(cut)] * len(before),
            out_specs=[by_tile(cut)] * 3,
            scratch_shapes=[pltpu.VMEM((cut, rows), BF16)] * 2 + [pltpu.VMEM((rows, tile), BF16)] * 3,
        ),
        out_shape=[pltpu.HBM((cut, hidden), F32 if scale is None else BF16)] * 3,
        compiler_params=params(40),
        cost_estimate=pl.CostEstimate(
            flops=2 * rows * width * hidden + 6 * rows * cut * hidden,
            bytes_accessed=2 * width * hidden + 6 * rows * hidden + 6 * cut * hidden,
            transcendentals=0,
        ),
        name="weight_grads",
    )(place.reshape(1).astype(jnp.int32), *in_hbm([*x_cuts, *s_cuts, *s_blocks, w_two, *[a for group in groups for a in group], *before]))


def ring_of(count):
    if count % 2:
        return list(range(count))
    return list(range(0, count, 2)) + list(range(count - 1, 0, -2))


def around(block, sections, count):
    walk = ring_of(count)

    def shift(step):
        return [
            (s * count + walk[i], s * count + walk[(i + step) % count])
            for s in range(sections)
            for i in range(count)
        ]

    axes = ("section", "dp")
    groups, ahead, behind = [[block]], block, block
    for _ in range(1, (count + 1) // 2):
        ahead = lax.ppermute(ahead, axes, shift(1))
        behind = lax.ppermute(behind, axes, shift(-1))
        groups.append([ahead, behind])
    if count % 2 == 0:
        half = block.shape[0] // 2
        front = lax.ppermute(ahead[:half], axes, shift(1))
        rear = lax.ppermute(behind[half:], axes, shift(-1))
        groups.append([jnp.concatenate([front, rear], axis=0)])
    return groups


def per_device(layer_inputs, out_grad, w_gate, w_up, w_down, slot_token, slot_gate):
    sections, replicas = lax.axis_size("section"), lax.axis_size("dp")
    last = lax.axis_index("section") == sections - 1
    half, replica = lax.axis_index("et"), lax.axis_index("dp")
    w_one, w_three, w_two = w_gate[0], w_up[0], w_down[0]
    x_mine, dy_mine = layer_inputs[0, 0], out_grad[0]
    slots, gates = slot_token[0, 0], slot_gate[0, 0][:, None]
    shard, width = x_mine.shape
    cut = width // replicas
    last_only = [(2 * (sections - 1) + e, 2 * (sections - 1) + 1 - e) for e in range(2)]
    first_only = [(e, 1 - e) for e in range(2)]

    def swapped(value, pairs):
        return lax.ppermute(value, ("section", "et"), pairs)

    def selector(of):
        return (slots[:, None] == of * shard + jnp.arange(shard, dtype=jnp.int32)[None, :]).astype(BF16)

    pick_mine, pick_theirs = selector(half), selector(1 - half)

    def picked(mine, theirs):
        return (
            jnp.dot(pick_mine, mine, preferred_element_type=F32)
            + jnp.dot(pick_theirs, theirs, preferred_element_type=F32)
        ).astype(BF16)

    def placed_back(pick, dy, back_mine, back_theirs):
        added = lax.dot_general(pick, back_mine, BY_ROWS, preferred_element_type=F32) + lax.dot_general(
            pick, back_theirs, BY_ROWS, preferred_element_type=F32
        )
        return (dy.astype(F32) + added).astype(BF16)

    dy_theirs = swapped(dy_mine, last_only)
    x_theirs = swapped(x_mine, last_only + first_only)
    w_one, w_three = load(w_one, w_three)
    x_rows = picked(x_mine, x_theirs)
    g_last = picked(dy_mine, dy_theirs)
    x_groups = around(x_rows, sections, replicas)

    def joined(groups):
        return [block for group in groups for block in group]

    back_last, part_last, *own = backward_rows(last, [x_rows], g_last, gates, w_one, w_three, w_two, None)
    other_last = swapped(back_last, last_only)
    ig_mine = placed_back(pick_mine, dy_mine, back_last, other_last)
    ig_theirs = placed_back(pick_theirs, dy_theirs, back_last, other_last)
    dy_first_mine = lax.ppermute(ig_mine, "section", [(1, 0)])
    dy_first_theirs = lax.ppermute(ig_theirs, "section", [(1, 0)])
    kept = [tuple(own), tuple(forward_rows(x_groups[1], w_one, w_three))]
    g_first = picked(dy_first_mine, dy_first_theirs)
    g_rows = jnp.where(last, g_last, g_first)
    s_rows = (gates * g_rows.astype(F32)).astype(BF16)
    s_groups = around(s_rows, sections, replicas)

    back_first, part_first, *third = backward_rows(
        jnp.logical_not(last), x_groups[2], g_first, gates, w_one, w_three, w_two, own
    )
    kept.append(tuple(third))
    other_first = swapped(back_first, first_only)
    part = jnp.where(last, part_last, part_first)[:, 0]
    gate_grad = part + lax.ppermute(part, "et", first_only)
    ig_first = placed_back(pick_mine, dy_first_mine, back_first, other_first)
    in_grad = jnp.where(last, ig_mine, ig_first)
    rest = joined(x_groups[3:])
    late = []
    for start in range(0, len(rest), 4):
        late.append(tuple(forward_rows(rest[start : start + 4], w_one, w_three)))

    sums = weight_grads(joined(x_groups[:3]), joined(s_groups[:3]), replica, cut, w_two, kept, [], None)
    far = joined(s_groups[3:])
    for index, group in enumerate(late):
        scale = 1.0 / replicas if index == len(late) - 1 else None
        here = slice(4 * index, 4 * index + 4)
        sums = weight_grads(rest[here], far[here], replica, cut, w_two, [group], sums, scale)
    return (in_grad[None, None], *[grad[None] for grad in sums], gate_grad[None, None])


def solution(mesh):
    placed = (
        P("section", None, ("dp", "et"), None),
        P(None, ("dp", "et"), None),
        P("section", None, "et"),
        P("section", None, "et"),
        P("section", None, "et"),
        P("section", None, "dp"),
        P("section", None, "dp"),
    )

    return jax.shard_map(
        per_device,
        mesh=mesh,
        in_specs=placed,
        out_specs=(
            P("section", None, ("dp", "et"), None),
            P("section", "dp", "et"),
            P("section", "dp", "et"),
            P("section", "dp", "et"),
            P("section", None, "dp"),
        ),
        check_vma=False,
    )
```

time: 192 us -> 224 us (1.17)
  local copies, waits for them, and re-layouts: 2.68 us -> 33 us
  Pallas kernels: 116 us -> 113 us
    pallas_call x4 -> x2, Pallas kernels: 66.6 us -> 27 us  [forward_rows(): pl.pallas_call(kernel, grid=(hidden // tile,), in_specs=[held(b) for b in...]
    unnamed x23 -> x45, local copies, waits for them, and re-layouts: 0.85 us -> 32.2 us
    pallas_call x1 -> x3, Pallas kernels: 20.1 us -> 46.9 us  [the longest x2 37.4 us: backward_rows(): pl.pallas_call(kernel, grid=(hidden // tile,), in_specs=[pl.BlockSpec(mem...]
    ppermute x6, waiting for transfers between devices: 7.45 us -> 24.8 us  [the longest x1 20.9 us: per_device(): dy_first_theirs = lax.ppermute(ig_theirs, 'section', [(1, 0)])]
    pallas_call x1 -> x2, Pallas kernels: 29.8 us -> 39.5 us  [weight_grads(): pl.pallas_call(kernel, grid_spec=pltpu.PrefetchScalarGridSpec(num_scalar_...]
    ppermute x4, waiting for transfers between devices: 10.3 us -> 2.11 us  [swapped(): return lax.ppermute(value, ('section', 'et'), pairs)]
    ppermute x6, waiting for transfers between devices: 13.8 us -> 9.31 us  [around(): behind = lax.ppermute(behind, axes, shift(-1))]
    dot_general x3, matrix products: 1.02 us -> 3.93 us  [picked(): jnp.dot(pick_theirs, theirs, preferred_element_type=F32)]
  transfers between devices with their start and end apart: 23 -> 23, of which waited for: 6 -> 5; matrix products, arithmetic and copies ran while one was open for 5% -> 5% of each run, Pallas kernels for 45% -> 31%
where the time goes in v2:
time: 224 us; the launch traced here: 223 us
  Pallas kernels  113 us (50%)
  waiting for transfers between devices  36.2 us (16%)
  local copies, waits for them, and re-layouts  33 us (15%)
  starting transfers between devices  28.4 us (13%)
  matrix products  9.37 us (4%)
    pallas_call x2, Pallas kernels, weight_grads(): pl.pallas_call(kernel, grid_spec=pltpu.PrefetchScalarGridSpec(num_scalar_...  39.5 us
    pallas_call x2, Pallas kernels, backward_rows(): pl.pallas_call(kernel, grid=(hidden // tile,), in_specs=[pl.BlockSpec(mem...  37.4 us
    unnamed x45, local copies, waits for them, and re-layouts  32.2 us
    pallas_call x2, Pallas kernels, forward_rows(): pl.pallas_call(kernel, grid=(hidden // tile,), in_specs=[held(b) for b in...  27 us
    ppermute x1, waiting for transfers between devices, per_device(): dy_first_theirs = lax.ppermute(ig_theirs, 'section', [(1, 0)])  20.9 us
    ppermute x6, starting transfers between devices, around(): behind = lax.ppermute(behind, axes, shift(-1))  10.7 us
    pallas_call x1, Pallas kernels, load(): pl.pallas_call(kernel, in_specs=[pl.BlockSpec(memory_space=pltpu.HBM)] *...  9.45 us
    ppermute x6, waiting for transfers between devices, around(): behind = lax.ppermute(behind, axes, shift(-1))  9.31 us
  transfers between devices with their start and end apart: 23, of which 5 were waited for; matrix products, arithmetic and copies ran while one was open for 5% of the time, Pallas kernels for 31%

profile of v2, /device:TPU:0, one launch (start us, length us, event | category | flops | bytes accessed | tf_op | source)
XLA Modules:
  0.0 223.0 jit_solution(14170802130749728630)
XLA Ops:
  0.6 1.5 collective-permute-start.1
  2.1 3.0 %collective-permute-start = (bf16[128,2048]{1,0:T(8,128)(2,1)}, bf16[128,2048]{1,0:T(8,128)(2,1)}, u32[]{:S(2)}, u32[]{:S(2)}) collective-permute-start(bf16[128,2048]{1,0:T(8,128)(2,1)} %bitcast.40), channel_id=1, source_target_pairs={{16,24},{24,16},{0,8},{8,0},{17,25},{25,17},{1,9},{9,1},{18,26},{2... | collective-permute-start | bytes 1572872 | tf_op jit(solution)/shard_map/ppermute | solution.py:297
  5.1 0.8 copy.14.refs_2_.refs_3_
  5.8 0.0 copy-start.14
  5.8 0.0 copy-start.12
  5.9 9.5 %load.1 = (bf16[2048,3584]{1,0:T(8,128)(2,1)S(1)}, bf16[2048,3584]{1,0:T(8,128)(2,1)S(1)}) custom-call(bf16[2048,3584]{1,0:T(8,128)(2,1)} %bitcast.37, bf16[2048,3584]{1,0:T(8,128)(2,1)} %bitcast.38), custom_call_target="tpu_custom_call" | custom-call | bytes 29360128 | tf_op jit(solution)/shard_map/load/pallas_call | solution.py:41
  15.3 0.3 fusion.16
  15.7 0.3 fusion.18
  16.0 2.1 collective-permute-done
  18.2 2.2 fusion.2.refs_0_.refs_1_
  20.4 2.0 collective-permute-start.6
  22.4 0.1 collective-permute-start.4
  22.5 0.0 collective-permute-done.1
  22.5 1.4 fusion.3.refs_1_
  23.9 11.7 %backward_rows.2 = (bf16[128,2048]{1,0:T(8,128)(2,1)S(1)}, f32[128,1]{1,0:T(8,128)S(1)}, bf16[128,3584]{1,0:T(8,128)(2,1)}, bf16[128,3584]{1,0:T(8,128)(2,1)}, bf16[128,3584]{1,0:T(8,128)(2,1)}) custom-call(s32[1]{0:T(128)} %bitcast.2.flag, bf16[128,2048]{1,0:T(8,128)(2,1)} %fusion.2.refs_0_.refs_1_, bf16[128,2048]{1,0:T(8,128)(2,1)S(1)} %fusion.3.refs_1_, ...), custom_call_target="tpu_custom_call" | custom-call | flops 9395240960 | bytes 14680064 | tf_op jit(solution)/shard_map/backward_rows/pallas_call | solution.py:155
  35.6 5.2 %copy-done = bf16[2048,3584]{1,0:T(8,128)(2,1)} copy-done((bf16[2048,3584]{1,0:T(8,128)(2,1)}, bf16[2048,3584]{1,0:T(8,128)(2,1)S(1)}, u32[]{:S(2)}) %copy-start) | copy-done | bytes 14680088
  40.8 5.2 %copy-done.3 = bf16[2048,3584]{1,0:T(8,128)(2,1)} copy-done((bf16[2048,3584]{1,0:T(8,128)(2,1)}, bf16[2048,3584]{1,0:T(8,128)(2,1)S(1)}, u32[]{:S(2)}) %copy-start.3) | copy-done | bytes 14680088
  46.0 0.7 collective-permute-start.2
  46.7 0.4 fusion.23
  47.1 0.4 fusion.14
  47.5 0.0 collective-permute-done.2
  47.5 1.5 add_convert_fusion
  49.0 0.0 copy-start.15
  49.0 1.3 collective-permute-start.8
  50.3 0.4 fusion.4
  50.7 1.3 collective-permute-start.3
  52.0 2.0 collective-permute-start.7
  54.0 0.1 collective-permute-start.5
  54.2 20.9 %collective-permute-done.8 = bf16[128,2048]{1,0:T(8,128)(2,1)S(1)} collective-permute-done((bf16[128,2048]{1,0:T(8,128)(2,1)S(1)}, bf16[128,2048]{1,0:T(8,128)(2,1)S(1)}, u32[]{:S(2)}, u32[]{:S(2)}) %collective-permute-start.8) | collective-permute-done | bytes 524320 | tf_op jit(solution)/shard_map/ppermute | solution.py:331
  75.1 0.3 fusion.20
  75.4 1.4 collective-permute-done.3
  76.8 0.4 multiply_convert_fusion
  77.2 0.8 copy-done.16
  78.1 0.2 copy-done.17
  78.3 5.2 %copy-done.1 = bf16[2048,3584]{1,0:T(8,128)(2,1)S(1)} copy-done((bf16[2048,3584]{1,0:T(8,128)(2,1)S(1)}, bf16[2048,3584]{1,0:T(8,128)(2,1)}, u32[]{:S(2)}) %copy-start.1) | copy-done | bytes 14680088
  83.4 5.2 %copy-done.4 = bf16[2048,3584]{1,0:T(8,128)(2,1)S(1)} copy-done((bf16[2048,3584]{1,0:T(8,128)(2,1)S(1)}, bf16[2048,3584]{1,0:T(8,128)(2,1)}, u32[]{:S(2)}) %copy-start.4) | copy-done | bytes 14680088
  88.6 25.7 %backward_rows.3 = (bf16[128,2048]{1,0:T(8,128)(2,1)S(1)}, f32[128,1]{1,0:T(8,128)S(1)}, bf16[256,3584]{1,0:T(8,128)(2,1)}, bf16[256,3584]{1,0:T(8,128)(2,1)}, bf16[256,3584]{1,0:T(8,128)(2,1)}) custom-call(s32[1]{0:T(128)} %bitcast.8.flag, bf16[128,2048]{1,0:T(8,128)(2,1)} %copy-done.17, bf16[128,2048]{1,0:T(8,128)(2,1)} %copy-done.16, ...), custom_call_target="tpu_custom_call" | custom-call | flops 13153337344 | bytes 14680064 | tf_op jit(solution)/shard_map/backward_rows/pallas_call | solution.py:155
  114.3 0.1 select_reduce_fusion
  114.4 1.7 collective-permute-start.22
  116.1 1.5 collective-permute-start.17
  117.6 0.5 collective-permute-start.14
  118.2 2.3 %collective-permute-start.9 = (bf16[128,2048]{1,0:T(8,128)(2,1)S(1)}, bf16[128,2048]{1,0:T(8,128)(2,1)S(1)}, u32[]{:S(2)}, u32[]{:S(2)}) collective-permute-start(bf16[128,2048]{1,0:T(8,128)(2,1)S(1)} %get-tuple-element.35), channel_id=1, source_target_pairs={{0,8},{8,0},{1,9},{9,1},{2,10},{10,2},{3,11},{11,3},{4,12},{12,4},... | collective-permute-start | bytes 1572872 | tf_op jit(solution)/shard_map/ppermute | solution.py:297
  120.4 1.7 collective-permute-start.11
  122.2 0.3 collective-permute-start.10
  122.5 5.2 %copy-done.2 = bf16[2048,3584]{1,0:T(8,128)(2,1)S(1)} copy-done((bf16[2048,3584]{1,0:T(8,128)(2,1)S(1)}, bf16[2048,3584]{1,0:T(8,128)(2,1)}, u32[]{:S(2)}) %copy-start.2) | copy-done | bytes 14680088
  127.7 5.2 %copy-done.5 = bf16[2048,3584]{1,0:T(8,128)(2,1)S(1)} copy-done((bf16[2048,3584]{1,0:T(8,128)(2,1)S(1)}, bf16[2048,3584]{1,0:T(8,128)(2,1)}, u32[]{:S(2)}) %copy-start.5) | copy-done | bytes 14680088
  132.9 11.3 %forward_rows.3 = (bf16[256,3584]{1,0:T(8,128)(2,1)}, bf16[256,3584]{1,0:T(8,128)(2,1)}, bf16[256,3584]{1,0:T(8,128)(2,1)}) custom-call(bf16[128,2048]{1,0:T(8,128)(2,1)} %collective-permute-done.4.refs_0_.refs_2_, bf16[128,2048]{1,0:T(8,128)(2,1)} %collective-permute-done.6.refs_1_.refs_3_, bf16[2048,3584]{1,0:T(8,128)(2,1)S(1)} %copy-done.2, ...), custom_call_target="tpu_custom_call" | custom-call | flops 7516192768 | bytes 5505024 | tf_op jit(solution)/shard_map/forward_rows/pallas_call | solution.py:96
  144.1 0.5 add_bitcast_fusion
  144.7 1.7 collective-permute-start.13
  146.4 0.4 collective-permute-start.12
  146.8 1.7 collective-permute-start.18
  148.5 0.3 collective-permute-start.15
  148.9 0.4 fusion.9
  149.3 1.3 fusion.8
  150.5 2.5 %collective-permute-done.12 = bf16[64,2048]{1,0:T(8,128)(2,1)S(1)} collective-permute-done((bf16[64,2048]{1,0:T(8,128)(2,1)S(1)}, bf16[64,2048]{1,0:T(8,128)(2,1)S(1)}, u32[]{:S(2)}, u32[]{:S(2)}) %collective-permute-start.12) | collective-permute-done | bytes 262176 | tf_op jit(solution)/shard_map/ppermute | solution.py:278
  153.1 9.3 %collective-permute-done.18.refs_10_.refs_15_ = bf16[128,2048]{1,0:T(8,128)(2,1)S(1)} collective-permute-done((bf16[128,2048]{1,0:T(8,128)(2,1)S(1)}, bf16[128,2048]{1,0:T(8,128)(2,1)S(1)}, u32[]{:S(2)}, u32[]{:S(2)}) %collective-permute-start.18) | collective-permute-done | bytes 524320 | tf_op jit(solution)/shard_map/ppermute | solution.py:274
  162.4 1.7 collective-permute-start.19
  164.1 0.3 collective-permute-start.16
  164.5 15.7 %forward_rows.2 = (bf16[384,3584]{1,0:T(8,128)(2,1)}, bf16[384,3584]{1,0:T(8,128)(2,1)}, bf16[384,3584]{1,0:T(8,128)(2,1)}) custom-call(bf16[128,2048]{1,0:T(8,128)(2,1)} %copy-done.10, bf16[128,2048]{1,0:T(8,128)(2,1)} %copy-done.9, bf16[128,2048]{1,0:T(8,128)(2,1)} %copy-done.11, bf16[2048,3584]{1,0:T(8,128)(2,1)S(1)} %copy-done.2, ...), custom_call_target="tpu_custom_call" | custom-call | flops 11274289152 | bytes 8257536 | tf_op jit(solution)/shard_map/forward_rows/pallas_call | solution.py:96
  180.3 1.7 collective-permute-start.21
  182.0 0.4 collective-permute-start.20
  182.4 20.8 %weight_grads.2 = (f32[256,3584]{1,0:T(8,128)}, f32[256,3584]{1,0:T(8,128)}, f32[256,3584]{1,0:T(8,128)}) custom-call(s32[1]{0:T(128)} %bitcast.10.refs_0_, bf16[128,2048]{1,0:T(8,128)(2,1)} %fusion.2.refs_0_.refs_1_, bf16[128,2048]{1,0:T(8,128)(2,1)} %collective-permute-done.4.refs_0_.refs_2_, bf16[128,2048]{1,0:T(8,128)(2,1)} %collective-permute-done.6.refs_1_.refs_3_, ...), custom_call_target="tpu_custom_call" | custom-call | flops 12918456320 | bytes 33947648 | tf_op jit(solution)/shard_map/weight_grads/pallas_call | solution.py:230
  203.3 0.9 pad_maximum_fusion.refs_6_.refs_9_
  204.1 18.7 %weight_grads.3 = (bf16[256,3584]{1,0:T(8,128)(2,1)}, bf16[256,3584]{1,0:T(8,128)(2,1)}, bf16[256,3584]{1,0:T(8,128)(2,1)}) custom-call(s32[1]{0:T(128)} %bitcast.10.refs_0_, bf16[128,2048]{1,0:T(8,128)(2,1)} %copy-done.10, bf16[128,2048]{1,0:T(8,128)(2,1)} %copy-done.9, bf16[128,2048]{1,0:T(8,128)(2,1)} %copy-done.11, bf16[128,2048]{1,0:T(8,128)(2,1)} %copy-done.7, ...), custom_call_target="tpu_custom_call" | custom-call | flops 7751073792 | bytes 28442624 | tf_op jit(solution)/shard_map/weight_grads/pallas_call | solution.py:230
  (57 shorter events, 0.2 us)
Async XLA Ops:
  0.6 21.8 %collective-permute-start.1 = (bf16[128,2048]{1,0:T(8,128)(2,1)}, bf16[128,2048]{1,0:T(8,128)(2,1)}, u32[]{:S(2)}, u32[]{:S(2)}) collective-permute-start(bf16[128,2048]{1,0:T(8,128)(2,1)} %bitcast.39), channel_id=1, source_target_pairs={{16,24},{24,16},{17,25},{25,17},{18,26},{26,18},{19,27},{27,19},{2... | collective-permute-start | bytes 1572872 | tf_op jit(solution)/shard_map/ppermute | solution.py:297
  2.1 16.1 %collective-permute-start = (bf16[128,2048]{1,0:T(8,128)(2,1)}, bf16[128,2048]{1,0:T(8,128)(2,1)}, u32[]{:S(2)}, u32[]{:S(2)}) collective-permute-start(bf16[128,2048]{1,0:T(8,128)(2,1)} %bitcast.40), channel_id=1, source_target_pairs={{16,24},{24,16},{0,8},{8,0},{17,25},{25,17},{1,9},{9,1},{18,26},{2... | collective-permute-start | bytes 1572872 | tf_op jit(solution)/shard_map/ppermute | solution.py:297
  5.8 9.5 %copy-start.8 = (bf16[1,128,2048]{2,1,0:T(8,128)(2,1)S(1)}, bf16[1,128,2048]{2,1,0:T(8,128)(2,1)}, u32[]{:S(2)}) copy-start(bf16[1,128,2048]{2,1,0:T(8,128)(2,1)} %param.8) | copy-start | bytes 1572868
  5.8 9.5 %copy-start.14 = (s32[1,1,128]{2,1,0:T(1,128)S(1)}, s32[1,1,128]{2,1,0:T(1,128)}, u32[]{:S(2)}) copy-start(s32[1,1,128]{2,1,0:T(1,128)} %param.12) | copy-start | bytes 1540
  5.8 9.8 %copy-start.12 = (bf16[1,1,128,2048]{3,2,1,0:T(8,128)(2,1)S(1)}, bf16[1,1,128,2048]{3,2,1,0:T(8,128)(2,1)}, u32[]{:S(2)}) copy-start(bf16[1,1,128,2048]{3,2,1,0:T(8,128)(2,1)} %param.7) | copy-start | bytes 1572868
  20.4 31.6 %collective-permute-start.6 = (bf16[128,2048]{1,0:T(8,128)(2,1)}, bf16[128,2048]{1,0:T(8,128)(2,1)}, u32[]{:S(2)}, u32[]{:S(2)}) collective-permute-start(bf16[128,2048]{1,0:T(8,128)(2,1)} %fusion.2.refs_0_.refs_1_), channel_id=1, source_target_pairs={{0,1},{2,0},{4,2},{6,4},{7,6},{5,7},{3,5},{1,3},{16,17},{18,16},{2... | collective-permute-start | bytes 1572872 | tf_op jit(solution)/shard_map/ppermute | solution.py:274
  22.4 31.6 %collective-permute-start.4 = (bf16[128,2048]{1,0:T(8,128)(2,1)}, bf16[128,2048]{1,0:T(8,128)(2,1)}, u32[]{:S(2)}, u32[]{:S(2)}) collective-permute-start(bf16[128,2048]{1,0:T(8,128)(2,1)} %fusion.2.refs_0_.refs_1_), channel_id=1, source_target_pairs={{0,2},{2,4},{4,6},{6,7},{7,5},{5,3},{3,1},{1,0},{16,18},{18,20},{2... | collective-permute-start | bytes 1572872 | tf_op jit(solution)/shard_map/ppermute | solution.py:273
  35.6 5.2 %copy-start = (bf16[2048,3584]{1,0:T(8,128)(2,1)}, bf16[2048,3584]{1,0:T(8,128)(2,1)S(1)}, u32[]{:S(2)}) copy-start(bf16[2048,3584]{1,0:T(8,128)(2,1)S(1)} %get-tuple-element.29.refs_3_.refs_4_.refs_2_) | copy-start | bytes 44040196
  40.8 5.2 %copy-start.3 = (bf16[2048,3584]{1,0:T(8,128)(2,1)}, bf16[2048,3584]{1,0:T(8,128)(2,1)S(1)}, u32[]{:S(2)}) copy-start(bf16[2048,3584]{1,0:T(8,128)(2,1)S(1)} %get-tuple-element.30.refs_4_.refs_5_.refs_3_) | copy-start | bytes 44040196
  46.0 1.5 collective-permute-start.2
  49.0 27.8 %copy-start.15 = (f32[1,1,128]{2,1,0:T(1,128)S(1)}, f32[1,1,128]{2,1,0:T(1,128)}, u32[]{:S(2)}) copy-start(f32[1,1,128]{2,1,0:T(1,128)} %param.13) | copy-start | bytes 1540
  49.0 26.1 %collective-permute-start.8 = (bf16[128,2048]{1,0:T(8,128)(2,1)S(1)}, bf16[128,2048]{1,0:T(8,128)(2,1)S(1)}, u32[]{:S(2)}, u32[]{:S(2)}) collective-permute-start(bf16[128,2048]{1,0:T(8,128)(2,1)S(1)} %add_convert_fusion), channel_id=1, source_target_pairs={{16,0},{17,1},{18,2},{19,3},{20,4},{21,5},{22,6},{23,7},{24,8},{25... | collective-permute-start | bytes 1572872 | tf_op jit(solution)/shard_map/ppermute | solution.py:331
  50.7 26.1 %collective-permute-start.3 = (bf16[128,2048]{1,0:T(8,128)(2,1)S(1)}, bf16[128,2048]{1,0:T(8,128)(2,1)S(1)}, u32[]{:S(2)}, u32[]{:S(2)}) collective-permute-start(bf16[128,2048]{1,0:T(8,128)(2,1)S(1)} %fusion.4), channel_id=1, source_target_pairs={{16,0},{17,1},{18,2},{19,3},{20,4},{21,5},{22,6},{23,7},{24,8},{25... | collective-permute-start | bytes 1572872 | tf_op jit(solution)/shard_map/ppermute | solution.py:330
  52.0 25.2 %collective-permute-start.7 = (bf16[128,2048]{1,0:T(8,128)(2,1)}, bf16[128,2048]{1,0:T(8,128)(2,1)S(1)}, u32[]{:S(2)}, u32[]{:S(2)}) collective-permute-start(bf16[128,2048]{1,0:T(8,128)(2,1)} %collective-permute-done.6.refs_1_.refs_3_), channel_id=1, source_target_pairs={{0,1},{2,0},{4,2},{6,4},{7,6},{5,7},{3,5},{1,3},{16,17},{18,16},{2... | collective-permute-start | bytes 1572872 | tf_op jit(solution)/shard_map/ppermute | solution.py:274
  54.0 23.2 %collective-permute-start.5 = (bf16[128,2048]{1,0:T(8,128)(2,1)}, bf16[128,2048]{1,0:T(8,128)(2,1)S(1)}, u32[]{:S(2)}, u32[]{:S(2)}) collective-permute-start(bf16[128,2048]{1,0:T(8,128)(2,1)} %collective-permute-done.4.refs_0_.refs_2_), channel_id=1, source_target_pairs={{0,2},{2,4},{4,6},{6,7},{7,5},{5,3},{3,1},{1,0},{16,18},{18,20},{2... | collective-permute-start | bytes 1572872 | tf_op jit(solution)/shard_map/ppermute | solution.py:273
  77.2 40.4 %copy-start.13 = (bf16[128,2048]{1,0:T(8,128)(2,1)}, bf16[128,2048]{1,0:T(8,128)(2,1)S(1)}, u32[]{:S(2)}) copy-start(bf16[128,2048]{1,0:T(8,128)(2,1)S(1)} %get-tuple-element.53.refs_6_.refs_11_) | copy-start | bytes 1572868
  77.2 0.9 copy-start.16
  77.2 1.0 copy-start.17
  78.3 5.2 %copy-start.1 = (bf16[2048,3584]{1,0:T(8,128)(2,1)S(1)}, bf16[2048,3584]{1,0:T(8,128)(2,1)}, u32[]{:S(2)}) copy-start(bf16[2048,3584]{1,0:T(8,128)(2,1)} %copy-done) | copy-start | bytes 44040196
  83.4 5.2 %copy-start.4 = (bf16[2048,3584]{1,0:T(8,128)(2,1)S(1)}, bf16[2048,3584]{1,0:T(8,128)(2,1)}, u32[]{:S(2)}) copy-start(bf16[2048,3584]{1,0:T(8,128)(2,1)} %copy-done.3) | copy-start | bytes 44040196
  114.4 7.8 %collective-permute-start.22 = (f32[128]{0:T(128)S(1)}, f32[128]{0:T(128)S(1)}, u32[]{:S(2)}, u32[]{:S(2)}) collective-permute-start(f32[128]{0:T(128)S(1)} %select_reduce_fusion), channel_id=1, source_target_pairs={{0,8},{8,0},{1,9},{9,1},{2,10},{10,2},{3,11},{11,3},{4,12},{12,4},... | collective-permute-start | bytes 1544 | tf_op jit(solution)/shard_map/ppermute | solution.py:344
  116.1 30.7 %collective-permute-start.17 = (bf16[128,2048]{1,0:T(8,128)(2,1)S(1)}, bf16[128,2048]{1,0:T(8,128)(2,1)S(1)}, u32[]{:S(2)}, u32[]{:S(2)}) collective-permute-start(bf16[128,2048]{1,0:T(8,128)(2,1)S(1)} %get-tuple-element.53.refs_6_.refs_11_), channel_id=1, source_target_pairs={{0,1},{2,0},{4,2},{6,4},{7,6},{5,7},{3,5},{1,3},{16,17},{18,16},{2... | collective-permute-start | bytes 1572872 | tf_op jit(solution)/shard_map/ppermute | solution.py:274
  117.6 30.9 %collective-permute-start.14 = (bf16[128,2048]{1,0:T(8,128)(2,1)S(1)}, bf16[128,2048]{1,0:T(8,128)(2,1)S(1)}, u32[]{:S(2)}, u32[]{:S(2)}) collective-permute-start(bf16[128,2048]{1,0:T(8,128)(2,1)S(1)} %get-tuple-element.53.refs_6_.refs_11_), channel_id=1, source_target_pairs={{0,2},{2,4},{4,6},{6,7},{7,5},{5,3},{3,1},{1,0},{16,18},{18,20},{2... | collective-permute-start | bytes 1572872 | tf_op jit(solution)/shard_map/ppermute | solution.py:273
  118.2 30.7 %collective-permute-start.9 = (bf16[128,2048]{1,0:T(8,128)(2,1)S(1)}, bf16[128,2048]{1,0:T(8,128)(2,1)S(1)}, u32[]{:S(2)}, u32[]{:S(2)}) collective-permute-start(bf16[128,2048]{1,0:T(8,128)(2,1)S(1)} %get-tuple-element.35), channel_id=1, source_target_pairs={{0,8},{8,0},{1,9},{9,1},{2,10},{10,2},{3,11},{11,3},{4,12},{12,4},... | collective-permute-start | bytes 1572872 | tf_op jit(solution)/shard_map/ppermute | solution.py:297
  120.4 24.2 %collective-permute-start.11 = (bf16[128,2048]{1,0:T(8,128)(2,1)}, bf16[128,2048]{1,0:T(8,128)(2,1)S(1)}, u32[]{:S(2)}, u32[]{:S(2)}) collective-permute-start(bf16[128,2048]{1,0:T(8,128)(2,1)} %copy-done.16), channel_id=1, source_target_pairs={{0,1},{2,0},{4,2},{6,4},{7,6},{5,7},{3,5},{1,3},{16,17},{18,16},{2... | collective-permute-start | bytes 1572872 | tf_op jit(solution)/shard_map/ppermute | solution.py:274
  122.2 24.2 %collective-permute-start.10 = (bf16[128,2048]{1,0:T(8,128)(2,1)}, bf16[128,2048]{1,0:T(8,128)(2,1)S(1)}, u32[]{:S(2)}, u32[]{:S(2)}) collective-permute-start(bf16[128,2048]{1,0:T(8,128)(2,1)} %copy-done.17), channel_id=1, source_target_pairs={{0,2},{2,4},{4,6},{6,7},{7,5},{5,3},{3,1},{1,0},{16,18},{18,20},{2... | collective-permute-start | bytes 1572872 | tf_op jit(solution)/shard_map/ppermute | solution.py:273
  122.5 5.2 %copy-start.2 = (bf16[2048,3584]{1,0:T(8,128)(2,1)S(1)}, bf16[2048,3584]{1,0:T(8,128)(2,1)}, u32[]{:S(2)}) copy-start(bf16[2048,3584]{1,0:T(8,128)(2,1)} %copy-done) | copy-start | bytes 44040196
  127.7 5.2 %copy-start.5 = (bf16[2048,3584]{1,0:T(8,128)(2,1)S(1)}, bf16[2048,3584]{1,0:T(8,128)(2,1)}, u32[]{:S(2)}) copy-start(bf16[2048,3584]{1,0:T(8,128)(2,1)} %copy-done.3) | copy-start | bytes 44040196
  144.6 5.9 %copy-start.9 = (bf16[128,2048]{1,0:T(8,128)(2,1)}, bf16[128,2048]{1,0:T(8,128)(2,1)S(1)}, u32[]{:S(2)}) copy-start(bf16[128,2048]{1,0:T(8,128)(2,1)S(1)} %collective-permute-done.11.refs_1_.refs_2_) | copy-start | bytes 1572868
  144.7 8.4 %collective-permute-start.13 = (bf16[64,2048]{1,0:T(8,128)(2,1)S(1)}, bf16[64,2048]{1,0:T(8,128)(2,1)S(1)}, u32[]{:S(2)}, u32[]{:S(2)}) collective-permute-start(bf16[64,2048]{1,0:T(8,128)(2,1)S(1)} %slice.17), channel_id=1, source_target_pairs={{0,1},{2,0},{4,2},{6,4},{7,6},{5,7},{3,5},{1,3},{16,17},{18,16},{2... | collective-permute-start | bytes 786440 | tf_op jit(solution)/shard_map/ppermute | solution.py:279
  146.4 6.6 %copy-start.10 = (bf16[128,2048]{1,0:T(8,128)(2,1)}, bf16[128,2048]{1,0:T(8,128)(2,1)S(1)}, u32[]{:S(2)}) copy-start(bf16[128,2048]{1,0:T(8,128)(2,1)S(1)} %collective-permute-done.10.refs_0_.refs_1_) | copy-start | bytes 1572868
  146.4 6.6 %collective-permute-start.12 = (bf16[64,2048]{1,0:T(8,128)(2,1)S(1)}, bf16[64,2048]{1,0:T(8,128)(2,1)S(1)}, u32[]{:S(2)}, u32[]{:S(2)}) collective-permute-start(bf16[64,2048]{1,0:T(8,128)(2,1)S(1)} %slice.16), channel_id=1, source_target_pairs={{0,2},{2,4},{4,6},{6,7},{7,5},{5,3},{3,1},{1,0},{16,18},{18,20},{2... | collective-permute-start | bytes 786440 | tf_op jit(solution)/shard_map/ppermute | solution.py:278
  146.8 6.3 %copy-start.18 = (bf16[128,2048]{1,0:T(8,128)(2,1)}, bf16[128,2048]{1,0:T(8,128)(2,1)S(1)}, u32[]{:S(2)}) copy-start(bf16[128,2048]{1,0:T(8,128)(2,1)S(1)} %collective-permute-done.17.refs_8_.refs_13_) | copy-start | bytes 1572868
  146.8 15.6 %collective-permute-start.18 = (bf16[128,2048]{1,0:T(8,128)(2,1)S(1)}, bf16[128,2048]{1,0:T(8,128)(2,1)S(1)}, u32[]{:S(2)}, u32[]{:S(2)}) collective-permute-start(bf16[128,2048]{1,0:T(8,128)(2,1)S(1)} %collective-permute-done.17.refs_8_.refs_13_), channel_id=1, source_target_pairs={{0,1},{2,0},{4,2},{6,4},{7,6},{5,7},{3,5},{1,3},{16,17},{18,16},{2... | collective-permute-start | bytes 1572872 | tf_op jit(solution)/shard_map/ppermute | solution.py:274
  148.5 4.6 %copy-start.19 = (bf16[128,2048]{1,0:T(8,128)(2,1)}, bf16[128,2048]{1,0:T(8,128)(2,1)S(1)}, u32[]{:S(2)}) copy-start(bf16[128,2048]{1,0:T(8,128)(2,1)S(1)} %collective-permute-done.14.refs_7_.refs_12_) | copy-start | bytes 1572868
  148.5 15.6 %collective-permute-start.15 = (bf16[128,2048]{1,0:T(8,128)(2,1)S(1)}, bf16[128,2048]{1,0:T(8,128)(2,1)S(1)}, u32[]{:S(2)}, u32[]{:S(2)}) collective-permute-start(bf16[128,2048]{1,0:T(8,128)(2,1)S(1)} %collective-permute-done.14.refs_7_.refs_12_), channel_id=1, source_target_pairs={{0,2},{2,4},{4,6},{6,7},{7,5},{5,3},{3,1},{1,0},{16,18},{18,20},{2... | collective-permute-start | bytes 1572872 | tf_op jit(solution)/shard_map/ppermute | solution.py:273
  153.1 11.3 %copy-start.11 = (bf16[128,2048]{1,0:T(8,128)(2,1)}, bf16[128,2048]{1,0:T(8,128)(2,1)S(1)}, u32[]{:S(2)}) copy-start(bf16[128,2048]{1,0:T(8,128)(2,1)S(1)} %constant_dynamic-update-slice_fusion.refs_2_.refs_3_) | copy-start | bytes 1572868
  162.4 17.8 %copy-start.20 = (bf16[128,2048]{1,0:T(8,128)(2,1)}, bf16[128,2048]{1,0:T(8,128)(2,1)S(1)}, u32[]{:S(2)}) copy-start(bf16[128,2048]{1,0:T(8,128)(2,1)S(1)} %collective-permute-done.18.refs_10_.refs_15_) | copy-start | bytes 1572868
  162.4 17.8 %collective-permute-start.19 = (bf16[128,2048]{1,0:T(8,128)(2,1)S(1)}, bf16[128,2048]{1,0:T(8,128)(2,1)S(1)}, u32[]{:S(2)}, u32[]{:S(2)}) collective-permute-start(bf16[128,2048]{1,0:T(8,128)(2,1)S(1)} %collective-permute-done.18.refs_10_.refs_15_), channel_id=1, source_target_pairs={{0,1},{2,0},{4,2},{6,4},{7,6},{5,7},{3,5},{1,3},{16,17},{18,16},{2... | collective-permute-start | bytes 1572872 | tf_op jit(solution)/shard_map/ppermute | solution.py:274
  164.1 16.1 %copy-start.21 = (bf16[128,2048]{1,0:T(8,128)(2,1)}, bf16[128,2048]{1,0:T(8,128)(2,1)S(1)}, u32[]{:S(2)}) copy-start(bf16[128,2048]{1,0:T(8,128)(2,1)S(1)} %collective-permute-done.15.refs_9_.refs_14_) | copy-start | bytes 1572868
  164.1 17.9 %collective-permute-start.16 = (bf16[128,2048]{1,0:T(8,128)(2,1)S(1)}, bf16[128,2048]{1,0:T(8,128)(2,1)S(1)}, u32[]{:S(2)}, u32[]{:S(2)}) collective-permute-start(bf16[128,2048]{1,0:T(8,128)(2,1)S(1)} %collective-permute-done.15.refs_9_.refs_14_), channel_id=1, source_target_pairs={{0,2},{2,4},{4,6},{6,7},{7,5},{5,3},{3,1},{1,0},{16,18},{18,20},{2... | collective-permute-start | bytes 1572872 | tf_op jit(solution)/shard_map/ppermute | solution.py:273
  180.2 23.0 %copy-start.6 = (bf16[128,2048]{1,0:T(8,128)(2,1)}, bf16[128,2048]{1,0:T(8,128)(2,1)S(1)}, u32[]{:S(2)}) copy-start(bf16[128,2048]{1,0:T(8,128)(2,1)S(1)} %collective-permute-done.19.refs_5_.refs_8_) | copy-start | bytes 1572868
  180.3 23.0 %collective-permute-start.21 = (bf16[64,2048]{1,0:T(8,128)(2,1)S(1)}, bf16[64,2048]{1,0:T(8,128)(2,1)S(1)}, u32[]{:S(2)}, u32[]{:S(2)}) collective-permute-start(bf16[64,2048]{1,0:T(8,128)(2,1)S(1)} %slice.19), channel_id=1, source_target_pairs={{0,1},{2,0},{4,2},{6,4},{7,6},{5,7},{3,5},{1,3},{16,17},{18,16},{2... | collective-permute-start | bytes 786440 | tf_op jit(solution)/shard_map/ppermute | solution.py:279
  182.0 21.3 %copy-start.7 = (bf16[128,2048]{1,0:T(8,128)(2,1)}, bf16[128,2048]{1,0:T(8,128)(2,1)S(1)}, u32[]{:S(2)}) copy-start(bf16[128,2048]{1,0:T(8,128)(2,1)S(1)} %collective-permute-done.16.refs_4_.refs_7_) | copy-start | bytes 1572868
  182.0 21.3 %collective-permute-start.20 = (bf16[64,2048]{1,0:T(8,128)(2,1)S(1)}, bf16[64,2048]{1,0:T(8,128)(2,1)S(1)}, u32[]{:S(2)}, u32[]{:S(2)}) collective-permute-start(bf16[64,2048]{1,0:T(8,128)(2,1)S(1)} %slice.18), channel_id=1, source_target_pairs={{0,2},{2,4},{4,6},{6,7},{7,5},{5,3},{3,1},{1,0},{16,18},{18,20},{2... | collective-permute-start | bytes 786440 | tf_op jit(solution)/shard_map/ppermute | solution.py:278

commit v3 on v2

--- a/solution.py
+++ b/solution.py
@@ -195,6 +195,7 @@
             x_turned[...] = stacked(x_cuts).T
             s_turned[...] = stacked(s_cuts).T
 
+        here_all = slab(tile)
         back = jnp.dot(stacked(s_refs), two[...], preferred_element_type=F32)
         start = 0
         for index, group_rows in enumerate(sizes):
@@ -211,8 +212,11 @@
         ):
             value = jnp.dot(left[...], right[...], preferred_element_type=F32)
             if sums:
-                value = sums[index][...] + value
-            out[...] = value if scale is None else (value * scale).astype(BF16)
+                value = sums[index][:, here_all] + value
+            if scale is None:
+                out[:, here_all] = value
+            else:
+                out[...] = (value * scale).astype(BF16)
 
     def by_tile(height):
         return pl.BlockSpec((height, tile), lambda i, at: (0, i))
@@ -236,19 +240,19 @@
             + [kept_whole((size, width))] * count
             + [by_tile(width)]
             + [by_tile(group_rows) for group_rows in sizes for _ in range(3)]
-            + [by_tile(cut)] * len(before),
-            out_specs=[by_tile(cut)] * 3,
+            + [RESIDENT] * len(before),
+            out_specs=[RESIDENT if scale is None else by_tile(cut)] * 3,
             scratch_shapes=[pltpu.VMEM((cut, rows), BF16)] * 2 + [pltpu.VMEM((rows, tile), BF16)] * 3,
         ),
-        out_shape=[pltpu.HBM((cut, hidden), F32 if scale is None else BF16)] * 3,
-        compiler_params=params(40),
+        out_shape=[pltpu.VMEM((cut, hidden), F32) if scale is None else pltpu.HBM((cut, hidden), BF16)] * 3,
+        compiler_params=params(24),
         cost_estimate=pl.CostEstimate(
             flops=2 * rows * width * hidden + 6 * rows * cut * hidden,
             bytes_accessed=2 * width * hidden + 6 * rows * hidden + 6 * cut * hidden,
             transcendentals=0,
         ),
         name="weight_grads",
-    )(place.reshape(1).astype(jnp.int32), *in_hbm([*x_cuts, *s_cuts, *s_blocks, w_two, *[a for group in groups for a in group], *before]))
+    )(place.reshape(1).astype(jnp.int32), *in_hbm([*x_cuts, *s_cuts, *s_blocks, w_two]), *in_hbm([a for group in groups for a in group]), *before)
 
 
 def ring_of(count):

time: 224 us -> 220 us (0.982)
  Pallas kernels: 113 us -> 110 us
    pallas_call x2, Pallas kernels: 39.5 us -> 35.9 us  [weight_grads(): pl.pallas_call(kernel, grid_spec=pltpu.PrefetchScalarGridSpec(num_scalar_...]
where the time goes in v3:
time: 220 us; the launch traced here: 219 us
  Pallas kernels  110 us (50%)
  waiting for transfers between devices  36.2 us (16%)
  local copies, waits for them, and re-layouts  33 us (15%)
  starting transfers between devices  28.4 us (13%)
  matrix products  9.37 us (4%)
    pallas_call x2, Pallas kernels, backward_rows(): pl.pallas_call(kernel, grid=(hidden // tile,), in_specs=[pl.BlockSpec(mem...  37.4 us
    pallas_call x2, Pallas kernels, weight_grads(): pl.pallas_call(kernel, grid_spec=pltpu.PrefetchScalarGridSpec(num_scalar_...  35.9 us
    unnamed x45, local copies, waits for them, and re-layouts  32.2 us
    pallas_call x2, Pallas kernels, forward_rows(): pl.pallas_call(kernel, grid=(hidden // tile,), in_specs=[held(b) for b in...  27 us
    ppermute x1, waiting for transfers between devices, per_device(): dy_first_theirs = lax.ppermute(ig_theirs, 'section', [(1, 0)])  20.9 us
    ppermute x6, starting transfers between devices, around(): behind = lax.ppermute(behind, axes, shift(-1))  10.7 us
    pallas_call x1, Pallas kernels, load(): pl.pallas_call(kernel, in_specs=[pl.BlockSpec(memory_space=pltpu.HBM)] *...  9.45 us
    ppermute x6, waiting for transfers between devices, around(): behind = lax.ppermute(behind, axes, shift(-1))  9.31 us
  transfers between devices with their start and end apart: 23, of which 5 were waited for; matrix products, arithmetic and copies ran while one was open for 5% of the time, Pallas kernels for 31%

profile of v3, /device:TPU:0, one launch (start us, length us, event | category | flops | bytes accessed | tf_op | source)
XLA Modules:
  0.0 219.3 jit_solution(16798541881614713993)
XLA Ops:
  0.6 1.5 collective-permute-start.1
  2.1 3.0 %collective-permute-start = (bf16[128,2048]{1,0:T(8,128)(2,1)}, bf16[128,2048]{1,0:T(8,128)(2,1)}, u32[]{:S(2)}, u32[]{:S(2)}) collective-permute-start(bf16[128,2048]{1,0:T(8,128)(2,1)} %bitcast.40), channel_id=1, source_target_pairs={{16,24},{24,16},{0,8},{8,0},{17,25},{25,17},{1,9},{9,1},{18,26},{2... | collective-permute-start | bytes 1572872 | tf_op jit(solution)/shard_map/ppermute | solution.py:301
  5.1 0.8 copy.14.refs_2_.refs_3_
  5.8 0.0 copy-start.14
  5.8 0.0 copy-start.12
  5.9 9.5 %load.1 = (bf16[2048,3584]{1,0:T(8,128)(2,1)S(1)}, bf16[2048,3584]{1,0:T(8,128)(2,1)S(1)}) custom-call(bf16[2048,3584]{1,0:T(8,128)(2,1)} %bitcast.37, bf16[2048,3584]{1,0:T(8,128)(2,1)} %bitcast.38), custom_call_target="tpu_custom_call" | custom-call | bytes 29360128 | tf_op jit(solution)/shard_map/load/pallas_call | solution.py:41
  15.3 0.3 fusion.16
  15.7 0.3 fusion.18
  16.0 2.1 collective-permute-done
  18.2 2.2 %fusion.2.refs_0_.refs_1_ = bf16[128,2048]{1,0:T(8,128)(2,1)} fusion(f32[128,2048]{1,0:T(8,128)S(1)} %fusion.18, bf16[128,2048]{1,0:T(8,128)(2,1)} %collective-permute-done, s32[128]{0:T(128)S(1)} %iota_add_fusion, s32[128]{0:T(128)S(1)} %bitcast.43), kind=kOutput, calls=%fused_computation.8 | convolution fusion | flops 67649536 | bytes 2098176 | tf_op jit(solution)/shard_map/dot_general | solution.py:311
  20.4 2.0 collective-permute-start.6
  22.4 0.1 collective-permute-start.4
  22.5 0.0 collective-permute-done.1
  22.5 1.4 fusion.3.refs_1_
  23.9 11.7 %backward_rows.2 = (bf16[128,2048]{1,0:T(8,128)(2,1)S(1)}, f32[128,1]{1,0:T(8,128)S(1)}, bf16[128,3584]{1,0:T(8,128)(2,1)}, bf16[128,3584]{1,0:T(8,128)(2,1)}, bf16[128,3584]{1,0:T(8,128)(2,1)}) custom-call(s32[1]{0:T(128)} %bitcast.2.flag, bf16[128,2048]{1,0:T(8,128)(2,1)} %fusion.2.refs_0_.refs_1_, bf16[128,2048]{1,0:T(8,128)(2,1)S(1)} %fusion.3.refs_1_, ...), custom_call_target="tpu_custom_call" | custom-call | flops 9395240960 | bytes 14680064 | tf_op jit(solution)/shard_map/backward_rows/pallas_call | solution.py:155
  35.6 5.2 %copy-done = bf16[2048,3584]{1,0:T(8,128)(2,1)} copy-done((bf16[2048,3584]{1,0:T(8,128)(2,1)}, bf16[2048,3584]{1,0:T(8,128)(2,1)S(1)}, u32[]{:S(2)}) %copy-start) | copy-done | bytes 14680088
  40.8 5.2 %copy-done.3 = bf16[2048,3584]{1,0:T(8,128)(2,1)} copy-done((bf16[2048,3584]{1,0:T(8,128)(2,1)}, bf16[2048,3584]{1,0:T(8,128)(2,1)S(1)}, u32[]{:S(2)}) %copy-start.3) | copy-done | bytes 14680088
  46.0 0.7 collective-permute-start.2
  46.7 0.4 fusion.23
  47.1 0.4 fusion.14
  47.5 0.0 collective-permute-done.2
  47.5 1.5 add_convert_fusion
  49.0 0.0 copy-start.15
  49.0 1.3 collective-permute-start.8
  50.3 0.4 fusion.4
  50.7 1.3 collective-permute-start.3
  52.0 2.0 collective-permute-start.7
  54.0 0.1 collective-permute-start.5
  54.2 20.9 %collective-permute-done.8 = bf16[128,2048]{1,0:T(8,128)(2,1)S(1)} collective-permute-done((bf16[128,2048]{1,0:T(8,128)(2,1)S(1)}, bf16[128,2048]{1,0:T(8,128)(2,1)S(1)}, u32[]{:S(2)}, u32[]{:S(2)}) %collective-permute-start.8) | collective-permute-done | bytes 524320 | tf_op jit(solution)/shard_map/ppermute | solution.py:335
  75.1 0.3 fusion.20
  75.4 1.4 collective-permute-done.3
  76.8 0.4 multiply_convert_fusion
  77.2 0.8 copy-done.16
  78.1 0.2 copy-done.17
  78.3 5.2 %copy-done.1 = bf16[2048,3584]{1,0:T(8,128)(2,1)S(1)} copy-done((bf16[2048,3584]{1,0:T(8,128)(2,1)S(1)}, bf16[2048,3584]{1,0:T(8,128)(2,1)}, u32[]{:S(2)}) %copy-start.1) | copy-done | bytes 14680088
  83.4 5.2 %copy-done.4 = bf16[2048,3584]{1,0:T(8,128)(2,1)S(1)} copy-done((bf16[2048,3584]{1,0:T(8,128)(2,1)S(1)}, bf16[2048,3584]{1,0:T(8,128)(2,1)}, u32[]{:S(2)}) %copy-start.4) | copy-done | bytes 14680088
  88.6 25.7 %backward_rows.3 = (bf16[128,2048]{1,0:T(8,128)(2,1)S(1)}, f32[128,1]{1,0:T(8,128)S(1)}, bf16[256,3584]{1,0:T(8,128)(2,1)}, bf16[256,3584]{1,0:T(8,128)(2,1)}, bf16[256,3584]{1,0:T(8,128)(2,1)}) custom-call(s32[1]{0:T(128)} %bitcast.8.flag, bf16[128,2048]{1,0:T(8,128)(2,1)} %copy-done.17, bf16[128,2048]{1,0:T(8,128)(2,1)} %copy-done.16, ...), custom_call_target="tpu_custom_call" | custom-call | flops 13153337344 | bytes 14680064 | tf_op jit(solution)/shard_map/backward_rows/pallas_call | solution.py:155
  114.3 0.1 select_reduce_fusion
  114.4 1.7 collective-permute-start.22
  116.1 1.5 collective-permute-start.17
  117.6 0.5 collective-permute-start.14
  118.2 2.3 %collective-permute-start.9 = (bf16[128,2048]{1,0:T(8,128)(2,1)S(1)}, bf16[128,2048]{1,0:T(8,128)(2,1)S(1)}, u32[]{:S(2)}, u32[]{:S(2)}) collective-permute-start(bf16[128,2048]{1,0:T(8,128)(2,1)S(1)} %get-tuple-element.35), channel_id=1, source_target_pairs={{0,8},{8,0},{1,9},{9,1},{2,10},{10,2},{3,11},{11,3},{4,12},{12,4},... | collective-permute-start | bytes 1572872 | tf_op jit(solution)/shard_map/ppermute | solution.py:301
  120.4 1.7 collective-permute-start.11
  122.2 0.3 collective-permute-start.10
  122.5 5.2 %copy-done.2 = bf16[2048,3584]{1,0:T(8,128)(2,1)S(1)} copy-done((bf16[2048,3584]{1,0:T(8,128)(2,1)S(1)}, bf16[2048,3584]{1,0:T(8,128)(2,1)}, u32[]{:S(2)}) %copy-start.2) | copy-done | bytes 14680088
  127.7 5.2 %copy-done.5 = bf16[2048,3584]{1,0:T(8,128)(2,1)S(1)} copy-done((bf16[2048,3584]{1,0:T(8,128)(2,1)S(1)}, bf16[2048,3584]{1,0:T(8,128)(2,1)}, u32[]{:S(2)}) %copy-start.5) | copy-done | bytes 14680088
  132.9 11.3 %forward_rows.3 = (bf16[256,3584]{1,0:T(8,128)(2,1)}, bf16[256,3584]{1,0:T(8,128)(2,1)}, bf16[256,3584]{1,0:T(8,128)(2,1)}) custom-call(bf16[128,2048]{1,0:T(8,128)(2,1)} %collective-permute-done.4.refs_0_.refs_2_, bf16[128,2048]{1,0:T(8,128)(2,1)} %collective-permute-done.6.refs_1_.refs_3_, bf16[2048,3584]{1,0:T(8,128)(2,1)S(1)} %copy-done.2, ...), custom_call_target="tpu_custom_call" | custom-call | flops 7516192768 | bytes 5505024 | tf_op jit(solution)/shard_map/forward_rows/pallas_call | solution.py:96
  144.1 0.5 add_bitcast_fusion
  144.7 1.7 collective-permute-start.13
  146.4 0.4 collective-permute-start.12
  146.8 1.7 collective-permute-start.18
  148.5 0.3 collective-permute-start.15
  148.9 0.4 fusion.9
  149.3 1.3 fusion.8
  150.5 2.5 %collective-permute-done.12 = bf16[64,2048]{1,0:T(8,128)(2,1)S(1)} collective-permute-done((bf16[64,2048]{1,0:T(8,128)(2,1)S(1)}, bf16[64,2048]{1,0:T(8,128)(2,1)S(1)}, u32[]{:S(2)}, u32[]{:S(2)}) %collective-permute-start.12) | collective-permute-done | bytes 262176 | tf_op jit(solution)/shard_map/ppermute | solution.py:282
  153.1 9.3 %collective-permute-done.18.refs_10_.refs_15_ = bf16[128,2048]{1,0:T(8,128)(2,1)S(1)} collective-permute-done((bf16[128,2048]{1,0:T(8,128)(2,1)S(1)}, bf16[128,2048]{1,0:T(8,128)(2,1)S(1)}, u32[]{:S(2)}, u32[]{:S(2)}) %collective-permute-start.18) | collective-permute-done | bytes 524320 | tf_op jit(solution)/shard_map/ppermute | solution.py:278
  162.4 1.7 collective-permute-start.19
  164.1 0.3 collective-permute-start.16
  164.5 15.7 %forward_rows.2 = (bf16[384,3584]{1,0:T(8,128)(2,1)}, bf16[384,3584]{1,0:T(8,128)(2,1)}, bf16[384,3584]{1,0:T(8,128)(2,1)}) custom-call(bf16[128,2048]{1,0:T(8,128)(2,1)} %copy-done.10, bf16[128,2048]{1,0:T(8,128)(2,1)} %copy-done.9, bf16[128,2048]{1,0:T(8,128)(2,1)} %copy-done.11, bf16[2048,3584]{1,0:T(8,128)(2,1)S(1)} %copy-done.2, ...), custom_call_target="tpu_custom_call" | custom-call | flops 11274289152 | bytes 8257536 | tf_op jit(solution)/shard_map/forward_rows/pallas_call | solution.py:96
  180.2 1.7 collective-permute-start.21
  182.0 0.4 collective-permute-start.20
  182.4 20.0 %weight_grads.2 = (f32[256,3584]{1,0:T(8,128)S(1)}, f32[256,3584]{1,0:T(8,128)S(1)}, f32[256,3584]{1,0:T(8,128)S(1)}) custom-call(s32[1]{0:T(128)} %bitcast.10.refs_0_, bf16[128,2048]{1,0:T(8,128)(2,1)} %fusion.2.refs_0_.refs_1_, bf16[128,2048]{1,0:T(8,128)(2,1)} %collective-permute-done.4.refs_0_.refs_2_, ...), custom_call_target="tpu_custom_call" | custom-call | flops 12918456320 | bytes 33947648 | tf_op jit(solution)/shard_map/weight_grads/pallas_call | solution.py:234
  202.4 0.9 pad_maximum_fusion.refs_6_.refs_9_
  203.3 15.9 %weight_grads.3 = (bf16[256,3584]{1,0:T(8,128)(2,1)}, bf16[256,3584]{1,0:T(8,128)(2,1)}, bf16[256,3584]{1,0:T(8,128)(2,1)}) custom-call(s32[1]{0:T(128)} %bitcast.10.refs_0_, bf16[128,2048]{1,0:T(8,128)(2,1)} %copy-done.10, bf16[128,2048]{1,0:T(8,128)(2,1)} %copy-done.9, bf16[128,2048]{1,0:T(8,128)(2,1)} %copy-done.11, bf16[128,2048]{1,0:T(8,128)(2,1)} %copy-done.7, ...), custom_call_target="tpu_custom_call" | custom-call | flops 7751073792 | bytes 28442624 | tf_op jit(solution)/shard_map/weight_grads/pallas_call | solution.py:234
  (57 shorter events, 0.2 us)
Async XLA Ops:
  0.6 21.8 %collective-permute-start.1 = (bf16[128,2048]{1,0:T(8,128)(2,1)}, bf16[128,2048]{1,0:T(8,128)(2,1)}, u32[]{:S(2)}, u32[]{:S(2)}) collective-permute-start(bf16[128,2048]{1,0:T(8,128)(2,1)} %bitcast.39), channel_id=1, source_target_pairs={{16,24},{24,16},{17,25},{25,17},{18,26},{26,18},{19,27},{27,19},{2... | collective-permute-start | bytes 1572872 | tf_op jit(solution)/shard_map/ppermute | solution.py:301
  2.1 16.1 %collective-permute-start = (bf16[128,2048]{1,0:T(8,128)(2,1)}, bf16[128,2048]{1,0:T(8,128)(2,1)}, u32[]{:S(2)}, u32[]{:S(2)}) collective-permute-start(bf16[128,2048]{1,0:T(8,128)(2,1)} %bitcast.40), channel_id=1, source_target_pairs={{16,24},{24,16},{0,8},{8,0},{17,25},{25,17},{1,9},{9,1},{18,26},{2... | collective-permute-start | bytes 1572872 | tf_op jit(solution)/shard_map/ppermute | solution.py:301
  5.8 9.5 %copy-start.8 = (bf16[1,128,2048]{2,1,0:T(8,128)(2,1)S(1)}, bf16[1,128,2048]{2,1,0:T(8,128)(2,1)}, u32[]{:S(2)}) copy-start(bf16[1,128,2048]{2,1,0:T(8,128)(2,1)} %param.8) | copy-start | bytes 1572868
  5.8 9.5 %copy-start.14 = (s32[1,1,128]{2,1,0:T(1,128)S(1)}, s32[1,1,128]{2,1,0:T(1,128)}, u32[]{:S(2)}) copy-start(s32[1,1,128]{2,1,0:T(1,128)} %param.12) | copy-start | bytes 1540
  5.8 9.8 %copy-start.12 = (bf16[1,1,128,2048]{3,2,1,0:T(8,128)(2,1)S(1)}, bf16[1,1,128,2048]{3,2,1,0:T(8,128)(2,1)}, u32[]{:S(2)}) copy-start(bf16[1,1,128,2048]{3,2,1,0:T(8,128)(2,1)} %param.7) | copy-start | bytes 1572868
  20.4 31.6 %collective-permute-start.6 = (bf16[128,2048]{1,0:T(8,128)(2,1)}, bf16[128,2048]{1,0:T(8,128)(2,1)}, u32[]{:S(2)}, u32[]{:S(2)}) collective-permute-start(bf16[128,2048]{1,0:T(8,128)(2,1)} %fusion.2.refs_0_.refs_1_), channel_id=1, source_target_pairs={{0,1},{2,0},{4,2},{6,4},{7,6},{5,7},{3,5},{1,3},{16,17},{18,16},{2... | collective-permute-start | bytes 1572872 | tf_op jit(solution)/shard_map/ppermute | solution.py:278
  22.4 31.6 %collective-permute-start.4 = (bf16[128,2048]{1,0:T(8,128)(2,1)}, bf16[128,2048]{1,0:T(8,128)(2,1)}, u32[]{:S(2)}, u32[]{:S(2)}) collective-permute-start(bf16[128,2048]{1,0:T(8,128)(2,1)} %fusion.2.refs_0_.refs_1_), channel_id=1, source_target_pairs={{0,2},{2,4},{4,6},{6,7},{7,5},{5,3},{3,1},{1,0},{16,18},{18,20},{2... | collective-permute-start | bytes 1572872 | tf_op jit(solution)/shard_map/ppermute | solution.py:277
  35.6 5.2 %copy-start = (bf16[2048,3584]{1,0:T(8,128)(2,1)}, bf16[2048,3584]{1,0:T(8,128)(2,1)S(1)}, u32[]{:S(2)}) copy-start(bf16[2048,3584]{1,0:T(8,128)(2,1)S(1)} %get-tuple-element.29.refs_3_.refs_4_.refs_2_) | copy-start | bytes 44040196
  40.8 5.2 %copy-start.3 = (bf16[2048,3584]{1,0:T(8,128)(2,1)}, bf16[2048,3584]{1,0:T(8,128)(2,1)S(1)}, u32[]{:S(2)}) copy-start(bf16[2048,3584]{1,0:T(8,128)(2,1)S(1)} %get-tuple-element.30.refs_4_.refs_5_.refs_3_) | copy-start | bytes 44040196
  46.0 1.5 collective-permute-start.2
  49.0 27.8 %copy-start.15 = (f32[1,1,128]{2,1,0:T(1,128)S(1)}, f32[1,1,128]{2,1,0:T(1,128)}, u32[]{:S(2)}) copy-start(f32[1,1,128]{2,1,0:T(1,128)} %param.13) | copy-start | bytes 1540
  49.0 26.1 %collective-permute-start.8 = (bf16[128,2048]{1,0:T(8,128)(2,1)S(1)}, bf16[128,2048]{1,0:T(8,128)(2,1)S(1)}, u32[]{:S(2)}, u32[]{:S(2)}) collective-permute-start(bf16[128,2048]{1,0:T(8,128)(2,1)S(1)} %add_convert_fusion), channel_id=1, source_target_pairs={{16,0},{17,1},{18,2},{19,3},{20,4},{21,5},{22,6},{23,7},{24,8},{25... | collective-permute-start | bytes 1572872 | tf_op jit(solution)/shard_map/ppermute | solution.py:335
  50.7 26.1 %collective-permute-start.3 = (bf16[128,2048]{1,0:T(8,128)(2,1)S(1)}, bf16[128,2048]{1,0:T(8,128)(2,1)S(1)}, u32[]{:S(2)}, u32[]{:S(2)}) collective-permute-start(bf16[128,2048]{1,0:T(8,128)(2,1)S(1)} %fusion.4), channel_id=1, source_target_pairs={{16,0},{17,1},{18,2},{19,3},{20,4},{21,5},{22,6},{23,7},{24,8},{25... | collective-permute-start | bytes 1572872 | tf_op jit(solution)/shard_map/ppermute | solution.py:334
  52.0 25.2 %collective-permute-start.7 = (bf16[128,2048]{1,0:T(8,128)(2,1)}, bf16[128,2048]{1,0:T(8,128)(2,1)S(1)}, u32[]{:S(2)}, u32[]{:S(2)}) collective-permute-start(bf16[128,2048]{1,0:T(8,128)(2,1)} %collective-permute-done.6.refs_1_.refs_3_), channel_id=1, source_target_pairs={{0,1},{2,0},{4,2},{6,4},{7,6},{5,7},{3,5},{1,3},{16,17},{18,16},{2... | collective-permute-start | bytes 1572872 | tf_op jit(solution)/shard_map/ppermute | solution.py:278
  54.0 23.2 %collective-permute-start.5 = (bf16[128,2048]{1,0:T(8,128)(2,1)}, bf16[128,2048]{1,0:T(8,128)(2,1)S(1)}, u32[]{:S(2)}, u32[]{:S(2)}) collective-permute-start(bf16[128,2048]{1,0:T(8,128)(2,1)} %collective-permute-done.4.refs_0_.refs_2_), channel_id=1, source_target_pairs={{0,2},{2,4},{4,6},{6,7},{7,5},{5,3},{3,1},{1,0},{16,18},{18,20},{2... | collective-permute-start | bytes 1572872 | tf_op jit(solution)/shard_map/ppermute | solution.py:277
  77.2 40.4 %copy-start.13 = (bf16[128,2048]{1,0:T(8,128)(2,1)}, bf16[128,2048]{1,0:T(8,128)(2,1)S(1)}, u32[]{:S(2)}) copy-start(bf16[128,2048]{1,0:T(8,128)(2,1)S(1)} %get-tuple-element.53.refs_6_.refs_11_) | copy-start | bytes 1572868
  77.2 0.9 copy-start.16
  77.2 1.0 copy-start.17
  78.3 5.2 %copy-start.1 = (bf16[2048,3584]{1,0:T(8,128)(2,1)S(1)}, bf16[2048,3584]{1,0:T(8,128)(2,1)}, u32[]{:S(2)}) copy-start(bf16[2048,3584]{1,0:T(8,128)(2,1)} %copy-done) | copy-start | bytes 44040196
  83.4 5.2 %copy-start.4 = (bf16[2048,3584]{1,0:T(8,128)(2,1)S(1)}, bf16[2048,3584]{1,0:T(8,128)(2,1)}, u32[]{:S(2)}) copy-start(bf16[2048,3584]{1,0:T(8,128)(2,1)} %copy-done.3) | copy-start | bytes 44040196
  114.4 7.8 %collective-permute-start.22 = (f32[128]{0:T(128)S(1)}, f32[128]{0:T(128)S(1)}, u32[]{:S(2)}, u32[]{:S(2)}) collective-permute-start(f32[128]{0:T(128)S(1)} %select_reduce_fusion), channel_id=1, source_target_pairs={{0,8},{8,0},{1,9},{9,1},{2,10},{10,2},{3,11},{11,3},{4,12},{12,4},... | collective-permute-start | bytes 1544 | tf_op jit(solution)/shard_map/ppermute | solution.py:348
  116.1 30.7 %collective-permute-start.17 = (bf16[128,2048]{1,0:T(8,128)(2,1)S(1)}, bf16[128,2048]{1,0:T(8,128)(2,1)S(1)}, u32[]{:S(2)}, u32[]{:S(2)}) collective-permute-start(bf16[128,2048]{1,0:T(8,128)(2,1)S(1)} %get-tuple-element.53.refs_6_.refs_11_), channel_id=1, source_target_pairs={{0,1},{2,0},{4,2},{6,4},{7,6},{5,7},{3,5},{1,3},{16,17},{18,16},{2... | collective-permute-start | bytes 1572872 | tf_op jit(solution)/shard_map/ppermute | solution.py:278
  117.6 30.9 %collective-permute-start.14 = (bf16[128,2048]{1,0:T(8,128)(2,1)S(1)}, bf16[128,2048]{1,0:T(8,128)(2,1)S(1)}, u32[]{:S(2)}, u32[]{:S(2)}) collective-permute-start(bf16[128,2048]{1,0:T(8,128)(2,1)S(1)} %get-tuple-element.53.refs_6_.refs_11_), channel_id=1, source_target_pairs={{0,2},{2,4},{4,6},{6,7},{7,5},{5,3},{3,1},{1,0},{16,18},{18,20},{2... | collective-permute-start | bytes 1572872 | tf_op jit(solution)/shard_map/ppermute | solution.py:277
  118.2 30.7 %collective-permute-start.9 = (bf16[128,2048]{1,0:T(8,128)(2,1)S(1)}, bf16[128,2048]{1,0:T(8,128)(2,1)S(1)}, u32[]{:S(2)}, u32[]{:S(2)}) collective-permute-start(bf16[128,2048]{1,0:T(8,128)(2,1)S(1)} %get-tuple-element.35), channel_id=1, source_target_pairs={{0,8},{8,0},{1,9},{9,1},{2,10},{10,2},{3,11},{11,3},{4,12},{12,4},... | collective-permute-start | bytes 1572872 | tf_op jit(solution)/shard_map/ppermute | solution.py:301
  120.4 24.2 %collective-permute-start.11 = (bf16[128,2048]{1,0:T(8,128)(2,1)}, bf16[128,2048]{1,0:T(8,128)(2,1)S(1)}, u32[]{:S(2)}, u32[]{:S(2)}) collective-permute-start(bf16[128,2048]{1,0:T(8,128)(2,1)} %copy-done.16), channel_id=1, source_target_pairs={{0,1},{2,0},{4,2},{6,4},{7,6},{5,7},{3,5},{1,3},{16,17},{18,16},{2... | collective-permute-start | bytes 1572872 | tf_op jit(solution)/shard_map/ppermute | solution.py:278
  122.2 24.2 %collective-permute-start.10 = (bf16[128,2048]{1,0:T(8,128)(2,1)}, bf16[128,2048]{1,0:T(8,128)(2,1)S(1)}, u32[]{:S(2)}, u32[]{:S(2)}) collective-permute-start(bf16[128,2048]{1,0:T(8,128)(2,1)} %copy-done.17), channel_id=1, source_target_pairs={{0,2},{2,4},{4,6},{6,7},{7,5},{5,3},{3,1},{1,0},{16,18},{18,20},{2... | collective-permute-start | bytes 1572872 | tf_op jit(solution)/shard_map/ppermute | solution.py:277
  122.5 5.2 %copy-start.2 = (bf16[2048,3584]{1,0:T(8,128)(2,1)S(1)}, bf16[2048,3584]{1,0:T(8,128)(2,1)}, u32[]{:S(2)}) copy-start(bf16[2048,3584]{1,0:T(8,128)(2,1)} %copy-done) | copy-start | bytes 44040196
  127.7 5.2 %copy-start.5 = (bf16[2048,3584]{1,0:T(8,128)(2,1)S(1)}, bf16[2048,3584]{1,0:T(8,128)(2,1)}, u32[]{:S(2)}) copy-start(bf16[2048,3584]{1,0:T(8,128)(2,1)} %copy-done.3) | copy-start | bytes 44040196
  144.6 5.9 %copy-start.9 = (bf16[128,2048]{1,0:T(8,128)(2,1)}, bf16[128,2048]{1,0:T(8,128)(2,1)S(1)}, u32[]{:S(2)}) copy-start(bf16[128,2048]{1,0:T(8,128)(2,1)S(1)} %collective-permute-done.11.refs_1_.refs_2_) | copy-start | bytes 1572868
  144.7 8.4 %collective-permute-start.13 = (bf16[64,2048]{1,0:T(8,128)(2,1)S(1)}, bf16[64,2048]{1,0:T(8,128)(2,1)S(1)}, u32[]{:S(2)}, u32[]{:S(2)}) collective-permute-start(bf16[64,2048]{1,0:T(8,128)(2,1)S(1)} %slice.17), channel_id=1, source_target_pairs={{0,1},{2,0},{4,2},{6,4},{7,6},{5,7},{3,5},{1,3},{16,17},{18,16},{2... | collective-permute-start | bytes 786440 | tf_op jit(solution)/shard_map/ppermute | solution.py:283
  146.4 6.6 %copy-start.10 = (bf16[128,2048]{1,0:T(8,128)(2,1)}, bf16[128,2048]{1,0:T(8,128)(2,1)S(1)}, u32[]{:S(2)}) copy-start(bf16[128,2048]{1,0:T(8,128)(2,1)S(1)} %collective-permute-done.10.refs_0_.refs_1_) | copy-start | bytes 1572868
  146.4 6.6 %collective-permute-start.12 = (bf16[64,2048]{1,0:T(8,128)(2,1)S(1)}, bf16[64,2048]{1,0:T(8,128)(2,1)S(1)}, u32[]{:S(2)}, u32[]{:S(2)}) collective-permute-start(bf16[64,2048]{1,0:T(8,128)(2,1)S(1)} %slice.16), channel_id=1, source_target_pairs={{0,2},{2,4},{4,6},{6,7},{7,5},{5,3},{3,1},{1,0},{16,18},{18,20},{2... | collective-permute-start | bytes 786440 | tf_op jit(solution)/shard_map/ppermute | solution.py:282
  146.8 6.3 %copy-start.18 = (bf16[128,2048]{1,0:T(8,128)(2,1)}, bf16[128,2048]{1,0:T(8,128)(2,1)S(1)}, u32[]{:S(2)}) copy-start(bf16[128,2048]{1,0:T(8,128)(2,1)S(1)} %collective-permute-done.17.refs_8_.refs_13_) | copy-start | bytes 1572868
  146.8 15.6 %collective-permute-start.18 = (bf16[128,2048]{1,0:T(8,128)(2,1)S(1)}, bf16[128,2048]{1,0:T(8,128)(2,1)S(1)}, u32[]{:S(2)}, u32[]{:S(2)}) collective-permute-start(bf16[128,2048]{1,0:T(8,128)(2,1)S(1)} %collective-permute-done.17.refs_8_.refs_13_), channel_id=1, source_target_pairs={{0,1},{2,0},{4,2},{6,4},{7,6},{5,7},{3,5},{1,3},{16,17},{18,16},{2... | collective-permute-start | bytes 1572872 | tf_op jit(solution)/shard_map/ppermute | solution.py:278
  148.5 4.6 %copy-start.19 = (bf16[128,2048]{1,0:T(8,128)(2,1)}, bf16[128,2048]{1,0:T(8,128)(2,1)S(1)}, u32[]{:S(2)}) copy-start(bf16[128,2048]{1,0:T(8,128)(2,1)S(1)} %collective-permute-done.14.refs_7_.refs_12_) | copy-start | bytes 1572868
  148.5 15.6 %collective-permute-start.15 = (bf16[128,2048]{1,0:T(8,128)(2,1)S(1)}, bf16[128,2048]{1,0:T(8,128)(2,1)S(1)}, u32[]{:S(2)}, u32[]{:S(2)}) collective-permute-start(bf16[128,2048]{1,0:T(8,128)(2,1)S(1)} %collective-permute-done.14.refs_7_.refs_12_), channel_id=1, source_target_pairs={{0,2},{2,4},{4,6},{6,7},{7,5},{5,3},{3,1},{1,0},{16,18},{18,20},{2... | collective-permute-start | bytes 1572872 | tf_op jit(solution)/shard_map/ppermute | solution.py:277
  153.1 11.3 %copy-start.11 = (bf16[128,2048]{1,0:T(8,128)(2,1)}, bf16[128,2048]{1,0:T(8,128)(2,1)S(1)}, u32[]{:S(2)}) copy-start(bf16[128,2048]{1,0:T(8,128)(2,1)S(1)} %constant_dynamic-update-slice_fusion.refs_2_.refs_3_) | copy-start | bytes 1572868
  162.4 17.7 %copy-start.20 = (bf16[128,2048]{1,0:T(8,128)(2,1)}, bf16[128,2048]{1,0:T(8,128)(2,1)S(1)}, u32[]{:S(2)}) copy-start(bf16[128,2048]{1,0:T(8,128)(2,1)S(1)} %collective-permute-done.18.refs_10_.refs_15_) | copy-start | bytes 1572868
  162.4 17.8 %collective-permute-start.19 = (bf16[128,2048]{1,0:T(8,128)(2,1)S(1)}, bf16[128,2048]{1,0:T(8,128)(2,1)S(1)}, u32[]{:S(2)}, u32[]{:S(2)}) collective-permute-start(bf16[128,2048]{1,0:T(8,128)(2,1)S(1)} %collective-permute-done.18.refs_10_.refs_15_), channel_id=1, source_target_pairs={{0,1},{2,0},{4,2},{6,4},{7,6},{5,7},{3,5},{1,3},{16,17},{18,16},{2... | collective-permute-start | bytes 1572872 | tf_op jit(solution)/shard_map/ppermute | solution.py:278
  164.1 16.1 %copy-start.21 = (bf16[128,2048]{1,0:T(8,128)(2,1)}, bf16[128,2048]{1,0:T(8,128)(2,1)S(1)}, u32[]{:S(2)}) copy-start(bf16[128,2048]{1,0:T(8,128)(2,1)S(1)} %collective-permute-done.15.refs_9_.refs_14_) | copy-start | bytes 1572868
  164.1 17.8 %collective-permute-start.16 = (bf16[128,2048]{1,0:T(8,128)(2,1)S(1)}, bf16[128,2048]{1,0:T(8,128)(2,1)S(1)}, u32[]{:S(2)}, u32[]{:S(2)}) collective-permute-start(bf16[128,2048]{1,0:T(8,128)(2,1)S(1)} %collective-permute-done.15.refs_9_.refs_14_), channel_id=1, source_target_pairs={{0,2},{2,4},{4,6},{6,7},{7,5},{5,3},{3,1},{1,0},{16,18},{18,20},{2... | collective-permute-start | bytes 1572872 | tf_op jit(solution)/shard_map/ppermute | solution.py:277
  180.2 22.2 %copy-start.6 = (bf16[128,2048]{1,0:T(8,128)(2,1)}, bf16[128,2048]{1,0:T(8,128)(2,1)S(1)}, u32[]{:S(2)}) copy-start(bf16[128,2048]{1,0:T(8,128)(2,1)S(1)} %collective-permute-done.19.refs_5_.refs_8_) | copy-start | bytes 1572868
  180.2 22.2 %collective-permute-start.21 = (bf16[64,2048]{1,0:T(8,128)(2,1)S(1)}, bf16[64,2048]{1,0:T(8,128)(2,1)S(1)}, u32[]{:S(2)}, u32[]{:S(2)}) collective-permute-start(bf16[64,2048]{1,0:T(8,128)(2,1)S(1)} %slice.19), channel_id=1, source_target_pairs={{0,1},{2,0},{4,2},{6,4},{7,6},{5,7},{3,5},{1,3},{16,17},{18,16},{2... | collective-permute-start | bytes 786440 | tf_op jit(solution)/shard_map/ppermute | solution.py:283
  182.0 20.4 %copy-start.7 = (bf16[128,2048]{1,0:T(8,128)(2,1)}, bf16[128,2048]{1,0:T(8,128)(2,1)S(1)}, u32[]{:S(2)}) copy-start(bf16[128,2048]{1,0:T(8,128)(2,1)S(1)} %collective-permute-done.16.refs_4_.refs_7_) | copy-start | bytes 1572868
  182.0 20.4 %collective-permute-start.20 = (bf16[64,2048]{1,0:T(8,128)(2,1)S(1)}, bf16[64,2048]{1,0:T(8,128)(2,1)S(1)}, u32[]{:S(2)}, u32[]{:S(2)}) collective-permute-start(bf16[64,2048]{1,0:T(8,128)(2,1)S(1)} %slice.18), channel_id=1, source_target_pairs={{0,2},{2,4},{4,6},{6,7},{7,5},{5,3},{3,1},{1,0},{16,18},{18,20},{2... | collective-permute-start | bytes 786440 | tf_op jit(solution)/shard_map/ppermute | solution.py:282

commit v4 on v3

--- a/solution.py
+++ b/solution.py
@@ -119,7 +119,7 @@
         x_refs, refs = refs[:count], refs[count:]
         g_ref, gate_ref, one, three, two, *refs = refs
         stored, refs = refs[: len(parts)], refs[len(parts) :]
-        back_ref, part_ref, slope_ref, active_ref, hidden_ref, total = refs
+        back_ref, part_ref, *made, total = refs
         step, here = pl.program_id(0), slab(tile)
 
         @pl.when(step == 0)
@@ -127,18 +127,18 @@
             total[...] = jnp.zeros_like(total)
             part_ref[...] = jnp.zeros_like(part_ref)
 
-        x = stacked(x_refs)
-        active, slope, product = forward_parts(
-            jnp.dot(x, one[:, here], preferred_element_type=F32),
-            jnp.dot(x, three[:, here], preferred_element_type=F32),
-        )
-        slope_ref[...] = slope.astype(BF16)
-        active_ref[...] = active.astype(BF16)
-        hidden_ref[...] = product.astype(BF16)
+        if made:
+            x = stacked(x_refs)
+            active, slope, product = forward_parts(
+                jnp.dot(x, one[:, here], preferred_element_type=F32),
+                jnp.dot(x, three[:, here], preferred_element_type=F32),
+            )
+            for ref, value in zip(made, (slope, active, product)):
+                ref[...] = value.astype(BF16)
 
         @pl.when(flag[0] > 0)
         def _():
-            slope_of, active_of, hidden_of = stored if parts else (slope_ref, active_ref, hidden_ref)
+            slope_of, active_of, hidden_of = stored if parts else made
             back = jnp.dot(g_ref[...], two[...], preferred_element_type=F32)
             part_ref[...] += jnp.sum(hidden_of[...].astype(F32) * back, axis=1, keepdims=True)
             scaled = gate_ref[...] * back
@@ -161,9 +161,9 @@
         + [columns(width, tile)]
         + [columns(rows, tile)] * len(parts),
         out_specs=[pl.BlockSpec((rows, width), lambda i: (0, 0)), pl.BlockSpec((rows, 1), lambda i: (0, 0))]
-        + [columns(height, tile)] * 3,
+        + [columns(height, tile)] * (3 if count else 0),
         out_shape=[jax.ShapeDtypeStruct((rows, width), BF16), jax.ShapeDtypeStruct((rows, 1), F32)]
-        + [pltpu.HBM((height, hidden), BF16)] * 3,
+        + [pltpu.HBM((height, hidden), BF16)] * (3 if count else 0),
         scratch_shapes=[pltpu.VMEM((rows, width), F32)],
         compiler_params=params(20),
         cost_estimate=pl.CostEstimate(
@@ -333,16 +333,15 @@
     ig_theirs = placed_back(pick_theirs, dy_theirs, back_last, other_last)
     dy_first_mine = lax.ppermute(ig_mine, "section", [(1, 0)])
     dy_first_theirs = lax.ppermute(ig_theirs, "section", [(1, 0)])
-    kept = [tuple(own), tuple(forward_rows(x_groups[1], w_one, w_three))]
+    kept = [tuple(own), tuple(forward_rows(x_groups[1] + x_groups[2], w_one, w_three))]
     g_first = picked(dy_first_mine, dy_first_theirs)
     g_rows = jnp.where(last, g_last, g_first)
     s_rows = (gates * g_rows.astype(F32)).astype(BF16)
     s_groups = around(s_rows, sections, replicas)
 
-    back_first, part_first, *third = backward_rows(
-        jnp.logical_not(last), x_groups[2], g_first, gates, w_one, w_three, w_two, own
+    back_first, part_first = backward_rows(
+        jnp.logical_not(last), [], g_first, gates, w_one, w_three, w_two, own
     )
-    kept.append(tuple(third))
     other_first = swapped(back_first, first_only)
     part = jnp.where(last, part_last, part_first)[:, 0]
     gate_grad = part + lax.ppermute(part, "et", first_only)

time: 220 us -> 209 us (0.950)
  local copies, waits for them, and re-layouts: 33 us -> 21.9 us
    unnamed x45 -> x41, local copies, waits for them, and re-layouts: 32.2 us -> 21 us
    pallas_call x2, Pallas kernels: 37.4 us -> 26.8 us  [backward_rows(): pl.pallas_call(kernel, grid=(hidden // tile,), in_specs=[pl.BlockSpec(mem...]
    pallas_call x2, Pallas kernels: 27 us -> 36.1 us  [forward_rows(): pl.pallas_call(kernel, grid=(hidden // tile,), in_specs=[held(b) for b in...]
    ppermute x6, waiting for transfers between devices: 9.31 us -> 5.69 us  [around(): behind = lax.ppermute(behind, axes, shift(-1))]
    ppermute x1, waiting for transfers between devices: 0.01 us -> 2.55 us  [per_device(): gate_grad = part + lax.ppermute(part, 'et', first_only)]
  transfers between devices with their start and end apart: 23 -> 23, of which waited for: 5 -> 7; matrix products, arithmetic and copies ran while one was open for 5% -> 5% of each run, Pallas kernels for 31% -> 44%
where the time goes in v4:
time: 209 us; the launch traced here: 208 us
  Pallas kernels  108 us (52%)
  waiting for transfers between devices  37.8 us (18%)
  starting transfers between devices  28.6 us (14%)
  local copies, waits for them, and re-layouts  21.9 us (10%)
  matrix products  9.36 us (4%)
    pallas_call x2, Pallas kernels, forward_rows(): pl.pallas_call(kernel, grid=(hidden // tile,), in_specs=[held(b) for b in...  36.1 us
    pallas_call x2, Pallas kernels, weight_grads(): pl.pallas_call(kernel, grid_spec=pltpu.PrefetchScalarGridSpec(num_scalar_...  35.7 us
    pallas_call x2, Pallas kernels, backward_rows(): pl.pallas_call(kernel, grid=(hidden // tile,), in_specs=[pl.BlockSpec(mem...  26.8 us
    unnamed x41, local copies, waits for them, and re-layouts  21 us
    ppermute x1, waiting for transfers between devices, per_device(): dy_first_theirs = lax.ppermute(ig_theirs, 'section', [(1, 0)])  20.8 us
    ppermute x6, starting transfers between devices, around(): behind = lax.ppermute(behind, axes, shift(-1))  9.92 us
    pallas_call x1, Pallas kernels, load(): pl.pallas_call(kernel, in_specs=[pl.BlockSpec(memory_space=pltpu.HBM)] *...  9.45 us
    ppermute x4, starting transfers between devices, swapped(): return lax.ppermute(value, ('section', 'et'), pairs)  8.68 us
  transfers between devices with their start and end apart: 23, of which 7 were waited for; matrix products, arithmetic and copies ran while one was open for 5% of the time, Pallas kernels for 44%

profile of v4, /device:TPU:0, one launch (start us, length us, event | category | flops | bytes accessed | tf_op | source)
XLA Modules:
  0.0 208.3 jit_solution(12711862306001112198)
XLA Ops:
  0.6 1.5 collective-permute-start.1
  2.1 3.0 %collective-permute-start = (bf16[128,2048]{1,0:T(8,128)(2,1)}, bf16[128,2048]{1,0:T(8,128)(2,1)}, u32[]{:S(2)}, u32[]{:S(2)}) collective-permute-start(bf16[128,2048]{1,0:T(8,128)(2,1)} %bitcast.40), channel_id=1, source_target_pairs={{16,24},{24,16},{0,8},{8,0},{17,25},{25,17},{1,9},{9,1},{18,26},{2... | collective-permute-start | bytes 1572872 | tf_op jit(solution)/shard_map/ppermute | solution.py:301
  5.1 0.8 copy.14.refs_2_.refs_1_
  5.8 0.0 copy-start.12
  5.8 0.0 copy-start.10
  5.9 9.5 %load.1 = (bf16[2048,3584]{1,0:T(8,128)(2,1)S(1)}, bf16[2048,3584]{1,0:T(8,128)(2,1)S(1)}) custom-call(bf16[2048,3584]{1,0:T(8,128)(2,1)} %bitcast.37, bf16[2048,3584]{1,0:T(8,128)(2,1)} %bitcast.38), custom_call_target="tpu_custom_call" | custom-call | bytes 29360128 | tf_op jit(solution)/shard_map/load/pallas_call | solution.py:41
  15.3 0.3 fusion.14
  15.7 0.3 fusion.16
  16.0 2.1 %collective-permute-done = bf16[128,2048]{1,0:T(8,128)(2,1)} collective-permute-done((bf16[128,2048]{1,0:T(8,128)(2,1)}, bf16[128,2048]{1,0:T(8,128)(2,1)}, u32[]{:S(2)}, u32[]{:S(2)}) %collective-permute-start) | collective-permute-done | bytes 524320 | tf_op jit(solution)/shard_map/ppermute | solution.py:301
  18.2 2.2 %fusion.1.refs_0_.refs_1_ = bf16[128,2048]{1,0:T(8,128)(2,1)} fusion(f32[128,2048]{1,0:T(8,128)S(1)} %fusion.16, bf16[128,2048]{1,0:T(8,128)(2,1)} %collective-permute-done, s32[128]{0:T(128)S(1)} %iota_add_fusion, s32[128]{0:T(128)S(1)} %bitcast.43), kind=kOutput, calls=%fused_computation.7 | convolution fusion | flops 67649536 | bytes 2098176 | tf_op jit(solution)/shard_map/dot_general | solution.py:311
  20.3 2.0 collective-permute-start.9
  22.4 0.1 collective-permute-start.6
  22.5 0.0 collective-permute-done.1
  22.5 1.4 fusion.2.refs_1_
  23.9 11.7 %backward_rows.2 = (bf16[128,2048]{1,0:T(8,128)(2,1)S(1)}, f32[128,1]{1,0:T(8,128)S(1)}, bf16[128,3584]{1,0:T(8,128)(2,1)}, bf16[128,3584]{1,0:T(8,128)(2,1)}, bf16[128,3584]{1,0:T(8,128)(2,1)}) custom-call(s32[1]{0:T(128)} %bitcast.2.flag, bf16[128,2048]{1,0:T(8,128)(2,1)} %fusion.1.refs_0_.refs_1_, bf16[128,2048]{1,0:T(8,128)(2,1)S(1)} %fusion.2.refs_1_, ...), custom_call_target="tpu_custom_call" | custom-call | flops 9395240960 | bytes 14680064 | tf_op jit(solution)/shard_map/backward_rows/pallas_call | solution.py:155
  35.5 5.2 %copy-done = bf16[2048,3584]{1,0:T(8,128)(2,1)} copy-done((bf16[2048,3584]{1,0:T(8,128)(2,1)}, bf16[2048,3584]{1,0:T(8,128)(2,1)S(1)}, u32[]{:S(2)}) %copy-start) | copy-done | bytes 14680088
  40.7 5.2 %copy-done.2 = bf16[2048,3584]{1,0:T(8,128)(2,1)} copy-done((bf16[2048,3584]{1,0:T(8,128)(2,1)}, bf16[2048,3584]{1,0:T(8,128)(2,1)S(1)}, u32[]{:S(2)}) %copy-start.2) | copy-done | bytes 14680088
  45.9 0.7 collective-permute-start.2
  46.6 0.4 fusion.23
  47.0 0.4 fusion.12
  47.4 0.0 copy-start.13
  47.4 0.0 collective-permute-done.2
  47.5 1.5 add_convert_fusion.1
  48.9 1.3 collective-permute-start.4
  50.2 0.4 fusion.3
  50.6 1.3 collective-permute-start.3
  51.9 0.0 collective-permute-done.9.refs_1_.refs_3_
  52.0 2.0 collective-permute-start.10
  54.0 0.1 collective-permute-start.7
  54.1 20.8 %collective-permute-done.4 = bf16[128,2048]{1,0:T(8,128)(2,1)S(1)} collective-permute-done((bf16[128,2048]{1,0:T(8,128)(2,1)S(1)}, bf16[128,2048]{1,0:T(8,128)(2,1)S(1)}, u32[]{:S(2)}, u32[]{:S(2)}) %collective-permute-start.4) | collective-permute-done | bytes 524320 | tf_op jit(solution)/shard_map/ppermute | solution.py:335
  74.9 0.3 fusion.20
  75.3 1.4 collective-permute-done.3
  76.7 0.4 multiply_convert_fusion
  77.1 1.7 collective-permute-start.17
  78.8 0.3 collective-permute-start.14
  79.2 5.2 %copy-done.1 = bf16[2048,3584]{1,0:T(8,128)(2,1)S(1)} copy-done((bf16[2048,3584]{1,0:T(8,128)(2,1)S(1)}, bf16[2048,3584]{1,0:T(8,128)(2,1)}, u32[]{:S(2)}) %copy-start.1) | copy-done | bytes 14680088
  84.3 5.2 %copy-done.3 = bf16[2048,3584]{1,0:T(8,128)(2,1)S(1)} copy-done((bf16[2048,3584]{1,0:T(8,128)(2,1)S(1)}, bf16[2048,3584]{1,0:T(8,128)(2,1)}, u32[]{:S(2)}) %copy-start.3) | copy-done | bytes 14680088
  89.5 15.2 %backward_rows.3 = (bf16[128,2048]{1,0:T(8,128)(2,1)S(1)}, f32[128,1]{1,0:T(8,128)S(1)}) custom-call(s32[1]{0:T(128)} %bitcast.8.flag, bf16[128,2048]{1,0:T(8,128)(2,1)S(1)} %get-tuple-element.48.refs_0_, f32[128,1]{1,0:T(8,128)S(1)} %copy.14.refs_2_.refs_1_, bf16[2048,3584]{1,0:T(8,128)(2,1)S(1)} %copy-done.1, bf16[2048,3584]{1,0:T(8,128)(2,1)S(1)} %copy-done.3, ...), custom_call_target="tpu_custom_call" | custom-call | flops 5637144576 | bytes 14680064 | tf_op jit(solution)/shard_map/backward_rows/pallas_call | solution.py:155
  104.7 3.6 %collective-permute-start.5 = (bf16[128,2048]{1,0:T(8,128)(2,1)S(1)}, bf16[128,2048]{1,0:T(8,128)(2,1)S(1)}, u32[]{:S(2)}, u32[]{:S(2)}) collective-permute-start(bf16[128,2048]{1,0:T(8,128)(2,1)S(1)} %get-tuple-element.32), channel_id=1, source_target_pairs={{0,8},{8,0},{1,9},{9,1},{2,10},{10,2},{3,11},{11,3},{4,12},{12,4},... | collective-permute-start | bytes 1572872 | tf_op jit(solution)/shard_map/ppermute | solution.py:301
  108.3 1.5 collective-permute-start.11
  109.8 0.6 collective-permute-start.8
  110.4 0.2 copy-done.15
  110.6 20.3 %forward_rows.3 = (bf16[512,3584]{1,0:T(8,128)(2,1)}, bf16[512,3584]{1,0:T(8,128)(2,1)}, bf16[512,3584]{1,0:T(8,128)(2,1)}) custom-call(bf16[128,2048]{1,0:T(8,128)(2,1)} %collective-permute-done.6.refs_0_.refs_2_, bf16[128,2048]{1,0:T(8,128)(2,1)} %collective-permute-done.9.refs_1_.refs_3_, bf16[128,2048]{1,0:T(8,128)(2,1)} %copy-done.15, ...), custom_call_target="tpu_custom_call" | custom-call | flops 15032385536 | bytes 11010048 | tf_op jit(solution)/shard_map/forward_rows/pallas_call | solution.py:96
  130.9 0.1 select_reduce_fusion
  131.1 0.6 collective-permute-start.22
  131.7 0.4 fusion.8
  132.1 2.6 %collective-permute-done.22 = f32[128]{0:T(128)S(1)} collective-permute-done((f32[128]{0:T(128)S(1)}, f32[128]{0:T(128)S(1)}, u32[]{:S(2)}, u32[]{:S(2)}) %collective-permute-start.22) | collective-permute-done | bytes 544 | tf_op jit(solution)/shard_map/ppermute | solution.py:347
  134.7 1.4 collective-permute-start.12
  136.1 0.5 add_bitcast_fusion
  136.6 0.7 collective-permute-start.13
  137.3 1.6 collective-permute-start.18
  139.0 0.4 collective-permute-start.15
  139.4 1.3 fusion.6
  140.6 3.2 %collective-permute-done.12 = bf16[64,2048]{1,0:T(8,128)(2,1)S(1)} collective-permute-done((bf16[64,2048]{1,0:T(8,128)(2,1)S(1)}, bf16[64,2048]{1,0:T(8,128)(2,1)S(1)}, u32[]{:S(2)}, u32[]{:S(2)}) %collective-permute-start.12) | collective-permute-done | bytes 262176 | tf_op jit(solution)/shard_map/ppermute | solution.py:282
  143.9 1.9 collective-permute-done.13
  145.9 5.7 %collective-permute-done.18.refs_10_.refs_15_ = bf16[128,2048]{1,0:T(8,128)(2,1)S(1)} collective-permute-done((bf16[128,2048]{1,0:T(8,128)(2,1)S(1)}, bf16[128,2048]{1,0:T(8,128)(2,1)S(1)}, u32[]{:S(2)}, u32[]{:S(2)}) %collective-permute-start.18) | collective-permute-done | bytes 524320 | tf_op jit(solution)/shard_map/ppermute | solution.py:278
  151.6 1.0 collective-permute-start.19
  152.5 1.1 collective-permute-start.16
  153.6 15.8 %forward_rows.2 = (bf16[384,3584]{1,0:T(8,128)(2,1)}, bf16[384,3584]{1,0:T(8,128)(2,1)}, bf16[384,3584]{1,0:T(8,128)(2,1)}) custom-call(bf16[128,2048]{1,0:T(8,128)(2,1)} %copy-done.8, bf16[128,2048]{1,0:T(8,128)(2,1)} %copy-done.7, bf16[128,2048]{1,0:T(8,128)(2,1)} %copy-done.9, bf16[2048,3584]{1,0:T(8,128)(2,1)S(1)} %copy-done.1, ...), custom_call_target="tpu_custom_call" | custom-call | flops 11274289152 | bytes 8257536 | tf_op jit(solution)/shard_map/forward_rows/pallas_call | solution.py:96
  169.4 1.0 collective-permute-start.21
  170.5 1.1 collective-permute-start.20
  171.6 19.9 %weight_grads.2 = (f32[256,3584]{1,0:T(8,128)S(1)}, f32[256,3584]{1,0:T(8,128)S(1)}, f32[256,3584]{1,0:T(8,128)S(1)}) custom-call(s32[1]{0:T(128)} %bitcast.10.refs_0_, bf16[128,2048]{1,0:T(8,128)(2,1)} %fusion.1.refs_0_.refs_1_, bf16[128,2048]{1,0:T(8,128)(2,1)} %collective-permute-done.6.refs_0_.refs_2_, ...), custom_call_target="tpu_custom_call" | custom-call | flops 12918456320 | bytes 33947648 | tf_op jit(solution)/shard_map/weight_grads/pallas_call | solution.py:234
  191.5 0.8 pad_maximum_fusion.refs_6_.refs_9_
  192.4 15.9 %weight_grads.3 = (bf16[256,3584]{1,0:T(8,128)(2,1)}, bf16[256,3584]{1,0:T(8,128)(2,1)}, bf16[256,3584]{1,0:T(8,128)(2,1)}) custom-call(s32[1]{0:T(128)} %bitcast.10.refs_0_, bf16[128,2048]{1,0:T(8,128)(2,1)} %copy-done.8, bf16[128,2048]{1,0:T(8,128)(2,1)} %copy-done.7, bf16[128,2048]{1,0:T(8,128)(2,1)} %copy-done.9, bf16[128,2048]{1,0:T(8,128)(2,1)} %copy-done.5, ...), custom_call_target="tpu_custom_call" | custom-call | flops 7751073792 | bytes 28442624 | tf_op jit(solution)/shard_map/weight_grads/pallas_call | solution.py:234
  (53 shorter events, 0.2 us)
Async XLA Ops:
  0.6 21.8 %collective-permute-start.1 = (bf16[128,2048]{1,0:T(8,128)(2,1)}, bf16[128,2048]{1,0:T(8,128)(2,1)}, u32[]{:S(2)}, u32[]{:S(2)}) collective-permute-start(bf16[128,2048]{1,0:T(8,128)(2,1)} %bitcast.39), channel_id=1, source_target_pairs={{16,24},{24,16},{17,25},{25,17},{18,26},{26,18},{19,27},{27,19},{2... | collective-permute-start | bytes 1572872 | tf_op jit(solution)/shard_map/ppermute | solution.py:301
  2.1 16.1 %collective-permute-start = (bf16[128,2048]{1,0:T(8,128)(2,1)}, bf16[128,2048]{1,0:T(8,128)(2,1)}, u32[]{:S(2)}, u32[]{:S(2)}) collective-permute-start(bf16[128,2048]{1,0:T(8,128)(2,1)} %bitcast.40), channel_id=1, source_target_pairs={{16,24},{24,16},{0,8},{8,0},{17,25},{25,17},{1,9},{9,1},{18,26},{2... | collective-permute-start | bytes 1572872 | tf_op jit(solution)/shard_map/ppermute | solution.py:301
  5.8 9.5 %copy-start.6 = (bf16[1,128,2048]{2,1,0:T(8,128)(2,1)S(1)}, bf16[1,128,2048]{2,1,0:T(8,128)(2,1)}, u32[]{:S(2)}) copy-start(bf16[1,128,2048]{2,1,0:T(8,128)(2,1)} %param.8) | copy-start | bytes 1572868
  5.8 9.5 %copy-start.12 = (s32[1,1,128]{2,1,0:T(1,128)S(1)}, s32[1,1,128]{2,1,0:T(1,128)}, u32[]{:S(2)}) copy-start(s32[1,1,128]{2,1,0:T(1,128)} %param.12) | copy-start | bytes 1540
  5.8 9.8 %copy-start.10 = (bf16[1,1,128,2048]{3,2,1,0:T(8,128)(2,1)S(1)}, bf16[1,1,128,2048]{3,2,1,0:T(8,128)(2,1)}, u32[]{:S(2)}) copy-start(bf16[1,1,128,2048]{3,2,1,0:T(8,128)(2,1)} %param.7) | copy-start | bytes 1572868
  20.3 31.6 %collective-permute-start.9 = (bf16[128,2048]{1,0:T(8,128)(2,1)}, bf16[128,2048]{1,0:T(8,128)(2,1)}, u32[]{:S(2)}, u32[]{:S(2)}) collective-permute-start(bf16[128,2048]{1,0:T(8,128)(2,1)} %fusion.1.refs_0_.refs_1_), channel_id=1, source_target_pairs={{0,1},{2,0},{4,2},{6,4},{7,6},{5,7},{3,5},{1,3},{16,17},{18,16},{2... | collective-permute-start | bytes 1572872 | tf_op jit(solution)/shard_map/ppermute | solution.py:278
  22.4 31.6 %collective-permute-start.6 = (bf16[128,2048]{1,0:T(8,128)(2,1)}, bf16[128,2048]{1,0:T(8,128)(2,1)}, u32[]{:S(2)}, u32[]{:S(2)}) collective-permute-start(bf16[128,2048]{1,0:T(8,128)(2,1)} %fusion.1.refs_0_.refs_1_), channel_id=1, source_target_pairs={{0,2},{2,4},{4,6},{6,7},{7,5},{5,3},{3,1},{1,0},{16,18},{18,20},{2... | collective-permute-start | bytes 1572872 | tf_op jit(solution)/shard_map/ppermute | solution.py:277
  35.5 5.2 %copy-start = (bf16[2048,3584]{1,0:T(8,128)(2,1)}, bf16[2048,3584]{1,0:T(8,128)(2,1)S(1)}, u32[]{:S(2)}) copy-start(bf16[2048,3584]{1,0:T(8,128)(2,1)S(1)} %get-tuple-element.26.refs_3_.refs_2_.refs_4_) | copy-start | bytes 44040196
  40.7 5.2 %copy-start.2 = (bf16[2048,3584]{1,0:T(8,128)(2,1)}, bf16[2048,3584]{1,0:T(8,128)(2,1)S(1)}, u32[]{:S(2)}) copy-start(bf16[2048,3584]{1,0:T(8,128)(2,1)S(1)} %get-tuple-element.27.refs_4_.refs_3_.refs_5_) | copy-start | bytes 44040196
  45.9 1.5 collective-permute-start.2
  47.4 29.3 %copy-start.13 = (f32[1,1,128]{2,1,0:T(1,128)S(1)}, f32[1,1,128]{2,1,0:T(1,128)}, u32[]{:S(2)}) copy-start(f32[1,1,128]{2,1,0:T(1,128)} %param.13) | copy-start | bytes 1540
  48.9 26.0 %collective-permute-start.4 = (bf16[128,2048]{1,0:T(8,128)(2,1)S(1)}, bf16[128,2048]{1,0:T(8,128)(2,1)S(1)}, u32[]{:S(2)}, u32[]{:S(2)}) collective-permute-start(bf16[128,2048]{1,0:T(8,128)(2,1)S(1)} %add_convert_fusion.1), channel_id=1, source_target_pairs={{16,0},{17,1},{18,2},{19,3},{20,4},{21,5},{22,6},{23,7},{24,8},{25... | collective-permute-start | bytes 1572872 | tf_op jit(solution)/shard_map/ppermute | solution.py:335
  50.6 26.0 %collective-permute-start.3 = (bf16[128,2048]{1,0:T(8,128)(2,1)S(1)}, bf16[128,2048]{1,0:T(8,128)(2,1)S(1)}, u32[]{:S(2)}, u32[]{:S(2)}) collective-permute-start(bf16[128,2048]{1,0:T(8,128)(2,1)S(1)} %fusion.3), channel_id=1, source_target_pairs={{16,0},{17,1},{18,2},{19,3},{20,4},{21,5},{22,6},{23,7},{24,8},{25... | collective-permute-start | bytes 1572872 | tf_op jit(solution)/shard_map/ppermute | solution.py:334
  52.0 56.3 %collective-permute-start.10 = (bf16[128,2048]{1,0:T(8,128)(2,1)}, bf16[128,2048]{1,0:T(8,128)(2,1)S(1)}, u32[]{:S(2)}, u32[]{:S(2)}) collective-permute-start(bf16[128,2048]{1,0:T(8,128)(2,1)} %collective-permute-done.9.refs_1_.refs_3_), channel_id=1, source_target_pairs={{0,1},{2,0},{4,2},{6,4},{7,6},{5,7},{3,5},{1,3},{16,17},{18,16},{2... | collective-permute-start | bytes 1572872 | tf_op jit(solution)/shard_map/ppermute | solution.py:278
  54.0 55.8 %collective-permute-start.7 = (bf16[128,2048]{1,0:T(8,128)(2,1)}, bf16[128,2048]{1,0:T(8,128)(2,1)S(1)}, u32[]{:S(2)}, u32[]{:S(2)}) collective-permute-start(bf16[128,2048]{1,0:T(8,128)(2,1)} %collective-permute-done.6.refs_0_.refs_2_), channel_id=1, source_target_pairs={{0,2},{2,4},{4,6},{6,7},{7,5},{5,3},{3,1},{1,0},{16,18},{18,20},{2... | collective-permute-start | bytes 1572872 | tf_op jit(solution)/shard_map/ppermute | solution.py:277
  77.1 27.6 %copy-start.11 = (bf16[128,2048]{1,0:T(8,128)(2,1)}, bf16[128,2048]{1,0:T(8,128)(2,1)S(1)}, u32[]{:S(2)}) copy-start(bf16[128,2048]{1,0:T(8,128)(2,1)S(1)} %get-tuple-element.47.refs_6_.refs_11_) | copy-start | bytes 1572868
  77.1 60.2 %collective-permute-start.17 = (bf16[128,2048]{1,0:T(8,128)(2,1)S(1)}, bf16[128,2048]{1,0:T(8,128)(2,1)S(1)}, u32[]{:S(2)}, u32[]{:S(2)}) collective-permute-start(bf16[128,2048]{1,0:T(8,128)(2,1)S(1)} %get-tuple-element.47.refs_6_.refs_11_), channel_id=1, source_target_pairs={{0,1},{2,0},{4,2},{6,4},{7,6},{5,7},{3,5},{1,3},{16,17},{18,16},{2... | collective-permute-start | bytes 1572872 | tf_op jit(solution)/shard_map/ppermute | solution.py:278
  78.8 60.1 %collective-permute-start.14 = (bf16[128,2048]{1,0:T(8,128)(2,1)S(1)}, bf16[128,2048]{1,0:T(8,128)(2,1)S(1)}, u32[]{:S(2)}, u32[]{:S(2)}) collective-permute-start(bf16[128,2048]{1,0:T(8,128)(2,1)S(1)} %get-tuple-element.47.refs_6_.refs_11_), channel_id=1, source_target_pairs={{0,2},{2,4},{4,6},{6,7},{7,5},{5,3},{3,1},{1,0},{16,18},{18,20},{2... | collective-permute-start | bytes 1572872 | tf_op jit(solution)/shard_map/ppermute | solution.py:277
  79.2 5.2 %copy-start.1 = (bf16[2048,3584]{1,0:T(8,128)(2,1)S(1)}, bf16[2048,3584]{1,0:T(8,128)(2,1)}, u32[]{:S(2)}) copy-start(bf16[2048,3584]{1,0:T(8,128)(2,1)} %copy-done) | copy-start | bytes 44040196
  84.3 5.2 %copy-start.3 = (bf16[2048,3584]{1,0:T(8,128)(2,1)S(1)}, bf16[2048,3584]{1,0:T(8,128)(2,1)}, u32[]{:S(2)}) copy-start(bf16[2048,3584]{1,0:T(8,128)(2,1)} %copy-done.2) | copy-start | bytes 44040196
  104.7 34.6 %collective-permute-start.5 = (bf16[128,2048]{1,0:T(8,128)(2,1)S(1)}, bf16[128,2048]{1,0:T(8,128)(2,1)S(1)}, u32[]{:S(2)}, u32[]{:S(2)}) collective-permute-start(bf16[128,2048]{1,0:T(8,128)(2,1)S(1)} %get-tuple-element.32), channel_id=1, source_target_pairs={{0,8},{8,0},{1,9},{9,1},{2,10},{10,2},{3,11},{11,3},{4,12},{12,4},... | collective-permute-start | bytes 1572872 | tf_op jit(solution)/shard_map/ppermute | solution.py:301
  108.3 2.1 %copy-start.14 = (bf16[128,2048]{1,0:T(8,128)(2,1)}, bf16[128,2048]{1,0:T(8,128)(2,1)S(1)}, u32[]{:S(2)}) copy-start(bf16[128,2048]{1,0:T(8,128)(2,1)S(1)} %collective-permute-done.10.refs_3_.refs_5_) | copy-start | bytes 1572868
  108.3 28.3 %collective-permute-start.11 = (bf16[128,2048]{1,0:T(8,128)(2,1)S(1)}, bf16[128,2048]{1,0:T(8,128)(2,1)S(1)}, u32[]{:S(2)}, u32[]{:S(2)}) collective-permute-start(bf16[128,2048]{1,0:T(8,128)(2,1)S(1)} %collective-permute-done.10.refs_3_.refs_5_), channel_id=1, source_target_pairs={{0,1},{2,0},{4,2},{6,4},{7,6},{5,7},{3,5},{1,3},{16,17},{18,16},{2... | collective-permute-start | bytes 1572872 | tf_op jit(solution)/shard_map/ppermute | solution.py:278
  109.8 0.8 copy-start.15
  109.8 21.2 %collective-permute-start.8 = (bf16[128,2048]{1,0:T(8,128)(2,1)S(1)}, bf16[128,2048]{1,0:T(8,128)(2,1)S(1)}, u32[]{:S(2)}, u32[]{:S(2)}) collective-permute-start(bf16[128,2048]{1,0:T(8,128)(2,1)S(1)} %collective-permute-done.7.refs_2_.refs_4_), channel_id=1, source_target_pairs={{0,2},{2,4},{4,6},{6,7},{7,5},{5,3},{3,1},{1,0},{16,18},{18,20},{2... | collective-permute-start | bytes 1572872 | tf_op jit(solution)/shard_map/ppermute | solution.py:277
  131.1 22.5 %copy-start.8 = (bf16[128,2048]{1,0:T(8,128)(2,1)}, bf16[128,2048]{1,0:T(8,128)(2,1)S(1)}, u32[]{:S(2)}) copy-start(bf16[128,2048]{1,0:T(8,128)(2,1)S(1)} %collective-permute-done.8.refs_0_.refs_1_) | copy-start | bytes 1572868
  131.1 3.6 %collective-permute-start.22 = (f32[128]{0:T(128)S(1)}, f32[128]{0:T(128)S(1)}, u32[]{:S(2)}, u32[]{:S(2)}) collective-permute-start(f32[128]{0:T(128)S(1)} %select_reduce_fusion), channel_id=1, source_target_pairs={{0,8},{8,0},{1,9},{9,1},{2,10},{10,2},{3,11},{11,3},{4,12},{12,4},... | collective-permute-start | bytes 1544 | tf_op jit(solution)/shard_map/ppermute | solution.py:347
  134.7 9.2 %collective-permute-start.12 = (bf16[64,2048]{1,0:T(8,128)(2,1)S(1)}, bf16[64,2048]{1,0:T(8,128)(2,1)S(1)}, u32[]{:S(2)}, u32[]{:S(2)}) collective-permute-start(bf16[64,2048]{1,0:T(8,128)(2,1)S(1)} %slice.16), channel_id=1, source_target_pairs={{0,2},{2,4},{4,6},{6,7},{7,5},{5,3},{3,1},{1,0},{16,18},{18,20},{2... | collective-permute-start | bytes 786440 | tf_op jit(solution)/shard_map/ppermute | solution.py:282
  136.6 17.0 %copy-start.7 = (bf16[128,2048]{1,0:T(8,128)(2,1)}, bf16[128,2048]{1,0:T(8,128)(2,1)S(1)}, u32[]{:S(2)}) copy-start(bf16[128,2048]{1,0:T(8,128)(2,1)S(1)} %collective-permute-done.11.refs_1_.refs_2_) | copy-start | bytes 1572868
  136.6 9.2 %collective-permute-start.13 = (bf16[64,2048]{1,0:T(8,128)(2,1)S(1)}, bf16[64,2048]{1,0:T(8,128)(2,1)S(1)}, u32[]{:S(2)}, u32[]{:S(2)}) collective-permute-start(bf16[64,2048]{1,0:T(8,128)(2,1)S(1)} %slice.17), channel_id=1, source_target_pairs={{0,1},{2,0},{4,2},{6,4},{7,6},{5,7},{3,5},{1,3},{16,17},{18,16},{2... | collective-permute-start | bytes 786440 | tf_op jit(solution)/shard_map/ppermute | solution.py:283
  137.3 32.0 %copy-start.16 = (bf16[128,2048]{1,0:T(8,128)(2,1)}, bf16[128,2048]{1,0:T(8,128)(2,1)S(1)}, u32[]{:S(2)}) copy-start(bf16[128,2048]{1,0:T(8,128)(2,1)S(1)} %collective-permute-done.17.refs_8_.refs_13_) | copy-start | bytes 1572868
  137.3 14.2 %collective-permute-start.18 = (bf16[128,2048]{1,0:T(8,128)(2,1)S(1)}, bf16[128,2048]{1,0:T(8,128)(2,1)S(1)}, u32[]{:S(2)}, u32[]{:S(2)}) collective-permute-start(bf16[128,2048]{1,0:T(8,128)(2,1)S(1)} %collective-permute-done.17.refs_8_.refs_13_), channel_id=1, source_target_pairs={{0,1},{2,0},{4,2},{6,4},{7,6},{5,7},{3,5},{1,3},{16,17},{18,16},{2... | collective-permute-start | bytes 1572872 | tf_op jit(solution)/shard_map/ppermute | solution.py:278
  139.0 30.4 %copy-start.17 = (bf16[128,2048]{1,0:T(8,128)(2,1)}, bf16[128,2048]{1,0:T(8,128)(2,1)S(1)}, u32[]{:S(2)}) copy-start(bf16[128,2048]{1,0:T(8,128)(2,1)S(1)} %collective-permute-done.14.refs_7_.refs_12_) | copy-start | bytes 1572868
  139.0 13.6 %collective-permute-start.15 = (bf16[128,2048]{1,0:T(8,128)(2,1)S(1)}, bf16[128,2048]{1,0:T(8,128)(2,1)S(1)}, u32[]{:S(2)}, u32[]{:S(2)}) collective-permute-start(bf16[128,2048]{1,0:T(8,128)(2,1)S(1)} %collective-permute-done.14.refs_7_.refs_12_), channel_id=1, source_target_pairs={{0,2},{2,4},{4,6},{6,7},{7,5},{5,3},{3,1},{1,0},{16,18},{18,20},{2... | collective-permute-start | bytes 1572872 | tf_op jit(solution)/shard_map/ppermute | solution.py:277
  145.9 7.7 %copy-start.9 = (bf16[128,2048]{1,0:T(8,128)(2,1)}, bf16[128,2048]{1,0:T(8,128)(2,1)S(1)}, u32[]{:S(2)}) copy-start(bf16[128,2048]{1,0:T(8,128)(2,1)S(1)} %constant_dynamic-update-slice_fusion.refs_2_.refs_3_) | copy-start | bytes 1572868
  151.6 17.8 %copy-start.18 = (bf16[128,2048]{1,0:T(8,128)(2,1)}, bf16[128,2048]{1,0:T(8,128)(2,1)S(1)}, u32[]{:S(2)}) copy-start(bf16[128,2048]{1,0:T(8,128)(2,1)S(1)} %collective-permute-done.18.refs_10_.refs_15_) | copy-start | bytes 1572868
  151.6 17.8 %collective-permute-start.19 = (bf16[128,2048]{1,0:T(8,128)(2,1)S(1)}, bf16[128,2048]{1,0:T(8,128)(2,1)S(1)}, u32[]{:S(2)}, u32[]{:S(2)}) collective-permute-start(bf16[128,2048]{1,0:T(8,128)(2,1)S(1)} %collective-permute-done.18.refs_10_.refs_15_), channel_id=1, source_target_pairs={{0,1},{2,0},{4,2},{6,4},{7,6},{5,7},{3,5},{1,3},{16,17},{18,16},{2... | collective-permute-start | bytes 1572872 | tf_op jit(solution)/shard_map/ppermute | solution.py:278
  152.5 16.9 %copy-start.19 = (bf16[128,2048]{1,0:T(8,128)(2,1)}, bf16[128,2048]{1,0:T(8,128)(2,1)S(1)}, u32[]{:S(2)}) copy-start(bf16[128,2048]{1,0:T(8,128)(2,1)S(1)} %collective-permute-done.15.refs_9_.refs_14_) | copy-start | bytes 1572868
  152.5 17.9 %collective-permute-start.16 = (bf16[128,2048]{1,0:T(8,128)(2,1)S(1)}, bf16[128,2048]{1,0:T(8,128)(2,1)S(1)}, u32[]{:S(2)}, u32[]{:S(2)}) collective-permute-start(bf16[128,2048]{1,0:T(8,128)(2,1)S(1)} %collective-permute-done.15.refs_9_.refs_14_), channel_id=1, source_target_pairs={{0,2},{2,4},{4,6},{6,7},{7,5},{5,3},{3,1},{1,0},{16,18},{18,20},{2... | collective-permute-start | bytes 1572872 | tf_op jit(solution)/shard_map/ppermute | solution.py:277
  169.4 22.1 %copy-start.4 = (bf16[128,2048]{1,0:T(8,128)(2,1)}, bf16[128,2048]{1,0:T(8,128)(2,1)S(1)}, u32[]{:S(2)}) copy-start(bf16[128,2048]{1,0:T(8,128)(2,1)S(1)} %collective-permute-done.19.refs_5_.refs_8_) | copy-start | bytes 1572868
  169.4 22.1 %collective-permute-start.21 = (bf16[64,2048]{1,0:T(8,128)(2,1)S(1)}, bf16[64,2048]{1,0:T(8,128)(2,1)S(1)}, u32[]{:S(2)}, u32[]{:S(2)}) collective-permute-start(bf16[64,2048]{1,0:T(8,128)(2,1)S(1)} %slice.19), channel_id=1, source_target_pairs={{0,1},{2,0},{4,2},{6,4},{7,6},{5,7},{3,5},{1,3},{16,17},{18,16},{2... | collective-permute-start | bytes 786440 | tf_op jit(solution)/shard_map/ppermute | solution.py:283
  170.5 21.0 %copy-start.5 = (bf16[128,2048]{1,0:T(8,128)(2,1)}, bf16[128,2048]{1,0:T(8,128)(2,1)S(1)}, u32[]{:S(2)}) copy-start(bf16[128,2048]{1,0:T(8,128)(2,1)S(1)} %collective-permute-done.16.refs_4_.refs_7_) | copy-start | bytes 1572868
  170.5 21.0 %collective-permute-start.20 = (bf16[64,2048]{1,0:T(8,128)(2,1)S(1)}, bf16[64,2048]{1,0:T(8,128)(2,1)S(1)}, u32[]{:S(2)}, u32[]{:S(2)}) collective-permute-start(bf16[64,2048]{1,0:T(8,128)(2,1)S(1)} %slice.18), channel_id=1, source_target_pairs={{0,2},{2,4},{4,6},{6,7},{7,5},{5,3},{3,1},{1,0},{16,18},{18,20},{2... | collective-permute-start | bytes 786440 | tf_op jit(solution)/shard_map/ppermute | solution.py:282
